TPU v7x, 32 devices: a whole 2x2x4 slice. The times are simulated.
32 devices in a mesh: beams: 2 (over y), wind: 4 (over z), cross: 4 (over x, core).
Axes of the slice: x: 2, y: 2, z: 4, core: 2. Of those that a mesh axis runs over, the one named last changes fastest.
Arguments:
- field_real: float32 [2048, 2048], P(('beams', 'wind'), 'cross'), parts along dimension 0, may hold values from -6 to 6
- field_imag: float32 [2048, 2048], P(('beams', 'wind'), 'cross'), parts along dimension 0, may hold values from -6 to 6
- absorb_index: int32 [2, 2048], P(None, 'cross'), may hold values from 0 to 7
- absorb_table: float32 [2, 8], replicated, may hold values from 0.3 to 3
- zone_map: int32 [1024, 2048], P('wind', 'cross'), may hold values from 0 to 7
- zone_conductivity: float32 [8], replicated, may hold values from 0.1 to 1
Outputs:
- field_real: float32 [2048, 2048], P(('beams', 'wind'), 'cross'), parts along dimension 0
- field_imag: float32 [2048, 2048], P(('beams', 'wind'), 'cross'), parts along dimension 0
- screen: float32 [2048, 2048], P(('beams', 'wind'), 'cross'), parts along dimension 0
There are 2 independent parts, one for each index of `beams`. A program takes and returns all parts, laid end to end along the dimension named above; an argument that names none is the same for every part. Nothing has to cross between parts.
All inputs are finite; a program needn't handle non-finite values.
Results may differ from a plain program's by a relative error of at most 0.0003.
Values sent between devices are 32-bit elements; how exact they have to be, the bound alone decides.
No kernel may reach another device: no remote copies, remote signals or barrier semaphores. Data moves between devices by JAX's collectives and lax.ppermute only.
A program may use at most 192 MiB of HBM per device.

v0:
```python
import math

import jax
import jax.numpy as jnp
from jax import lax
from jax.sharding import PartitionSpec as P

LAYERS = 2
ITERS = 2
SMOOTH = 2


diffraction = 2000.0
conduct_rate = 0.24


def extended(shard, sides, width):
    for axis, dim in sides:
        size, length = (lax.axis_size(axis), shard.shape[dim])
        up = [(i, (i + 1) % size) for i in range(size - 1)]
        down = [(j, i) for i, j in up]
        last = lax.slice_in_dim(shard, length - width, length, axis=dim)
        initial = lax.slice_in_dim(shard, 0, width, axis=dim)
        before = lax.ppermute(last, axis, up)
        after = lax.ppermute(initial, axis, down)
        shard = jnp.concatenate([before, shard, after], axis=dim)
    return shard


def carried_in(part, axis, combine, identity):
    place = lax.axis_index(axis)
    gathered = lax.all_gather(part, axis)
    state = jnp.zeros_like(part) + jnp.asarray(identity, part.dtype)

    def one(turn, state):
        return combine(state, lax.dynamic_index_in_dim(gathered, turn, 0, False))

    return lax.fori_loop(0, place, one, state)


def signed_freq(indices, length):
    shifted = jnp.where(indices < length // 2, indices, indices - length)
    return shifted.astype(jnp.float32) / length


def trig_table(first_ids, second_ids, length, sign_value):
    product = first_ids * second_ids % length
    phase_angle = product.astype(jnp.float32) * (sign_value * 2.0 * math.pi / length)
    return (jnp.cos(phase_angle), jnp.sin(phase_angle))


def complex_product(formula, real_part, imag_part, cosine, sine):
    highest = lax.Precision.HIGHEST
    out_real = jnp.einsum(formula, real_part, cosine, precision=highest) - jnp.einsum(
        formula, imag_part, sine, precision=highest
    )
    out_imag = jnp.einsum(formula, real_part, sine, precision=highest) + jnp.einsum(
        formula, imag_part, cosine, precision=highest
    )
    return (out_real, out_imag)


def transform(stacked, axis_dim, inverse):
    full_shape = stacked.shape
    length = full_shape[axis_dim]
    inner_len = math.gcd(length, 128)
    outer_len = length // inner_len
    leading = full_shape[1] if axis_dim == 2 else 1
    trailing = full_shape[2] if axis_dim == 1 else 1
    blocks = stacked.reshape(2, leading, outer_len, inner_len, trailing)
    sign_value = 1.0 if inverse else -1.0
    outer_ids = jnp.arange(outer_len, dtype=jnp.int32)
    inner_ids = jnp.arange(inner_len, dtype=jnp.int32)
    cos_outer, sin_outer = trig_table(outer_ids[:, None], outer_ids[None, :], outer_len, sign_value)
    first_real, first_imag = complex_product(
        "pabq,ak->pkbq", blocks[0], blocks[1], cos_outer, sin_outer
    )
    cos_twist, sin_twist = trig_table(outer_ids[:, None], inner_ids[None, :], length, sign_value)
    cos_twist = cos_twist[None, :, :, None]
    sin_twist = sin_twist[None, :, :, None]
    twist_real = first_real * cos_twist - first_imag * sin_twist
    twist_imag = first_real * sin_twist + first_imag * cos_twist
    cos_inner, sin_inner = trig_table(inner_ids[:, None], inner_ids[None, :], inner_len, sign_value)
    second_real, second_imag = complex_product(
        "pkbq,bm->pkmq", twist_real, twist_imag, cos_inner, sin_inner
    )
    result = jnp.stack([second_real, second_imag]).transpose(0, 1, 3, 2, 4).reshape(full_shape)
    if inverse:
        result = result * (1.0 / length)
    return result


def apply_phase(stacked, phase_angle):
    cosine = jnp.cos(phase_angle)
    sine = jnp.sin(phase_angle)
    return jnp.stack(
        [stacked[0] * cosine - stacked[1] * sine, stacked[0] * sine + stacked[1] * cosine]
    )


def along_joint(stacked, phase_rate, row_freq, col_freq):
    cross_count = lax.axis_size("cross")
    stacked = lax.all_to_all(stacked, ("wind", "cross"), split_axis=2, concat_axis=1, tiled=True)
    stacked = transform(stacked, 1, False)
    col_width = stacked.shape[2]
    joint_block = lax.axis_index("wind") * cross_count + lax.axis_index("cross")
    cols_held = lax.dynamic_slice_in_dim(col_freq, joint_block * col_width, col_width)
    phase_angle = -phase_rate * (
        row_freq[:, None] * row_freq[:, None] + cols_held[None, :] * cols_held[None, :]
    )
    stacked = apply_phase(stacked, phase_angle)
    stacked = transform(stacked, 1, True)
    return lax.all_to_all(stacked, ("wind", "cross"), split_axis=1, concat_axis=2, tiled=True)


def propagate_slab(slab_pair, share_step):
    rows_total = slab_pair.shape[1] * lax.axis_size("wind") * lax.axis_size("cross")
    cols_total = slab_pair.shape[2]
    phase_rate = share_step * diffraction
    row_freq = signed_freq(jnp.arange(rows_total, dtype=jnp.int32), rows_total)
    col_freq = signed_freq(jnp.arange(cols_total, dtype=jnp.int32), cols_total)
    stacked = transform(slab_pair, 2, False)
    stacked = along_joint(stacked, phase_rate, row_freq, col_freq)
    return transform(stacked, 2, True)


def conduct_core(padded, kappa_pad):
    height = padded.shape[0] - 2
    breadth = padded.shape[1] - 2
    center = padded[1:-1, 1:-1]
    kappa_mid = kappa_pad[1:-1, 1:-1]
    flux_sum = jnp.zeros_like(center)
    for offset_row, offset_col in ((0, 1), (2, 1), (1, 0), (1, 2)):
        neighbour = padded[offset_row : offset_row + height, offset_col : offset_col + breadth]
        kappa_side = kappa_pad[offset_row : offset_row + height, offset_col : offset_col + breadth]
        flux_sum = flux_sum + 0.5 * (kappa_mid + kappa_side) * (neighbour - center)
    return center + conduct_rate * flux_sum


def add_terms(earlier, later_term):
    return earlier + later_term


def layer_absorption(index_row, table_row, level_ids):
    one_hot = (index_row[:, None] == level_ids[None, :]).astype(jnp.float32)
    return jnp.sum(one_hot * table_row[None, :], axis=1)


def on_device(field_real, field_imag, absorb_index, absorb_table, zone_map, zone_conductivity):
    rows_here, cols_here = field_real.shape
    conductivity = jnp.zeros((rows_here, cols_here), jnp.float32)
    for zone_no in range(zone_conductivity.shape[0]):
        conductivity = jnp.where(zone_map == zone_no, zone_conductivity[zone_no], conductivity)
    level_ids = jnp.arange(absorb_table.shape[1], dtype=jnp.int32)
    combined = lax.all_to_all(
        jnp.stack([field_real, field_imag, conductivity]),
        "cross",
        split_axis=1,
        concat_axis=2,
        tiled=True,
    )
    slab_pair = combined[:2]
    kappa_rows = extended(combined[2], ((("wind", "cross"), 0),), 1)
    kappa_pad = jnp.pad(kappa_rows, ((0, 0), (1, 1)))
    index_full = lax.all_gather(absorb_index, "cross", axis=1, tiled=True)
    slab_rows = slab_pair.shape[1]
    rows_total = slab_rows * lax.axis_size("wind") * lax.axis_size("cross")
    slab_ids = jnp.arange(slab_rows, dtype=jnp.int32)
    lower_slab = (slab_ids[:, None] >= slab_ids[None, :]).astype(jnp.float32)
    screen_phase = jnp.zeros((slab_rows, slab_pair.shape[2]), jnp.float32)
    for layer_no in range(LAYERS):
        absorption = layer_absorption(index_full[layer_no], absorb_table[layer_no], level_ids)
        screen_phase = jnp.zeros((slab_rows, slab_pair.shape[2]), jnp.float32)
        for round_no in range(ITERS):
            middle = propagate_slab(apply_phase(slab_pair, screen_phase), 0.5)
            intensity = middle[0] * middle[0] + middle[1] * middle[1]
            deposit = absorption[None, :] * intensity * (1.0 / rows_total)
            partial_heat = jnp.dot(lower_slab, deposit, precision=lax.Precision.HIGHEST)
            totals = partial_heat[-1]
            upstream = carried_in(totals, ("wind", "cross"), add_terms, jnp.zeros_like(totals))
            heat_field = partial_heat + upstream[None, :]
            for smooth_no in range(SMOOTH):
                padded = extended(heat_field, ((("wind", "cross"), 0),), 1)
                padded = jnp.pad(padded, ((0, 0), (1, 1)))
                heat_field = conduct_core(padded, kappa_pad)
            screen_phase = -heat_field
        slab_pair = propagate_slab(apply_phase(slab_pair, screen_phase), 1.0)
    returned = lax.all_to_all(
        jnp.stack([slab_pair[0], slab_pair[1], screen_phase]),
        "cross",
        split_axis=2,
        concat_axis=1,
        tiled=True,
    )
    return (returned[0], returned[1], returned[2])


def solution(mesh):
    in_specs = (
        P(("beams", "wind"), "cross"),
        P(("beams", "wind"), "cross"),
        P(None, "cross"),
        P(),
        P("wind", "cross"),
        P(),
    )
    out_specs = (
        P(("beams", "wind"), "cross"),
        P(("beams", "wind"), "cross"),
        P(("beams", "wind"), "cross"),
    )
    return jax.shard_map(
        on_device, mesh=mesh, in_specs=in_specs, out_specs=out_specs, check_vma=False
    )
```

profile of v0, /device:TPU:16, one launch (start us, length us, event | category | flops | bytes accessed | tf_op | source)
XLA Modules:
  0.0 1006.1 jit_solution(1498844778639409519)
XLA Ops:
  16.1 25.6 %all-to-all-done = f32[3,256,512]{2,0,1:T(4,128)S(1)} async-done(((f32[3,256,512]{2,0,1:T(4,128)}), f32[3,256,512]{2,0,1:T(4,128)S(1)}, u32[]{:S(2)}, u32[]{:S(2)}) %all-to-all-start) | async-done | bytes 1572896 | tf_op jit(solution)/shard_map/all_to_all | solution.py:155
  53.8 8.8 copy.2312
  72.6 24.5 %all-to-all-done.1 = f32[16,1,16384]{2,1,0:T(1,128)S(1)} async-done(((f32[16,1,16384]{2,1,0:T(1,128)}), f32[16,1,16384]{2,1,0:T(1,128)S(1)}, u32[]{:S(2)}, u32[]{:S(2)}) %all-to-all-start.1) | async-done | bytes 1048608 | tf_op jit(solution)/shard_map/all_to_all | solution.py:103
  132.9 7.9 all_gather.15
  148.6 9.5 all-to-all-done.2
  166.6 14.7 %all-gather = f32[16,1,2048]{2,1,0:T(1,128)S(1)} all-gather(f32[1,1,2048]{2,1,0:T(1,128)S(1)} %slice_bitcast_fusion.41), channel_id=1, replica_groups=mesh['beams'=2,'wind'=4,'cross'=4] {'wind','cross'}, dimensions={0}, use_global_device_ids=true | all-gather | bytes 139264 | tf_op jit(solution)/shard_map/all_gather | solution.py:32
  223.4 32.5 %all_to_all.210 = f32[16,1,16384]{2,1,0:T(1,128)} all-to-all(f32[16,1,16384]{2,1,0:T(1,128)} %reshape.1674), channel_id=1, replica_groups=mesh['beams'=2,'wind'=4,'cross'=4] {'wind','cross'}, dimensions={0} | all-to-all | bytes 2097152 | tf_op jit(solution)/shard_map/all_to_all | solution.py:103
  295.0 25.1 %all-to-all-done.4 = f32[2,1024,128]{2,0,1:T(2,128)} async-done(((f32[2,1024,128]{2,0,1:T(2,128)}), f32[2,1024,128]{2,0,1:T(2,128)}, u32[]{:S(2)}, u32[]{:S(2)}) %all-to-all-start.4) | async-done | bytes 1048608 | tf_op jit(solution)/shard_map/all_to_all | solution.py:113
  331.9 14.8 %all-gather.1 = f32[16,1,2048]{2,1,0:T(1,128)S(1)} all-gather(f32[1,1,2048]{2,1,0:T(1,128)S(1)} %slice_bitcast_fusion.38), channel_id=1, replica_groups=mesh['beams'=2,'wind'=4,'cross'=4] {'wind','cross'}, dimensions={0}, use_global_device_ids=true | all-gather | bytes 139264 | tf_op jit(solution)/shard_map/all_gather | solution.py:32
  347.4 7.0 while.41
  393.9 34.8 %all_to_all.211 = f32[16,1,16384]{2,1,0:T(1,128)} all-to-all(f32[16,1,16384]{2,1,0:T(1,128)S(1)} %reshape.1676), channel_id=1, replica_groups=mesh['beams'=2,'wind'=4,'cross'=4] {'wind','cross'}, dimensions={0} | all-to-all | bytes 2097152 | tf_op jit(solution)/shard_map/all_to_all | solution.py:103
  457.7 29.5 %all_to_all.212 = f32[2,1024,128]{2,0,1:T(2,128)S(1)} all-to-all(f32[2,1024,128]{2,0,1:T(2,128)S(1)} %copy.1660), channel_id=1, replica_groups=mesh['beams'=2,'wind'=4,'cross'=4] {'wind','cross'}, dimensions={1} | all-to-all | bytes 2097152 | tf_op jit(solution)/shard_map/all_to_all | solution.py:113
  517.1 29.6 %all_to_all.213 = f32[16,1,16384]{2,1,0:T(1,128)} all-to-all(f32[16,1,16384]{2,1,0:T(1,128)S(1)} %reshape.1678), channel_id=1, replica_groups=mesh['beams'=2,'wind'=4,'cross'=4] {'wind','cross'}, dimensions={0} | all-to-all | bytes 2097152 | tf_op jit(solution)/shard_map/all_to_all | solution.py:103
  581.5 25.0 %all-to-all-done.8 = f32[2,1024,128]{2,0,1:T(2,128)S(1)} async-done(((f32[2,1024,128]{2,0,1:T(2,128)}), f32[2,1024,128]{2,0,1:T(2,128)S(1)}, u32[]{:S(2)}, u32[]{:S(2)}) %all-to-all-start.8) | async-done | bytes 1048608 | tf_op jit(solution)/shard_map/all_to_all | solution.py:113
  614.9 14.8 %all-gather.2 = f32[16,1,2048]{2,1,0:T(1,128)S(1)} all-gather(f32[1,1,2048]{2,1,0:T(1,128)S(1)} %slice_bitcast_fusion.37), channel_id=1, replica_groups=mesh['beams'=2,'wind'=4,'cross'=4] {'wind','cross'}, dimensions={0}, use_global_device_ids=true | all-gather | bytes 139264 | tf_op jit(solution)/shard_map/all_gather | solution.py:32
  673.5 31.4 %all_to_all.214 = f32[16,1,16384]{2,1,0:T(1,128)} all-to-all(f32[16,1,16384]{2,1,0:T(1,128)} %reshape.1680), channel_id=1, replica_groups=mesh['beams'=2,'wind'=4,'cross'=4] {'wind','cross'}, dimensions={0} | all-to-all | bytes 2097152 | tf_op jit(solution)/shard_map/all_to_all | solution.py:103
  743.9 25.1 %all-to-all-done.10 = f32[2,1024,128]{2,0,1:T(2,128)} async-done(((f32[2,1024,128]{2,0,1:T(2,128)}), f32[2,1024,128]{2,0,1:T(2,128)}, u32[]{:S(2)}, u32[]{:S(2)}) %all-to-all-start.10) | async-done | bytes 1048608 | tf_op jit(solution)/shard_map/all_to_all | solution.py:113
  780.8 14.8 %all-gather.3 = f32[16,1,2048]{2,1,0:T(1,128)S(1)} all-gather(f32[1,1,2048]{2,1,0:T(1,128)S(1)} %slice_bitcast_fusion.36), channel_id=1, replica_groups=mesh['beams'=2,'wind'=4,'cross'=4] {'wind','cross'}, dimensions={0}, use_global_device_ids=true | all-gather | bytes 139264 | tf_op jit(solution)/shard_map/all_gather | solution.py:32
  796.3 7.0 while.43
  834.8 8.8 copy.2307
  847.0 34.7 %all_to_all.215 = f32[16,1,16384]{2,1,0:T(1,128)S(1)} all-to-all(f32[16,1,16384]{2,1,0:T(1,128)S(1)} %reshape.1682), channel_id=1, replica_groups=mesh['beams'=2,'wind'=4,'cross'=4] {'wind','cross'}, dimensions={0} | all-to-all | bytes 2097152 | tf_op jit(solution)/shard_map/all_to_all | solution.py:103
  918.6 23.7 %all-to-all-done.12 = f32[2,1024,128]{2,0,1:T(2,128)S(1)} async-done(((f32[2,1024,128]{2,0,1:T(2,128)}), f32[2,1024,128]{2,0,1:T(2,128)S(1)}, u32[]{:S(2)}, u32[]{:S(2)}) %all-to-all-start.12) | async-done | bytes 1048608 | tf_op jit(solution)/shard_map/all_to_all | solution.py:113
  951.4 10.3 %copy.2306 = f32[3,64,2048]{1,0,2:T(4,128)} copy(f32[3,64,2048]{1,2,0:T(8,128)S(1)} %pad_maximum_fusion) | data formatting | bytes 3145728 | tf_op jit(solution)/shard_map/stack | solution.py:189
  966.6 22.8 %all_to_all.216 = f32[4,1,98304]{2,1,0:T(1,128)S(1)} all-to-all(f32[4,1,98304]{2,1,0:T(1,128)S(1)} %reshape.1684), channel_id=1, replica_groups=mesh['beams'=2,'wind'=4,'cross'=4] {'cross'}, dimensions={0} | all-to-all | bytes 3145728 | tf_op jit(solution)/shard_map/all_to_all | solution.py:188
  (556 shorter events, 533.1 us)
Async XLA Ops:
  12.4 29.2 %all-to-all-start = ((f32[3,256,512]{2,0,1:T(4,128)}), f32[3,256,512]{2,0,1:T(4,128)S(1)}, u32[]{:S(2)}, u32[]{:S(2)}) async-start(f32[3,256,512]{2,0,1:T(4,128)} %pad_maximum_fusion.1), calls=%async_computation | async-start | bytes 4194304 | tf_op jit(solution)/shard_map/all_to_all | solution.py:155
  66.7 30.4 %all-to-all-start.1 = ((f32[16,1,16384]{2,1,0:T(1,128)}), f32[16,1,16384]{2,1,0:T(1,128)S(1)}, u32[]{:S(2)}, u32[]{:S(2)}) async-start(f32[16,1,16384]{2,1,0:T(1,128)} %reshape.1672), calls=%async_computation.1 | async-start | bytes 2097152 | tf_op jit(solution)/shard_map/all_to_all | solution.py:103
  128.3 29.8 %all-to-all-start.2 = ((f32[2,1024,128]{2,0,1:T(2,128)}), f32[2,1024,128]{2,0,1:T(2,128)S(1)}, u32[]{:S(2)}, u32[]{:S(2)}) async-start(f32[2,1024,128]{2,0,1:T(2,128)} %copy.1572), calls=%async_computation.2 | async-start | bytes 2097152 | tf_op jit(solution)/shard_map/all_to_all | solution.py:113
  141.9 46.5 %collective-permute-start = (f32[1,2048]{1,0:T(1,128)S(1)}, f32[1,2048]{1,0:T(1,128)S(1)}, u32[]{:S(2)}, u32[]{:S(2)}) collective-permute-start(f32[1,2048]{1,0:T(1,128)S(1)} %bitcast.1458), channel_id=1, source_target_pairs={{0,1},{1,2},{2,3},{3,4},{4,5},{5,6},{6,7},{7,8},{8,9},{9,10},{10,1... | collective-permute-start | bytes 24584 | tf_op jit(solution)/shard_map/ppermute | solution.py:24
  144.1 44.2 %collective-permute-start.2 = (f32[1,2048]{1,0:T(1,128)S(1)}, f32[1,2048]{1,0:T(1,128)S(1)}, u32[]{:S(2)}, u32[]{:S(2)}) collective-permute-start(f32[1,2048]{1,0:T(1,128)S(1)} %bitcast.1457), channel_id=1, source_target_pairs={{1,0},{2,1},{3,2},{4,3},{5,4},{6,5},{7,6},{8,7},{9,8},{10,9},{11,1... | collective-permute-start | bytes 24584 | tf_op jit(solution)/shard_map/ppermute | solution.py:25
  181.8 6.8 collective-permute-start.1
  184.2 5.5 collective-permute-start.3
  190.7 7.2 collective-permute-start.4
  193.1 5.5 collective-permute-start.5
  289.8 30.3 %all-to-all-start.4 = ((f32[2,1024,128]{2,0,1:T(2,128)}), f32[2,1024,128]{2,0,1:T(2,128)}, u32[]{:S(2)}, u32[]{:S(2)}) async-start(f32[2,1024,128]{2,0,1:T(2,128)} %copy.1616), calls=%async_computation.4 | async-start | bytes 2097152 | tf_op jit(solution)/shard_map/all_to_all | solution.py:113
  354.5 6.5 collective-permute-start.6
  357.6 4.7 collective-permute-start.7
  363.1 6.5 collective-permute-start.8
  367.1 4.7 collective-permute-start.9
  576.5 30.0 %all-to-all-start.8 = ((f32[2,1024,128]{2,0,1:T(2,128)}), f32[2,1024,128]{2,0,1:T(2,128)S(1)}, u32[]{:S(2)}, u32[]{:S(2)}) async-start(f32[2,1024,128]{2,0,1:T(2,128)} %copy.1710), calls=%async_computation.8 | async-start | bytes 2097152 | tf_op jit(solution)/shard_map/all_to_all | solution.py:113
  630.3 6.5 collective-permute-start.10
  632.6 5.5 collective-permute-start.11
  639.0 9.1 collective-permute-start.12
  641.3 6.9 collective-permute-start.13
  738.7 30.2 %all-to-all-start.10 = ((f32[2,1024,128]{2,0,1:T(2,128)}), f32[2,1024,128]{2,0,1:T(2,128)}, u32[]{:S(2)}, u32[]{:S(2)}) async-start(f32[2,1024,128]{2,0,1:T(2,128)} %copy.1759), calls=%async_computation.10 | async-start | bytes 2097152 | tf_op jit(solution)/shard_map/all_to_all | solution.py:113
  803.4 6.5 collective-permute-start.14
  812.0 6.5 collective-permute-start.16
  816.0 4.7 collective-permute-start.17
  912.4 30.0 %all-to-all-start.12 = ((f32[2,1024,128]{2,0,1:T(2,128)}), f32[2,1024,128]{2,0,1:T(2,128)S(1)}, u32[]{:S(2)}, u32[]{:S(2)}) async-start(f32[2,1024,128]{2,0,1:T(2,128)} %copy.1807), calls=%async_computation.12 | async-start | bytes 2097152 | tf_op jit(solution)/shard_map/all_to_all | solution.py:113
  (10 other events, 71.6 us)
where the time goes:
time: 1020 us; the launch traced here: 1010 us
  blocking collectives  282 us (28%)
  local copies, waits for them, and re-layouts  207 us (20%)
  waiting for transfers between devices  168 us (16%)
  matrix products  160 us (16%)
  starting transfers between devices  92.4 us (9%)
  other arithmetic  91.4 us (9%)
    all_to_all x5, blocking collectives, along_joint(): lax.all_to_all(stacked, ('wind', 'cross'), split_axis=2, concat_axis=1, t...  163 us
    all_to_all x5, waiting for transfers between devices, along_joint(): lax.all_to_all(stacked, ('wind', 'cross'), split_axis=1, concat_axis=2, t...  108 us
    all_gather x4, blocking collectives, carried_in(): gathered = lax.all_gather(part, axis)  59.2 us
    unnamed x54, local copies, waits for them, and re-layouts  55.3 us
    dot_general x48, matrix products, complex_product(): jnp.einsum(formula, imag_part, cosine, precision=highest)  40.5 us
    dot_general x48, matrix products, complex_product(): jnp.einsum(formula, imag_part, sine, precision=highest)  39.7 us
    reshape x6, local copies, waits for them, and re-layouts, transform(): jnp.stack([second_real, second_imag]).transpose(0, 1, 3, 2, 4)  39.4 us
    dot_general x48, matrix products, complex_product(): jnp.einsum(formula, real_part, cosine, precision=highest)  38.4 us
  transfers between devices with their start and end apart: 25, of which 14 were waited for; matrix products, arithmetic and copies ran while one was open for 1% of the time, Pallas kernels for 0%

commit v1 on v0

--- a/solution.py
+++ b/solution.py
@@ -1,17 +1,566 @@
+import functools
 import math
 
 import jax
 import jax.numpy as jnp
+import numpy as np
 from jax import lax
+from jax.experimental import pallas as pl
+from jax.experimental.pallas import tpu as pltpu
 from jax.sharding import PartitionSpec as P
 
 LAYERS = 2
 ITERS = 2
 SMOOTH = 2
-
+INNER = 128
+CHUNK = 16
 
 diffraction = 2000.0
 conduct_rate = 0.24
+
+F32 = jnp.float32
+BF16 = jnp.bfloat16
+WHOLE = pl.BlockSpec(memory_space=pltpu.VMEM)
+SCALAR = pl.BlockSpec(memory_space=pltpu.SMEM)
+
+
+def split_np(values):
+    high = values.astype(np.float32).astype(jnp.bfloat16)
+    low = (values - high.astype(np.float64)).astype(np.float32).astype(jnp.bfloat16)
+    return high, low
+
+
+def dft_matrices():
+    ids = np.arange(INNER)
+    angle = 2.0 * np.pi * (np.outer(ids, ids) % INNER) / INNER
+    cosine, sine = np.cos(angle), np.sin(angle)
+    left = np.block([[cosine, sine], [-sine, cosine]])
+    return np.stack([*split_np(left), *split_np(left.T)])
+
+
+def chirp_columns(length, shares):
+    outer = length // INNER
+    k = np.arange(outer)[:, None]
+    m = np.arange(INNER)[None, :]
+    twist = -2.0 * np.pi * ((k * m) % length) / length
+    tables = [np.cos(twist), np.sin(twist)]
+    p = k + outer * m
+    freq = np.where(p < length // 2, p, p - length) / length
+    for share in shares:
+        angle = -share * diffraction * freq * freq
+        tables += [np.cos(angle) / length, np.sin(angle) / length]
+    return np.concatenate(tables, axis=0).astype(np.float32)
+
+
+def row_table(length, shares):
+    cols = chirp_columns(length, shares).T
+    return np.pad(cols, ((0, 0), (0, -cols.shape[1] % 128)))
+
+
+def split(x):
+    high = x.astype(BF16)
+    return high, (x - high.astype(F32)).astype(BF16)
+
+
+def times(a, b):
+    return (a[0] * b[0] - a[1] * b[1], a[0] * b[1] + a[1] * b[0])
+
+
+def small_fft(points, sign):
+    count = len(points)
+    if count == 1:
+        return points
+    even = small_fft(points[0::2], sign)
+    odd = small_fft(points[1::2], sign)
+    half = count // 2
+    out = [None] * count
+    for k in range(half):
+        re, im = odd[k]
+        if k == 0:
+            turn = (re, im)
+        elif 4 * k == count:
+            turn = (-im, re) if sign > 0 else (im, -re)
+        elif 8 * k == count:
+            root = math.sqrt(0.5)
+            turn = (root * (re - im), root * (im + re)) if sign > 0 else (root * (re + im), root * (im - re))
+        elif 8 * k == 3 * count:
+            root = math.sqrt(0.5)
+            turn = (-root * (re + im), root * (re - im)) if sign > 0 else (root * (im - re), -root * (re + im))
+        else:
+            c = math.cos(2.0 * math.pi * k / count)
+            s = sign * math.sin(2.0 * math.pi * k / count)
+            turn = (c * re - s * im, s * re + c * im)
+        out[k] = (even[k][0] + turn[0], even[k][1] + turn[1])
+        out[k + half] = (even[k][0] - turn[0], even[k][1] - turn[1])
+    return out
+
+
+def cos_sin(x):
+    turns = jnp.floor(x * (2.0 / math.pi) + 0.5)
+    r = ((x - turns * 1.5703125) - turns * 4.837512969970703125e-4) - turns * 7.549789954891882e-8
+    quad = turns.astype(jnp.int32)
+    z = r * r
+    s = r + r * z * (-1.6666654611e-1 + z * (8.3321608736e-3 - z * 1.9515295891e-4))
+    c = 1.0 - 0.5 * z + z * z * (4.166664568298827e-2 + z * (-1.388731625493765e-3 + z * 2.443315711809948e-5))
+    odd = (quad & 1) == 1
+    sin_x = jnp.where(odd, c, s)
+    cos_x = jnp.where(odd, s, c)
+    sin_x = jnp.where((quad & 2) == 2, -sin_x, sin_x)
+    cos_x = jnp.where(((quad + 1) & 2) == 2, -cos_x, cos_x)
+    return cos_x, sin_x
+
+
+def screened(value, screen):
+    return times(value, cos_sin(screen))
+
+
+def triple(a_high, a_low, b_high, b_low):
+    dot = functools.partial(jnp.dot, preferred_element_type=F32)
+    return dot(a_high, b_high) + dot(a_high, b_low) + dot(a_low, b_high)
+
+
+def lower_ones(size):
+    r = lax.broadcasted_iota(jnp.int32, (size, size), 0)
+    c = lax.broadcasted_iota(jnp.int32, (size, size), 1)
+    return jnp.where(r >= c, 1.0, 0.0).astype(BF16)
+
+
+def chunks(count, body):
+    def step(i, carry):
+        body(pl.multiple_of(i * CHUNK, CHUNK))
+        return carry
+
+    lax.fori_loop(0, count // CHUNK, step, 0)
+
+
+def along_rows(read, writes, dft, table, xh, xl, y, z):
+    outer = xh.shape[1] // 128
+    rows = lambda k: pl.ds(k * 128, 128)
+    col = lambda part, off: table[pl.ds(off, CHUNK), part : part + 1]
+
+    def put(k, off, value):
+        for at, v in ((0, value[0]), (INNER, value[1])):
+            xh[pl.ds(at + off, CHUNK), rows(k)], xl[pl.ds(at + off, CHUNK), rows(k)] = split(v)
+
+    def first(off):
+        for k, value in enumerate(small_fft([read(a, off) for a in range(outer)], -1)):
+            if k:
+                value = times(value, (col(k, off), col(outer + k, off)))
+            put(k, off, value)
+
+    chunks(INNER, first)
+    y[...] = triple(dft[0], dft[1], xh[...], xl[...])
+    for n, write in enumerate(writes):
+
+        def middle(off, n=n):
+            for k in range(outer):
+                value = (y[pl.ds(off, CHUNK), rows(k)], y[pl.ds(INNER + off, CHUNK), rows(k)])
+                base = (2 + 2 * n) * outer + k
+                put(k, off, times(value, (col(base, off), col(base + outer, off))))
+
+        chunks(INNER, middle)
+        z[...] = triple(dft[2], dft[3], xh[...], xl[...])
+
+        def last(off, write=write):
+            values = []
+            for k in range(outer):
+                value = (z[pl.ds(off, CHUNK), rows(k)], z[pl.ds(INNER + off, CHUNK), rows(k)])
+                if k:
+                    value = times(value, (col(k, off), -col(outer + k, off)))
+                values.append(value)
+            for a, value in enumerate(small_fft(values, 1)):
+                write(a, off, value)
+
+        chunks(INNER, last)
+
+
+def along_cols(read, writes, dft, table, xh, xl, y, z):
+    outer = table.shape[0] // (2 * (1 + len(writes)))
+    height = xh.shape[0] // outer
+    row = lambda part: table[part : part + 1, :]
+
+    def put(k, off, value):
+        for at, v in ((0, value[0]), (INNER, value[1])):
+            spot = (pl.ds(k * height + off, CHUNK), pl.ds(at, INNER))
+            xh[spot], xl[spot] = split(v)
+
+    def get(ref, k, off):
+        return tuple(ref[pl.ds(k * height + off, CHUNK), pl.ds(at, INNER)] for at in (0, INNER))
+
+    def first(off):
+        for k, value in enumerate(small_fft([read(b, off) for b in range(outer)], -1)):
+            if k:
+                value = times(value, (row(k), row(outer + k)))
+            put(k, off, value)
+
+    chunks(height, first)
+    y[...] = triple(xh[...], xl[...], dft[2], dft[3])
+    for n, write in enumerate(writes):
+
+        def middle(off, n=n):
+            for k in range(outer):
+                base = (2 + 2 * n) * outer + k
+                put(k, off, times(get(y, k, off), (row(base), row(base + outer))))
+
+        chunks(height, middle)
+        z[...] = triple(xh[...], xl[...], dft[0], dft[1])
+
+        def last(off, write=write):
+            values = []
+            for k in range(outer):
+                value = get(z, k, off)
+                if k:
+                    value = times(value, (row(k), -row(outer + k)))
+                values.append(value)
+            for b, value in enumerate(small_fft(values, 1)):
+                write(b, off, value)
+
+        chunks(height, last)
+
+
+class Plan:
+    def __init__(self, rows_here, cols_here, wind, cross):
+        self.wind, self.cross = wind, cross
+        self.devices = wind * cross
+        self.rows_here, self.cols_here = rows_here, cols_here
+        self.height = rows_here // cross
+        self.width = cols_here // wind
+        self.rows, self.cols = rows_here * wind, cols_here * cross
+
+    def slot(self, block):
+        return (block % self.wind) * self.cross + block // self.wind
+
+    def home_a(self, ref, a, off):
+        n = a * INNER
+        src, at = n // self.rows_here, n % self.rows_here
+        return tuple(ref[src, p, pl.ds(at + off, CHUNK), :] for p in (0, 1))
+
+    def spot_a(self, a, off):
+        per = INNER // self.height
+        return a * per + off // self.height, lax.rem(off, self.height)
+
+    def flip_a(self, ref, a, off):
+        s, at = self.spot_a(a, off)
+        at = pl.multiple_of(at, CHUNK)
+        return tuple(ref[s, pl.ds(p * self.height + at, CHUNK), :] for p in (0, 1))
+
+    def send_a(self, ref, a, off, value):
+        s, at = self.spot_a(a, off)
+        at = pl.multiple_of(at, CHUNK)
+        for p in (0, 1):
+            ref[s, pl.ds(p * self.height + at, CHUNK), :] = value[p]
+
+    def home_b(self, ref, b, off):
+        per = self.cols_here // INNER
+        return tuple(ref[b // per, pl.ds(p * self.height + off, CHUNK), pl.ds((b % per) * INNER, INNER)] for p in (0, 1))
+
+    def flip_b(self, ref, b, off):
+        return tuple(ref[self.slot(b), pl.ds(p * self.height + off, CHUNK), :] for p in (0, 1))
+
+    def send_b(self, ref, b, off, value):
+        for p in (0, 1):
+            ref[self.slot(b), pl.ds(p * self.height + off, CHUNK), :] = value[p]
+
+    def back_b(self, ref, b, off, value):
+        per = self.cols_here // INNER
+        for p in (0, 1):
+            ref[b // per, pl.ds(p * self.height + off, CHUNK), pl.ds((b % per) * INNER, INNER)] = value[p]
+
+    @property
+    def sent(self):
+        return jax.ShapeDtypeStruct((self.devices, 2 * self.height, self.width), F32)
+
+    def work_a(self):
+        wide = (self.rows // INNER) * self.width
+        return [
+            pltpu.VMEM((2 * INNER, wide), BF16),
+            pltpu.VMEM((2 * INNER, wide), BF16),
+            pltpu.VMEM((2 * INNER, wide), F32),
+            pltpu.VMEM((2 * INNER, wide), F32),
+        ]
+
+    def work_b(self):
+        tall = (self.cols // INNER) * self.height
+        return [
+            pltpu.VMEM((tall, 2 * INNER), BF16),
+            pltpu.VMEM((tall, 2 * INNER), BF16),
+            pltpu.VMEM((tall, 2 * INNER), F32),
+            pltpu.VMEM((tall, 2 * INNER), F32),
+        ]
+
+
+def call(body, outs, scratch, specs=None, name=None):
+    def run(*args):
+        in_specs = [SCALAR if a.dtype == jnp.int32 else WHOLE for a in args]
+        return pl.pallas_call(
+            body,
+            out_shape=outs,
+            in_specs=in_specs,
+            out_specs=[WHOLE] * len(outs),
+            scratch_shapes=scratch,
+            name=name,
+        )(*args)
+
+    return run
+
+
+def rows_send(plan, read_field, dft, table, field):
+    def body(dft, table, field, out, *work):
+        along_rows(functools.partial(read_field, field), [functools.partial(plan.send_a, out)], dft, table, *work)
+
+    return call(body, [plan.sent], plan.work_a(), name="rows_send")(dft, table, field)[0]
+
+
+def cols_send(plan, read_field, back, dft, table, field):
+    out = jax.ShapeDtypeStruct((plan.cross, 2 * plan.height, plan.cols_here), F32) if back else plan.sent
+
+    def body(dft, table, field, out, *work):
+        put = plan.back_b if back else plan.send_b
+        along_cols(functools.partial(read_field, field), [functools.partial(put, out)], dft, table, *work)
+
+    return call(body, [out], plan.work_b(), name="cols_send")(dft, table, field)[0]
+
+
+def cols_heat(plan, layer, dft, table, received, home):
+    blocks = plan.cols // INNER
+    h = plan.height
+    per = plan.cols_here // INNER
+
+    def full(dft, table, received, home, part, totals, first, last, xh, xl, y, z, dep, dh, dl):
+        def write(b, off, value):
+            alpha = home[b // per, 3 * h + layer : 3 * h + layer + 1, pl.ds((b % per) * INNER, INNER)]
+            deposit = alpha * (value[0] * value[0] + value[1] * value[1])
+            spot = (pl.ds(off, CHUNK), pl.ds(b * INNER, INNER))
+            dep[spot] = deposit
+            dh[spot], dl[spot] = split(deposit)
+
+        along_cols(functools.partial(plan.flip_b, received), [write], dft, table, xh, xl, y, z)
+        ones = lower_ones(h)
+        dot = functools.partial(jnp.dot, preferred_element_type=F32)
+        part[...] = dot(ones, dh[...]) + dot(ones, dl[...])
+        for b in range(blocks):
+            lanes = slice(b * INNER, (b + 1) * INNER)
+            at = (b % per) * INNER
+            first[b, 0:8, :] = dep[0:8, lanes]
+            last[b, 0:8, :] = dep[h - 8 : h, lanes]
+            first[b, 8:16, :] = home[b // per, 2 * h : 2 * h + 8, at : at + INNER]
+            last[b, 8:16, :] = home[b // per, 3 * h - 8 : 3 * h, at : at + INNER]
+            total = part[h - 1 : h, lanes]
+            for d in range(plan.devices):
+                totals[d, b : b + 1, :] = total
+
+    edge = jax.ShapeDtypeStruct((blocks, 16, INNER), F32)
+    outs = [
+        jax.ShapeDtypeStruct((h, plan.cols), F32),
+        jax.ShapeDtypeStruct((plan.devices, blocks, INNER), F32),
+        edge,
+        edge,
+    ]
+    scratch = plan.work_b() + [pltpu.VMEM((h, plan.cols), F32), pltpu.VMEM((h, plan.cols), BF16), pltpu.VMEM((h, plan.cols), BF16)]
+    return call(full, outs, scratch, name="cols_heat")(dft, table, received, home)
+
+
+def conducted(mid, up, down, left, right, k_mid, k_up, k_down, k_left, k_right):
+    flux = (k_mid + k_up) * (up - mid) + (k_mid + k_down) * (down - mid)
+    flux = flux + (k_mid + k_left) * (left - mid) + (k_mid + k_right) * (right - mid)
+    return mid + (0.5 * conduct_rate) * flux
+
+
+def cols_screen(plan, read_field, dft, table, field, home, part, totals, above, below, me):
+    blocks = plan.cols // INNER
+    h = plan.height
+    per = plan.cols_here // INNER
+    PAD = 16
+
+    def body(dft, table, field, home, part, totals, above, below, me, out, xh, xl, y, z, h0, h1, kx):
+        place = me[0]
+        zeros = jnp.zeros((PAD, plan.cols), F32)
+        for ref in (h0, kx, h1):
+            ref[0:PAD, :] = zeros
+            ref[h + PAD : h + 2 * PAD, :] = zeros
+        upstream = jnp.zeros((blocks, INNER), F32)
+        for d in range(plan.devices):
+            upstream = upstream + jnp.where(d < place, totals[d], 0.0)
+        inner_low = jnp.where(place < plan.devices - 1, 1.0, 0.0)
+        for b in range(blocks):
+            lanes = slice(b * INNER, (b + 1) * INNER)
+            at = (b % per) * INNER
+            base = upstream[b : b + 1, :]
+            h0[PAD : PAD + h, lanes] = part[:, lanes] + base
+            value = base
+            for j in range(SMOOTH):
+                h0[PAD - 1 - j : PAD - j, lanes] = value
+                value = value - above[b, 7 - j : 8 - j, :]
+            value = base + part[h - 1 : h, lanes]
+            for j in range(SMOOTH):
+                value = value + below[b, j : j + 1, :]
+                h0[PAD + h + j : PAD + h + j + 1, lanes] = value * inner_low
+            kx[PAD - 8 : PAD, lanes] = above[b, 8:16, :]
+            kx[PAD : PAD + h, lanes] = home[b // per, 2 * h : 3 * h, at : at + INNER]
+            kx[PAD + h : PAD + h + 8, lanes] = below[b, 8:16, :]
+        lane = lax.broadcasted_iota(jnp.int32, (8, plan.cols), 1)
+        row = lax.broadcasted_iota(jnp.int32, (8, plan.cols), 0)
+
+        def sides(x):
+            left = jnp.where(lane == 0, 0.0, pltpu.roll(x, 1, 1))
+            right = jnp.where(lane == plan.cols - 1, 0.0, pltpu.roll(x, plan.cols - 1, 1))
+            return left, right
+
+        def smooth(src, dst, low, count, masked):
+            def step(i, carry):
+                base = pl.multiple_of(low + i * 8, 8)
+                value = src[pl.ds(base - 8, 24), :]
+                kap = kx[pl.ds(base - 8, 24), :]
+                mid, k_mid = value[8:16], kap[8:16]
+                left, right = sides(mid)
+                k_left, k_right = sides(k_mid)
+                new = conducted(
+                    mid, value[7:15], value[9:17], left, right, k_mid, kap[7:15], kap[9:17], k_left, k_right
+                )
+                if masked:
+                    n = row + base
+                    bad = ((n < PAD) & (place == 0)) | ((n >= PAD + h) & (place == plan.devices - 1))
+                    new = jnp.where(bad, 0.0, new)
+                dst[pl.ds(base, 8), :] = new
+                return carry
+
+            lax.fori_loop(0, count, step, 0)
+
+        refs = [h0, h1]
+        for n in range(SMOOTH):
+            if n < SMOOTH - 1:
+                smooth(refs[n % 2], refs[(n + 1) % 2], PAD - 8, (h + 16) // 8, True)
+            else:
+                smooth(refs[n % 2], refs[(n + 1) % 2], PAD, h // 8, False)
+        final = refs[SMOOTH % 2]
+
+        def read(b, off):
+            screen = -final[pl.ds(PAD + off, CHUNK), pl.ds(b * INNER, INNER)]
+            return screened(read_field(field, b, off), screen)
+
+        along_cols(read, [functools.partial(plan.send_b, out)], dft, table, xh, xl, y, z)
+
+    tall = pltpu.VMEM((h + 2 * PAD, plan.cols), F32)
+    return call(body, [plan.sent], plan.work_b() + [tall] * 3, name="cols_screen")(
+        dft, table, field, home, part, totals, above, below, me
+    )[0]
+
+
+def rows_heat(plan, dft, table, received, alpha, home):
+    width = plan.width
+
+    def body(dft, table, received, alpha, home, heat, edge_left, edge_right, xh, xl, y, z, dep):
+        def write(a, off, value):
+            deposit = alpha[...] * (value[0] * value[0] + value[1] * value[1])
+            rows = pl.ds(a * INNER + off, CHUNK)
+            dep[rows, 0:width], dep[rows, width : 2 * width] = split(deposit)
+
+        along_rows(functools.partial(plan.flip_a, received), [write], dft, table, xh, xl, y, z)
+        tile = 2 * INNER
+        ones = lower_ones(tile)
+        carry = jnp.zeros((1, width), F32)
+        for g in range(plan.rows // tile):
+            both = jnp.dot(ones, dep[g * tile : (g + 1) * tile, :], preferred_element_type=F32)
+            value = both[:, :width] + both[:, width:] + carry
+            heat[g * tile : (g + 1) * tile, :] = value
+            carry = value[tile - 1 : tile, :]
+        lane = lax.broadcasted_iota(jnp.int32, (INNER, width), 1)
+        for g in range(plan.rows // INNER):
+            n = g * INNER
+            src, at = n // plan.rows_here, n % plan.rows_here
+            value = heat[n : n + INNER, :]
+            kap = home[src, 2, at : at + INNER, :]
+            mixed = jnp.where((lane >= 8) & (lane < 64), pltpu.roll(kap, 8, 1), value)
+            mixed = jnp.where((lane >= 64) & (lane < width - 8), pltpu.roll(kap, width - 8, 1), mixed)
+            turned = mixed.T
+            edge_left[:, n : n + INNER] = turned[0:16, :]
+            edge_right[:, n : n + INNER] = turned[width - 16 : width, :]
+
+    edge = jax.ShapeDtypeStruct((16, plan.rows), F32)
+    outs = [jax.ShapeDtypeStruct((plan.rows, width), F32), edge, edge]
+    scratch = plan.work_a() + [pltpu.VMEM((plan.rows, 2 * width), BF16)]
+    return call(body, outs, scratch, name="rows_heat")(dft, table, received, alpha, home)
+
+
+def rows_screen(plan, read_field, sets, keep, dft, table, field, heat, home, from_left, from_right, me):
+    width = plan.width
+    PAD = 8
+    step_rows = 32
+
+    def body(dft, table, field, heat, home, from_left, from_right, me, *refs):
+        outs, rest = refs[:sets], refs[sets:]
+        screen, rest = (rest[0], rest[1:]) if keep else (rest[-1], rest[:-1])
+        xh, xl, y, z, h0, h1, kx = rest
+        place = me[0]
+        zeros = jnp.zeros((PAD, 2 * width), F32)
+        for ref in (h0, h1, kx):
+            ref[0:PAD, :] = zeros
+            ref[plan.rows + PAD : plan.rows + 2 * PAD, :] = zeros
+        lane = lax.broadcasted_iota(jnp.int32, (INNER, width), 1)
+        for g in range(plan.rows // INNER):
+            n = g * INNER
+            src, at = n // plan.rows_here, n % plan.rows_here
+            spot = slice(PAD + n, PAD + n + INNER)
+            h0[spot, 0:width] = heat[n : n + INNER, :]
+            kx[spot, 0:width] = home[src, 2, at : at + INNER, :]
+            turned = jnp.concatenate(
+                [from_right[:, n : n + INNER], jnp.zeros((width - 32, INNER), F32), from_left[:, n : n + INNER]], axis=0
+            ).T
+            h0[spot, width : 2 * width] = jnp.where((lane < 8) | (lane >= width - 8), turned, 0.0)
+            kap = jnp.where(lane < 8, pltpu.roll(turned, width - 8, 1), 0.0)
+            kx[spot, width : 2 * width] = jnp.where(lane >= width - 8, pltpu.roll(turned, 8, 1), kap)
+        wide = lax.broadcasted_iota(jnp.int32, (step_rows, 2 * width), 1)
+        bad = (wide >= width) & (wide < width + width // 2) & (place == plan.devices - 1)
+        bad = bad | ((wide >= width + width // 2) & (place == 0))
+
+        def smooth(src, dst):
+            def step(i, carry):
+                base = pl.multiple_of(i * step_rows, step_rows)
+                value = src[pl.ds(base, step_rows + 16), :]
+                kap = kx[pl.ds(base, step_rows + 16), :]
+                mid, k_mid = value[8:-8], kap[8:-8]
+                new = conducted(
+                    mid, value[7:-9], value[9:-7], pltpu.roll(mid, 1, 1), pltpu.roll(mid, 2 * width - 1, 1),
+                    k_mid, kap[7:-9], kap[9:-7], pltpu.roll(k_mid, 1, 1), pltpu.roll(k_mid, 2 * width - 1, 1),
+                )
+                dst(base, jnp.where(bad, 0.0, new))
+                return carry
+
+            lax.fori_loop(0, plan.rows // step_rows, step, 0)
+
+        def into(ref):
+            def put(base, value):
+                ref[pl.ds(base + PAD, step_rows), :] = value
+
+            return put
+
+        def into_screen(base, value):
+            screen[pl.ds(base, step_rows), :] = -value[:, :width]
+
+        refs = [h0, h1]
+        for n in range(SMOOTH):
+            smooth(refs[n % 2], into(refs[(n + 1) % 2]) if n < SMOOTH - 1 else into_screen)
+
+        def read(a, off):
+            return screened(read_field(field, a, off), screen[pl.ds(a * INNER + off, CHUNK), :])
+
+        along_rows(read, [functools.partial(plan.send_a, out) for out in outs], dft, table, xh, xl, y, z)
+
+    outs = [plan.sent] * sets
+    flat = (plan.rows, width)
+    tall = pltpu.VMEM((plan.rows + 2 * PAD, 2 * width), F32)
+    scratch = plan.work_a() + [tall] * 3
+    if keep:
+        outs = outs + [jax.ShapeDtypeStruct(flat, F32)]
+    else:
+        scratch = scratch + [pltpu.VMEM(flat, F32)]
+    return call(body, outs, scratch, name="rows_screen")(dft, table, field, heat, home, from_left, from_right, me)
+
+
+def next_prev(value_up, value_down, axes, order):
+    up = list(zip(order[:-1], order[1:]))
+    down = [(j, i) for i, j in up]
+    return lax.ppermute(value_up, axes, up), lax.ppermute(value_down, axes, down)
 
 
 def extended(shard, sides, width):
@@ -146,7 +695,7 @@
     return jnp.sum(one_hot * table_row[None, :], axis=1)
 
 
-def on_device(field_real, field_imag, absorb_index, absorb_table, zone_map, zone_conductivity):
+def wide_device(field_real, field_imag, absorb_index, absorb_table, zone_map, zone_conductivity):
     rows_here, cols_here = field_real.shape
     conductivity = jnp.zeros((rows_here, cols_here), jnp.float32)
     for zone_no in range(zone_conductivity.shape[0]):
@@ -195,6 +744,74 @@
     return (returned[0], returned[1], returned[2])
 
 
+def on_device(field_real, field_imag, absorb_index, absorb_table, zone_map, zone_conductivity):
+    plan = Plan(*field_real.shape, lax.axis_size("wind"), lax.axis_size("cross"))
+    fits = plan.width == INNER and INNER % plan.height == 0 and plan.height % CHUNK == 0
+    if not fits or plan.rows_here % INNER or plan.rows % (2 * INNER):
+        return wide_device(field_real, field_imag, absorb_index, absorb_table, zone_map, zone_conductivity)
+    wind, cross = plan.wind, plan.cross
+    w, c = lax.axis_index("wind"), lax.axis_index("cross")
+    row_place = jnp.reshape(w * cross + c, (1,)).astype(jnp.int32)
+    col_place = jnp.reshape(c * wind + w, (1,)).astype(jnp.int32)
+    grid_axes = ("wind", "cross")
+
+    conductivity = jnp.zeros(field_real.shape, F32)
+    for zone_no in range(zone_conductivity.shape[0]):
+        conductivity = jnp.where(zone_map == zone_no, zone_conductivity[zone_no], conductivity)
+    alpha = jnp.zeros(absorb_index.shape, F32)
+    for level in range(absorb_table.shape[1]):
+        alpha = jnp.where(absorb_index == level, absorb_table[:, level : level + 1], alpha)
+    alpha = alpha * (1.0 / plan.rows)
+    alpha_a = lax.dynamic_slice_in_dim(alpha, w * plan.width, plan.width, axis=1)
+
+    stacked = jnp.stack([field_real, field_imag, conductivity])
+    to_a = stacked.reshape(3, plan.rows_here, wind, plan.width).transpose(2, 0, 1, 3)
+    home_a = lax.all_to_all(to_a, "wind", split_axis=0, concat_axis=0, tiled=True)
+    to_b = [s.reshape(cross, plan.height, plan.cols_here) for s in (field_real, field_imag, conductivity)]
+    alpha_rows = jnp.pad(alpha, ((0, -LAYERS % 8), (0, 0)))
+    to_b.append(jnp.broadcast_to(alpha_rows[None], (cross,) + alpha_rows.shape))
+    home_b = lax.all_to_all(jnp.concatenate(to_b, axis=1), "cross", split_axis=0, concat_axis=0, tiled=True)
+
+    dft = jnp.asarray(dft_matrices())
+    tab_a = lambda *shares: jnp.asarray(row_table(plan.rows, shares))
+    tab_b = lambda *shares: jnp.asarray(chirp_columns(plan.cols, shares))
+
+    def flip(x):
+        return lax.all_to_all(x, grid_axes, split_axis=0, concat_axis=0, tiled=True)
+
+    def heat_b(layer, share, received):
+        part, totals, first, last = cols_heat(plan, layer, dft, tab_b(share), received, home_b)
+        totals = lax.all_to_all(totals, grid_axes, split_axis=0, concat_axis=0, tiled=True)
+        above, below = next_prev(last, first, grid_axes, list(range(plan.devices)))
+        return part, totals, above, below, row_place
+
+    def heat_a(layer, share, received):
+        heat, left, right = rows_heat(plan, dft, tab_a(share), received, alpha_a[layer : layer + 1], home_a)
+        from_left, from_right = next_prev(right, left, grid_axes, [plan.slot(i) for i in range(plan.devices)])
+        return heat, home_a, from_left, from_right, col_place
+
+    sent = rows_send(plan, plan.home_a, dft, tab_a(0.5), home_a)
+    parts = heat_b(0, 0.5, flip(sent))
+    sent = cols_screen(plan, plan.home_b, dft, tab_b(0.5), home_b, home_b, *parts)
+    parts = heat_a(0, 0.5, flip(sent))
+    sent_middle, sent_field = rows_screen(plan, plan.home_a, 2, False, dft, tab_a(1.5, 1.0), home_a, *parts)
+    middle = flip(sent_middle)
+    field_b = cols_send(plan, plan.flip_b, False, dft, tab_b(1.0), flip(sent_field))
+    field_a = flip(field_b)
+    parts = heat_b(1, 1.5, middle)
+    sent = cols_screen(plan, plan.flip_b, dft, tab_b(0.5), field_b, home_b, *parts)
+    parts = heat_a(1, 0.5, flip(sent))
+    sent, screen = rows_screen(plan, plan.flip_a, 1, True, dft, tab_a(1.0), field_a, *parts)
+    back = cols_send(plan, plan.flip_b, True, dft, tab_b(1.0), flip(sent))
+    back = lax.all_to_all(back, "cross", split_axis=0, concat_axis=0, tiled=True)
+    out_real = back[:, : plan.height].reshape(field_real.shape)
+    out_imag = back[:, plan.height :].reshape(field_real.shape)
+    screen = screen.reshape(wind, plan.rows_here, plan.width)
+    screen = lax.all_to_all(screen, "wind", split_axis=0, concat_axis=0, tiled=True)
+    screen = screen.transpose(1, 0, 2).reshape(field_real.shape)
+    return (out_real, out_imag, screen)
+
+
 def solution(mesh):
     in_specs = (
         P(("beams", "wind"), "cross"),

time: 1020 us -> 446 us (0.44)
  local copies, waits for them, and re-layouts: 207 us -> 14.1 us
  matrix products: 160 us -> 0 us
  blocking collectives: 282 us -> 124 us
  Pallas kernels: 0 us -> 98.8 us
  other arithmetic: 91.4 us -> 10.1 us
  waiting for transfers between devices: 168 us -> 126 us
  starting transfers between devices: 92.4 us -> 65.8 us
    dot_general x196 -> x0, matrix products: 160 us -> none  [the longest x48 40.5 us: complex_product(): jnp.einsum(formula, imag_part, cosine, precision=highest)]
    pallas_call x0 -> x11, Pallas kernels: none -> 98.8 us  [run(): pl.pallas_call(body, out_shape=outs, in_specs=in_specs, out_specs=[WHOLE]...]
    all_to_all x7 -> x4, blocking collectives: 215 us -> 124 us  [flip(): return lax.all_to_all(x, grid_axes, split_axis=0, concat_axis=0, tiled=True)]
    all_gather x5 -> x0, blocking collectives: 67 us -> none  [the longest x4 59.2 us: carried_in(): gathered = lax.all_gather(part, axis)]
    unnamed x54 -> x41, local copies, waits for them, and re-layouts: 55.3 us -> 7.25 us
    reshape x6 -> x1, local copies, waits for them, and re-layouts: 39.4 us -> 0.86 us  [on_device(): screen = screen.transpose(1, 0, 2).reshape(field_real.shape)]
    all_to_all x7 -> x9, waiting for transfers between devices: 158 us -> 121 us  [the longest x3 57.2 us: flip(): return lax.all_to_all(x, grid_axes, split_axis=0, concat_axis=0, tiled=True)]
    ppermute x18 -> x8, starting transfers between devices: 58.8 us -> 24.6 us  [the longest x4 15.3 us: next_prev(): lax.ppermute(value_down, axes, down)]
  transfers between devices with their start and end apart: 25 -> 17, of which waited for: 14 -> 11; matrix products, arithmetic and copies ran while one was open for 1% -> 1% of each run, Pallas kernels for 0% -> 7%
where the time goes in v1:
time: 446 us; the launch traced here: 440 us
  waiting for transfers between devices  126 us (28%)
  blocking collectives  124 us (28%)
  Pallas kernels  98.8 us (22%)
  starting transfers between devices  65.8 us (15%)
  local copies, waits for them, and re-layouts  14.1 us (3%)
  other arithmetic  10.1 us (2%)
    all_to_all x4, blocking collectives, flip(): return lax.all_to_all(x, grid_axes, split_axis=0, concat_axis=0, tiled=True)  124 us
    pallas_call x11, Pallas kernels, run(): pl.pallas_call(body, out_shape=outs, in_specs=in_specs, out_specs=[WHOLE]...  98.8 us
    all_to_all x3, waiting for transfers between devices, flip(): return lax.all_to_all(x, grid_axes, split_axis=0, concat_axis=0, tiled=True)  57.2 us
    all_to_all x1, waiting for transfers between devices, on_device(): lax.all_to_all(to_a, 'wind', split_axis=0, concat_axis=0, tiled=True)  29.9 us
    all_to_all x3, starting transfers between devices, flip(): return lax.all_to_all(x, grid_axes, split_axis=0, concat_axis=0, tiled=True)  15.6 us
    ppermute x4, starting transfers between devices, next_prev(): lax.ppermute(value_down, axes, down)  15.3 us
    all_to_all x1, waiting for transfers between devices, on_device(): lax.all_to_all(jnp.concatenate(to_b, axis=1), 'cross', split_axis=0, conc...  14 us
    all_to_all x1, waiting for transfers between devices, on_device(): lax.all_to_all(back, 'cross', split_axis=0, concat_axis=0, tiled=True)  13.5 us
  transfers between devices with their start and end apart: 17, of which 11 were waited for; matrix products, arithmetic and copies ran while one was open for 1% of the time, Pallas kernels for 7%

profile of v1, /device:TPU:16, one launch (start us, length us, event | category | flops | bytes accessed | tf_op | source)
XLA Modules:
  0.0 439.5 jit_solution(5107751628095908493)
XLA Ops:
  13.4 5.3 %all-to-all-start = ((f32[4,3,256,128]{3,2,1,0:T(8,128)}), f32[4,3,256,128]{3,2,1,0:T(8,128)S(1)}, u32[]{:S(2)}, u32[]{:S(2)}) async-start(f32[4,3,256,128]{3,2,1,0:T(8,128)} %maximum_bitcast_fusion), calls=%async_computation | async-start | bytes 3145728 | tf_op jit(solution)/shard_map/all_to_all | solution.py:769
  22.5 29.9 %all-to-all-done.field.home = f32[4,3,256,128]{3,2,1,0:T(8,128)S(1)} async-done(((f32[4,3,256,128]{3,2,1,0:T(8,128)}), f32[4,3,256,128]{3,2,1,0:T(8,128)S(1)}, u32[]{:S(2)}, u32[]{:S(2)}) %all-to-all-start) | async-done | bytes 1572896 | tf_op jit(solution)/shard_map/all_to_all | solution.py:769
  57.2 6.7 %rows_send.1 = f32[16,128,128]{2,1,0:T(8,128)} custom-call(bf16[4,256,256]{2,1,0:T(8,128)(2,1)} %constant.14.clone.dft, f32[128,128]{1,0:T(8,128)} %constant.15.clone.table, f32[4,3,256,128]{3,2,1,0:T(8,128)} %copy-done), custom_call_target="tpu_custom_call" | custom-call | tf_op jit(solution)/shard_map/rows_send/pallas_call | solution.py:295
  63.9 14.0 %all-to-all-done.1.home.field = f32[4,200,512]{2,1,0:T(8,128)S(1)} async-done(((f32[4,200,512]{2,1,0:T(8,128)}), f32[4,200,512]{2,1,0:T(8,128)S(1)}, u32[]{:S(2)}, u32[]{:S(2)}) %all-to-all-start.1) | async-done | bytes 1638432 | tf_op jit(solution)/shard_map/all_to_all | solution.py:773
  77.9 32.6 %all_to_all.65.received = f32[16,128,128]{2,1,0:T(8,128)} all-to-all(f32[16,128,128]{2,1,0:T(8,128)} %rows_send.1), channel_id=1, replica_groups=mesh['beams'=2,'wind'=4,'cross'=4] {'wind','cross'}, dimensions={0} | all-to-all | bytes 2097152 | tf_op jit(solution)/shard_map/all_to_all | solution.py:780
  110.5 6.4 %cols_heat.2 = (f32[64,2048]{1,0:T(8,128)}, f32[16,16,128]{2,1,0:T(8,128)}, f32[16,16,128]{2,1,0:T(8,128)}, f32[16,16,128]{2,1,0:T(8,128)}) custom-call(bf16[4,256,256]{2,1,0:T(8,128)(2,1)} %constant.14.clone.dft, f32[64,128]{1,0:T(8,128)} %constant.16.clone.table, f32[16,128,128]{2,1,0:T(8,128)} %all_to_all.65.received, f32[4,200,512]{2,1,0:T(8,128)} %copy-done.1), custom_call_target="tpu_custom_call" | custom-call | tf_op jit(solution)/shard_map/cols_heat/pallas_call | solution.py:295
  131.4 10.0 %cols_screen.2 = f32[16,128,128]{2,1,0:T(8,128)} custom-call(bf16[4,256,256]{2,1,0:T(8,128)(2,1)} %constant.14.clone.dft, f32[64,128]{1,0:T(8,128)} %constant.16.clone.table, f32[4,200,512]{2,1,0:T(8,128)} %copy-done.1, f32[4,200,512]{2,1,0:T(8,128)} %copy-done.1, f32[64,2048]{1,0:T(8,128)} %get-tuple-element.21.part, f32[16,16,128]{2,1,0:T(8,128)} %copy-done.7, ...), custom_call_target="tpu_custom_call" | custom-call | tf_op jit(solution)/shard_map/cols_screen/pallas_call | solution.py:295
  141.4 6.3 %all-to-all-start.4 = ((f32[16,128,128]{2,1,0:T(8,128)}), f32[16,128,128]{2,1,0:T(8,128)S(1)}, u32[]{:S(2)}, u32[]{:S(2)}) async-start(f32[16,128,128]{2,1,0:T(8,128)} %cols_screen.2), calls=%async_computation.4 | async-start | bytes 2097152 | tf_op jit(solution)/shard_map/all_to_all | solution.py:780
  148.3 24.5 %all-to-all-done.4.received = f32[16,128,128]{2,1,0:T(8,128)S(1)} async-done(((f32[16,128,128]{2,1,0:T(8,128)}), f32[16,128,128]{2,1,0:T(8,128)S(1)}, u32[]{:S(2)}, u32[]{:S(2)}) %all-to-all-start.4) | async-done | bytes 1048608 | tf_op jit(solution)/shard_map/all_to_all | solution.py:780
  173.9 7.4 %rows_heat.2 = (f32[1024,128]{1,0:T(8,128)}, f32[16,1024]{1,0:T(8,128)}, f32[16,1024]{1,0:T(8,128)}) custom-call(bf16[4,256,256]{2,1,0:T(8,128)(2,1)} %constant.14.clone.dft, f32[128,128]{1,0:T(8,128)} %constant.15.clone.table, f32[16,128,128]{2,1,0:T(8,128)} %copy-done.2, f32[1,128]{1,0:T(1,128)} %get-tuple-element.50.alpha, f32[4,3,256,128]{3,2,1,0:T(8,128)} %copy-done), custom_call_target="tpu_custom_call" | custom-call | tf_op jit(solution)/shard_map/rows_heat/pallas_call | solution.py:295
  190.2 18.3 %rows_screen.2 = (f32[16,128,128]{2,1,0:T(8,128)}, f32[16,128,128]{2,1,0:T(8,128)}) custom-call(bf16[4,256,256]{2,1,0:T(8,128)(2,1)} %constant.14.clone.dft, f32[128,128]{1,0:T(8,128)} %constant.17.clone.table, f32[4,3,256,128]{3,2,1,0:T(8,128)} %copy-done, f32[1024,128]{1,0:T(8,128)} %get-tuple-element.25.heat, f32[4,3,256,128]{3,2,1,0:T(8,128)} %copy-done, ...), custom_call_target="tpu_custom_call" | custom-call | tf_op jit(solution)/shard_map/rows_screen/pallas_call | solution.py:295
  208.4 31.2 %all_to_all.66.received = f32[16,128,128]{2,1,0:T(8,128)} all-to-all(f32[16,128,128]{2,1,0:T(8,128)} %get-tuple-element.29), channel_id=1, replica_groups=mesh['beams'=2,'wind'=4,'cross'=4] {'wind','cross'}, dimensions={0} | all-to-all | bytes 2097152 | tf_op jit(solution)/shard_map/all_to_all | solution.py:780
  244.3 6.4 %cols_heat.3 = (f32[64,2048]{1,0:T(8,128)}, f32[16,16,128]{2,1,0:T(8,128)}, f32[16,16,128]{2,1,0:T(8,128)}, f32[16,16,128]{2,1,0:T(8,128)}) custom-call(bf16[4,256,256]{2,1,0:T(8,128)(2,1)} %constant.14.clone.dft, f32[64,128]{1,0:T(8,128)} %constant.19.clone.table, f32[16,128,128]{2,1,0:T(8,128)} %all_to_all.66.received, f32[4,200,512]{2,1,0:T(8,128)} %copy-done.1), custom_call_target="tpu_custom_call" | custom-call | tf_op jit(solution)/shard_map/cols_heat/pallas_call | solution.py:295
  250.7 18.7 %all-to-all-done.5.field = f32[16,128,128]{2,1,0:T(8,128)S(1)} async-done(((f32[16,128,128]{2,1,0:T(8,128)}), f32[16,128,128]{2,1,0:T(8,128)S(1)}, u32[]{:S(2)}, u32[]{:S(2)}) %all-to-all-start.5) | async-done | bytes 1048608 | tf_op jit(solution)/shard_map/all_to_all | solution.py:780
  280.4 5.5 %cols_send.2.field = f32[16,128,128]{2,1,0:T(8,128)} custom-call(bf16[4,256,256]{2,1,0:T(8,128)(2,1)} %constant.14.clone.dft, f32[64,128]{1,0:T(8,128)} %constant.18.clone.table, f32[16,128,128]{2,1,0:T(8,128)} %copy-done.4), custom_call_target="tpu_custom_call" | custom-call | tf_op jit(solution)/shard_map/cols_send/pallas_call | solution.py:295
  286.7 9.9 %cols_screen.3 = f32[16,128,128]{2,1,0:T(8,128)} custom-call(bf16[4,256,256]{2,1,0:T(8,128)(2,1)} %constant.14.clone.dft, f32[64,128]{1,0:T(8,128)} %constant.16.clone.table, f32[16,128,128]{2,1,0:T(8,128)} %cols_send.2.field, f32[4,200,512]{2,1,0:T(8,128)} %copy-done.1, f32[64,2048]{1,0:T(8,128)} %get-tuple-element.30.part, f32[16,16,128]{2,1,0:T(8,128)} %copy-done.8, ...), custom_call_target="tpu_custom_call" | custom-call | tf_op jit(solution)/shard_map/cols_screen/pallas_call | solution.py:295
  296.7 30.3 %all_to_all.67.received = f32[16,128,128]{2,1,0:T(8,128)} all-to-all(f32[16,128,128]{2,1,0:T(8,128)} %cols_screen.3), channel_id=1, replica_groups=mesh['beams'=2,'wind'=4,'cross'=4] {'wind','cross'}, dimensions={0} | all-to-all | bytes 2097152 | tf_op jit(solution)/shard_map/all_to_all | solution.py:780
  331.6 7.4 %rows_heat.3 = (f32[1024,128]{1,0:T(8,128)}, f32[16,1024]{1,0:T(8,128)}, f32[16,1024]{1,0:T(8,128)}) custom-call(bf16[4,256,256]{2,1,0:T(8,128)(2,1)} %constant.14.clone.dft, f32[128,128]{1,0:T(8,128)} %constant.15.clone.table, f32[16,128,128]{2,1,0:T(8,128)} %all_to_all.67.received, f32[1,128]{1,0:T(1,128)} %get-tuple-element.49.alpha, ...), custom_call_target="tpu_custom_call" | custom-call | tf_op jit(solution)/shard_map/rows_heat/pallas_call | solution.py:295
  344.8 13.9 %all-to-all-done.6.field = f32[16,128,128]{2,1,0:T(8,128)S(1)} async-done(((f32[16,128,128]{2,1,0:T(8,128)}), f32[16,128,128]{2,1,0:T(8,128)S(1)}, u32[]{:S(2)}, u32[]{:S(2)}) %all-to-all-start.6) | async-done | bytes 1048608 | tf_op jit(solution)/shard_map/all_to_all | solution.py:780
  359.7 15.2 %rows_screen.3 = (f32[16,128,128]{2,1,0:T(8,128)}, f32[1024,128]{1,0:T(8,128)}) custom-call(bf16[4,256,256]{2,1,0:T(8,128)(2,1)} %constant.14.clone.dft, f32[128,128]{1,0:T(8,128)} %constant.20.clone.table, f32[16,128,128]{2,1,0:T(8,128)} %copy-done.3, f32[1024,128]{1,0:T(8,128)} %get-tuple-element.34.heat, f32[4,3,256,128]{3,2,1,0:T(8,128)} %copy-done, ...), custom_call_target="tpu_custom_call" | custom-call | tf_op jit(solution)/shard_map/rows_screen/pallas_call | solution.py:295
  374.9 29.9 %all_to_all.68.field = f32[16,128,128]{2,1,0:T(8,128)} all-to-all(f32[16,128,128]{2,1,0:T(8,128)} %get-tuple-element.37), channel_id=1, replica_groups=mesh['beams'=2,'wind'=4,'cross'=4] {'wind','cross'}, dimensions={0} | all-to-all | bytes 2097152 | tf_op jit(solution)/shard_map/all_to_all | solution.py:780
  409.0 5.5 %cols_send.3 = f32[4,128,512]{2,1,0:T(8,128)} custom-call(bf16[4,256,256]{2,1,0:T(8,128)(2,1)} %constant.14.clone.dft, f32[64,128]{1,0:T(8,128)} %constant.18.clone.table, f32[16,128,128]{2,1,0:T(8,128)} %all_to_all.68.field), custom_call_target="tpu_custom_call" | custom-call | tf_op jit(solution)/shard_map/cols_send/pallas_call | solution.py:295
  414.5 6.0 %all-to-all-done.12 = f32[4,256,128]{2,1,0:T(8,128)S(1)} async-done(((f32[4,256,128]{2,1,0:T(8,128)}), f32[4,256,128]{2,1,0:T(8,128)S(1)}, u32[]{:S(2)}, u32[]{:S(2)}) %all-to-all-start.12) | async-done | bytes 524320 | tf_op jit(solution)/shard_map/all_to_all | solution.py:810
  424.9 13.5 %all-to-all-done.11 = f32[4,128,512]{2,1,0:T(8,128)S(1)} async-done(((f32[4,128,512]{2,1,0:T(8,128)}), f32[4,128,512]{2,1,0:T(8,128)S(1)}, u32[]{:S(2)}, u32[]{:S(2)}) %all-to-all-start.11) | async-done | bytes 1048608 | tf_op jit(solution)/shard_map/all_to_all | solution.py:806
  (82 shorter events, 83.6 us)
Async XLA Ops:
  0.6 8.4 %copy-start.6 = (f32[256,512]{1,0:T(8,128)S(1)}, f32[256,512]{1,0:T(8,128)}, u32[]{:S(2)}) copy-start(f32[256,512]{1,0:T(8,128)} %param.18) | copy-start | bytes 1572868
  13.4 6.3 %copy-start.17 = (f32[2,8]{1,0:T(2,128)S(1)}, f32[2,8]{1,0:T(2,128)}, u32[]{:S(2)}) copy-start(f32[2,8]{1,0:T(2,128)} %param.21) | copy-start | bytes 196
  13.4 6.6 %copy-start.18 = (s32[2,512]{1,0:T(2,128)S(1)}, s32[2,512]{1,0:T(2,128)}, u32[]{:S(2)}) copy-start(s32[2,512]{1,0:T(2,128)} %param.20) | copy-start | bytes 12292
  13.4 39.0 %all-to-all-start = ((f32[4,3,256,128]{3,2,1,0:T(8,128)}), f32[4,3,256,128]{3,2,1,0:T(8,128)S(1)}, u32[]{:S(2)}, u32[]{:S(2)}) async-start(f32[4,3,256,128]{3,2,1,0:T(8,128)} %maximum_bitcast_fusion), calls=%async_computation | async-start | bytes 3145728 | tf_op jit(solution)/shard_map/all_to_all | solution.py:769
  53.6 24.3 %all-to-all-start.1 = ((f32[4,200,512]{2,1,0:T(8,128)}), f32[4,200,512]{2,1,0:T(8,128)S(1)}, u32[]{:S(2)}, u32[]{:S(2)}) async-start(f32[4,200,512]{2,1,0:T(8,128)} %pad_maximum_fusion), calls=%async_computation.1 | async-start | bytes 3276800 | tf_op jit(solution)/shard_map/all_to_all | solution.py:773
  77.9 32.6 %copy-start.1 = (f32[4,200,512]{2,1,0:T(8,128)}, f32[4,200,512]{2,1,0:T(8,128)S(1)}, u32[]{:S(2)}) copy-start(f32[4,200,512]{2,1,0:T(8,128)S(1)} %all-to-all-done.1.home.field) | copy-start | bytes 4915204
  116.9 13.8 %all-to-all-start.3 = ((f32[16,16,128]{2,1,0:T(8,128)}), f32[16,16,128]{2,1,0:T(8,128)S(1)}, u32[]{:S(2)}, u32[]{:S(2)}) async-start(f32[16,16,128]{2,1,0:T(8,128)} %get-tuple-element.22), calls=%async_computation.3 | async-start | bytes 262144 | tf_op jit(solution)/shard_map/all_to_all | solution.py:784
  121.4 7.4 %collective-permute-start = (f32[16,16,128]{2,1,0:T(8,128)}, f32[16,16,128]{2,1,0:T(8,128)S(1)}, u32[]{:S(2)}, u32[]{:S(2)}) collective-permute-start(f32[16,16,128]{2,1,0:T(8,128)} %get-tuple-element.23), channel_id=1, source_target_pairs={{0,1},{1,2},{2,3},{3,4},{4,5},{5,6},{6,7},{7,8},{8,9},{9,10},{10,1... | collective-permute-start | bytes 393224 | tf_op jit(solution)/shard_map/ppermute | solution.py:563
  123.5 7.3 %collective-permute-start.1 = (f32[16,16,128]{2,1,0:T(8,128)}, f32[16,16,128]{2,1,0:T(8,128)S(1)}, u32[]{:S(2)}, u32[]{:S(2)}) collective-permute-start(f32[16,16,128]{2,1,0:T(8,128)} %get-tuple-element.24), channel_id=1, source_target_pairs={{1,0},{2,1},{3,2},{4,3},{5,4},{6,5},{7,6},{8,7},{9,8},{10,9},{11,1... | collective-permute-start | bytes 393224 | tf_op jit(solution)/shard_map/ppermute | solution.py:563
  128.8 1.9 copy-start.9
  141.4 31.5 %all-to-all-start.4 = ((f32[16,128,128]{2,1,0:T(8,128)}), f32[16,128,128]{2,1,0:T(8,128)S(1)}, u32[]{:S(2)}, u32[]{:S(2)}) async-start(f32[16,128,128]{2,1,0:T(8,128)} %cols_screen.2), calls=%async_computation.4 | async-start | bytes 2097152 | tf_op jit(solution)/shard_map/all_to_all | solution.py:780
  181.2 6.4 %collective-permute-start.2 = (f32[16,1024]{1,0:T(8,128)}, f32[16,1024]{1,0:T(8,128)S(1)}, u32[]{:S(2)}, u32[]{:S(2)}) collective-permute-start(f32[16,1024]{1,0:T(8,128)} %get-tuple-element.26), channel_id=1, source_target_pairs={{0,4},{4,8},{8,12},{12,1},{1,5},{5,9},{9,13},{13,2},{2,6},{6,10},{... | collective-permute-start | bytes 196616 | tf_op jit(solution)/shard_map/ppermute | solution.py:563
  183.2 6.4 %collective-permute-start.3 = (f32[16,1024]{1,0:T(8,128)}, f32[16,1024]{1,0:T(8,128)S(1)}, u32[]{:S(2)}, u32[]{:S(2)}) collective-permute-start(f32[16,1024]{1,0:T(8,128)} %get-tuple-element.27), channel_id=1, source_target_pairs={{4,0},{8,4},{12,8},{1,12},{5,1},{9,5},{13,9},{2,13},{6,2},{10,6},{... | collective-permute-start | bytes 196616 | tf_op jit(solution)/shard_map/ppermute | solution.py:563
  187.6 1.9 copy-start.14
  239.6 29.8 %all-to-all-start.5 = ((f32[16,128,128]{2,1,0:T(8,128)}), f32[16,128,128]{2,1,0:T(8,128)S(1)}, u32[]{:S(2)}, u32[]{:S(2)}) async-start(f32[16,128,128]{2,1,0:T(8,128)} %get-tuple-element.28), calls=%async_computation.5 | async-start | bytes 2097152 | tf_op jit(solution)/shard_map/all_to_all | solution.py:780
  269.4 11.0 %copy-start.4 = (f32[16,128,128]{2,1,0:T(8,128)}, f32[16,128,128]{2,1,0:T(8,128)S(1)}, u32[]{:S(2)}) copy-start(f32[16,128,128]{2,1,0:T(8,128)S(1)} %all-to-all-done.5.field) | copy-start | bytes 3145732
  269.4 16.6 %all-to-all-start.8 = ((f32[16,16,128]{2,1,0:T(8,128)}), f32[16,16,128]{2,1,0:T(8,128)S(1)}, u32[]{:S(2)}, u32[]{:S(2)}) async-start(f32[16,16,128]{2,1,0:T(8,128)} %get-tuple-element.31), calls=%async_computation.8 | async-start | bytes 262144 | tf_op jit(solution)/shard_map/all_to_all | solution.py:784
  273.9 12.0 %collective-permute-start.4 = (f32[16,16,128]{2,1,0:T(8,128)}, f32[16,16,128]{2,1,0:T(8,128)S(1)}, u32[]{:S(2)}, u32[]{:S(2)}) collective-permute-start(f32[16,16,128]{2,1,0:T(8,128)} %get-tuple-element.32), channel_id=1, source_target_pairs={{0,1},{1,2},{2,3},{3,4},{4,5},{5,6},{6,7},{7,8},{8,9},{9,10},{10,1... | collective-permute-start | bytes 393224 | tf_op jit(solution)/shard_map/ppermute | solution.py:563
  276.0 10.0 %collective-permute-start.5 = (f32[16,16,128]{2,1,0:T(8,128)}, f32[16,16,128]{2,1,0:T(8,128)S(1)}, u32[]{:S(2)}, u32[]{:S(2)}) collective-permute-start(f32[16,16,128]{2,1,0:T(8,128)} %get-tuple-element.33), channel_id=1, source_target_pairs={{1,0},{2,1},{3,2},{4,3},{5,4},{6,5},{7,6},{8,7},{9,8},{10,9},{11,1... | collective-permute-start | bytes 393224 | tf_op jit(solution)/shard_map/ppermute | solution.py:563
  327.0 31.7 %all-to-all-start.6 = ((f32[16,128,128]{2,1,0:T(8,128)}), f32[16,128,128]{2,1,0:T(8,128)S(1)}, u32[]{:S(2)}, u32[]{:S(2)}) async-start(f32[16,128,128]{2,1,0:T(8,128)} %cols_send.2.field), calls=%async_computation.6 | async-start | bytes 2097152 | tf_op jit(solution)/shard_map/all_to_all | solution.py:780
  339.0 19.7 %collective-permute-start.6 = (f32[16,1024]{1,0:T(8,128)}, f32[16,1024]{1,0:T(8,128)S(1)}, u32[]{:S(2)}, u32[]{:S(2)}) collective-permute-start(f32[16,1024]{1,0:T(8,128)} %get-tuple-element.35), channel_id=1, source_target_pairs={{0,4},{4,8},{8,12},{12,1},{1,5},{5,9},{9,13},{13,2},{2,6},{6,10},{... | collective-permute-start | bytes 196616 | tf_op jit(solution)/shard_map/ppermute | solution.py:563
  342.3 16.4 %collective-permute-start.7 = (f32[16,1024]{1,0:T(8,128)}, f32[16,1024]{1,0:T(8,128)S(1)}, u32[]{:S(2)}, u32[]{:S(2)}) collective-permute-start(f32[16,1024]{1,0:T(8,128)} %get-tuple-element.36), channel_id=1, source_target_pairs={{4,0},{8,4},{12,8},{1,12},{5,1},{9,5},{13,9},{2,13},{6,2},{10,6},{... | collective-permute-start | bytes 196616 | tf_op jit(solution)/shard_map/ppermute | solution.py:563
  404.8 15.8 %all-to-all-start.12 = ((f32[4,256,128]{2,1,0:T(8,128)}), f32[4,256,128]{2,1,0:T(8,128)S(1)}, u32[]{:S(2)}, u32[]{:S(2)}) async-start(f32[4,256,128]{2,1,0:T(8,128)} %bitcast.19), calls=%async_computation.12 | async-start | bytes 1048576 | tf_op jit(solution)/shard_map/all_to_all | solution.py:810
  420.5 17.9 %all-to-all-start.11 = ((f32[4,128,512]{2,1,0:T(8,128)}), f32[4,128,512]{2,1,0:T(8,128)S(1)}, u32[]{:S(2)}, u32[]{:S(2)}) async-start(f32[4,128,512]{2,1,0:T(8,128)} %cols_send.3), calls=%async_computation.11 | async-start | bytes 2097152 | tf_op jit(solution)/shard_map/all_to_all | solution.py:806
  (12 other events, 10.2 us)

commit v2 on v1

--- a/solution.py
+++ b/solution.py
@@ -174,9 +174,15 @@
         chunks(INNER, last)
 
 
-def along_cols(read, writes, dft, table, xh, xl, y, z):
+def along_cols(main, read, writes, dft, table, xh, xl, y, z):
     outer = table.shape[0] // (2 * (1 + len(writes)))
     height = xh.shape[0] // outer
+
+    def every(body):
+        chunks(main, body)
+        if height > main:
+            body(main)
+
     row = lambda part: table[part : part + 1, :]
 
     def put(k, off, value):
@@ -193,7 +199,7 @@
                 value = times(value, (row(k), row(outer + k)))
             put(k, off, value)
 
-    chunks(height, first)
+    every(first)
     y[...] = triple(xh[...], xl[...], dft[2], dft[3])
     for n, write in enumerate(writes):
 
@@ -202,7 +208,7 @@
                 base = (2 + 2 * n) * outer + k
                 put(k, off, times(get(y, k, off), (row(base), row(base + outer))))
 
-        chunks(height, middle)
+        every(middle)
         z[...] = triple(xh[...], xl[...], dft[0], dft[1])
 
         def last(off, write=write):
@@ -215,7 +221,7 @@
             for b, value in enumerate(small_fft(values, 1)):
                 write(b, off, value)
 
-        chunks(height, last)
+        every(last)
 
 
 class Plan:
@@ -227,13 +233,17 @@
         self.width = cols_here // wind
         self.rows, self.cols = rows_here * wind, cols_here * cross
 
+    def local(self, w, c):
+        return w + (c % 2) * (self.wind - 1 - 2 * w)
+
     def slot(self, block):
-        return (block % self.wind) * self.cross + block // self.wind
+        c, i = block // self.wind, block % self.wind
+        return self.local(i, c) * self.cross + c
 
     def home_a(self, ref, a, off):
         n = a * INNER
         src, at = n // self.rows_here, n % self.rows_here
-        return tuple(ref[src, p, pl.ds(at + off, CHUNK), :] for p in (0, 1))
+        return tuple(ref[src, pl.ds(p * self.rows_here + at + off, CHUNK), :] for p in (0, 1))
 
     def spot_a(self, a, off):
         per = INNER // self.height
@@ -250,9 +260,26 @@
         for p in (0, 1):
             ref[s, pl.ds(p * self.height + at, CHUNK), :] = value[p]
 
+    def send_edges(self, ref):
+        h = self.height
+        for d in range(self.devices):
+            for p in (0, 1):
+                at = 2 * h + 4 * p
+                before = ref[d - 1, p * h + h - 2 : p * h + h, :] if d else jnp.zeros((2, self.width), F32)
+                after = ref[d + 1, p * h : p * h + 2, :] if d + 1 < self.devices else jnp.zeros((2, self.width), F32)
+                ref[d, at : at + 2, :] = before
+                ref[d, at + 2 : at + 4, :] = after
+
     def home_b(self, ref, b, off):
         per = self.cols_here // INNER
         return tuple(ref[b // per, pl.ds(p * self.height + off, CHUNK), pl.ds((b % per) * INNER, INNER)] for p in (0, 1))
+
+    def wide_b(self, ref, b, off):
+        if isinstance(off, int):
+            extra = ref[self.slot(b), 2 * self.height : 2 * self.height + 8, :]
+            turned = jnp.concatenate([extra[4:8], extra[0:4]], axis=0)
+            return jnp.concatenate([extra, extra], axis=0), jnp.concatenate([turned, turned], axis=0)
+        return self.flip_b(ref, b, off)
 
     def flip_b(self, ref, b, off):
         return tuple(ref[self.slot(b), pl.ds(p * self.height + off, CHUNK), :] for p in (0, 1))
@@ -279,8 +306,12 @@
             pltpu.VMEM((2 * INNER, wide), F32),
         ]
 
-    def work_b(self):
-        tall = (self.cols // INNER) * self.height
+    @property
+    def sent_wide(self):
+        return jax.ShapeDtypeStruct((self.devices, 2 * self.height + 8, self.width), F32)
+
+    def work_b(self, extra=0):
+        tall = (self.cols // INNER) * (self.height + extra)
         return [
             pltpu.VMEM((tall, 2 * INNER), BF16),
             pltpu.VMEM((tall, 2 * INNER), BF16),
@@ -289,26 +320,117 @@
         ]
 
 
-def call(body, outs, scratch, specs=None, name=None):
+def call(body, outs, scratch, name, near=(), near_outs=(), far=()):
     def run(*args):
-        in_specs = [SCALAR if a.dtype == jnp.int32 else WHOLE for a in args]
+        specs = [SCALAR if a.size <= 8 else WHOLE for a in args]
+        spaces = [pltpu.VMEM if i in near else pltpu.HBM if i in far else None for i in range(len(args))]
+        args = [pltpu.with_memory_space_constraint(a, space) if space else a for a, space in zip(args, spaces)]
         return pl.pallas_call(
             body,
-            out_shape=outs,
-            in_specs=in_specs,
+            out_shape=[pltpu.VMEM(o.shape, o.dtype) if i in near_outs else o for i, o in enumerate(outs)],
+            in_specs=specs,
             out_specs=[WHOLE] * len(outs),
             scratch_shapes=scratch,
             name=name,
+            compiler_params=pltpu.CompilerParams(vmem_limit_bytes=24 * 1024 * 1024),
         )(*args)
 
     return run
+
+
+def prepare(plan, field_real, field_imag, zone_map, alpha, zone_conductivity, place):
+    h = plan.height
+
+    def body(real, imag, zones, alpha, levels, place, field_a, *refs):
+        to_b, to_a, kappa = refs[: plan.cross], refs[plan.cross : -1], refs[-1]
+        w, c = place[0], place[1]
+        for n in range(plan.wind):
+            lanes = pl.ds(pl.multiple_of(plan.local(n, c) * plan.width, plan.width), plan.width)
+            field_a[n, 0 : plan.rows_here, :] = real[:, lanes]
+            field_a[n, plan.rows_here : 2 * plan.rows_here, :] = imag[:, lanes]
+
+        def step(off):
+            ids = zones[pl.ds(off, CHUNK), :]
+            value = jnp.zeros(ids.shape, F32)
+            for n in range(levels.shape[0]):
+                value = jnp.where(ids == n, levels[n], value)
+            kappa[pl.ds(off, CHUNK), :] = value
+
+        chunks(plan.rows_here, step)
+        for s, out in enumerate(to_b):
+            at = pl.multiple_of(lax.rem(c + s, plan.cross) * h, h)
+            out[0:h, :] = real[pl.ds(at, h), :]
+            out[h : 2 * h, :] = imag[pl.ds(at, h), :]
+            out[2 * h : 3 * h, :] = kappa[pl.ds(at, h), :]
+            out[3 * h :, :] = alpha[...]
+        for t, out in enumerate(to_a):
+            n = lax.rem(w + t, plan.wind)
+            lanes = pl.ds(pl.multiple_of(plan.local(n, c) * plan.width, plan.width), plan.width)
+            out[...] = kappa[:, lanes]
+
+    outs = [jax.ShapeDtypeStruct((plan.wind, 2 * plan.rows_here, plan.width), F32)]
+    outs += [jax.ShapeDtypeStruct((3 * h + 8, plan.cols_here), F32)] * plan.cross
+    outs += [jax.ShapeDtypeStruct((plan.rows_here, plan.width), F32)] * plan.wind
+    scratch = [pltpu.VMEM(field_real.shape, F32)]
+    return call(body, outs, scratch, "prepare", (), (0,), (0, 1, 2))(
+        field_real, field_imag, zone_map, alpha, zone_conductivity, place
+    )
+
+
+def home_rows(plan, parts, place):
+    h = plan.height
+
+    def body(*refs):
+        place, field, kappa, alpha = refs[plan.cross :]
+        for s, ref in enumerate(refs[: plan.cross]):
+            c = lax.rem(place[1] + plan.cross - s, plan.cross)
+            lanes = pl.ds(pl.multiple_of(c * plan.cols_here, plan.cols_here), plan.cols_here)
+            field[c] = ref[0 : 2 * h, :]
+            kappa[:, lanes] = ref[2 * h : 3 * h, :]
+            alpha[:, lanes] = ref[3 * h :, :]
+
+    outs = [
+        jax.ShapeDtypeStruct((plan.cross, 2 * h, plan.cols_here), F32),
+        jax.ShapeDtypeStruct((h, plan.cols), F32),
+        jax.ShapeDtypeStruct((8, plan.cols), F32),
+    ]
+    return call(body, outs, [], "home_rows", range(plan.cross))(*parts, place)
+
+
+def shifted(parts, axis):
+    size = lax.axis_size(axis)
+    return [parts[0]] + [lax.ppermute(parts[s], axis, [(i, (i + s) % size) for i in range(size)]) for s in range(1, size)]
+
+
+def in_order(parts, place, which, name):
+    size = len(parts)
+
+    def body(*refs):
+        place, out = refs[size], refs[-1]
+        for s, ref in enumerate(refs[:size]):
+            out[lax.rem(place[which] + size - s, size)] = ref[...]
+
+    out = jax.ShapeDtypeStruct((size,) + parts[0].shape, F32)
+    return call(body, [out], [], name, range(size))(*parts, place)[0]
+
+
+def home_screen(plan, parts, place):
+    def body(*refs):
+        place, out = refs[plan.wind], refs[-1]
+        for t, ref in enumerate(refs[: plan.wind]):
+            w = lax.rem(place[0] + plan.wind - t, plan.wind)
+            out[:, pl.ds(pl.multiple_of(plan.local(w, place[1]) * plan.width, plan.width), plan.width)] = ref[...]
+
+    out = jax.ShapeDtypeStruct((plan.rows_here, plan.cols_here), F32)
+    return call(body, [out], [], "home_screen", range(plan.wind))(*parts, place)[0]
 
 
 def rows_send(plan, read_field, dft, table, field):
     def body(dft, table, field, out, *work):
         along_rows(functools.partial(read_field, field), [functools.partial(plan.send_a, out)], dft, table, *work)
-
-    return call(body, [plan.sent], plan.work_a(), name="rows_send")(dft, table, field)[0]
+        plan.send_edges(out)
+
+    return call(body, [plan.sent_wide], plan.work_a(), "rows_send", (0, 1, 2), (0,))(dft, table, field)[0]
 
 
 def cols_send(plan, read_field, back, dft, table, field):
@@ -316,48 +438,42 @@
 
     def body(dft, table, field, out, *work):
         put = plan.back_b if back else plan.send_b
-        along_cols(functools.partial(read_field, field), [functools.partial(put, out)], dft, table, *work)
-
-    return call(body, [out], plan.work_b(), name="cols_send")(dft, table, field)[0]
-
-
-def cols_heat(plan, layer, dft, table, received, home):
+        along_cols(plan.height, functools.partial(read_field, field), [functools.partial(put, out)], dft, table, *work)
+
+    return call(body, [out], plan.work_b(), "cols_send", (0, 1, 2), () if back else (0,))(dft, table, field)[0]
+
+
+def cols_heat(plan, layer, copies, dft, table, received, absorption):
     blocks = plan.cols // INNER
     h = plan.height
-    per = plan.cols_here // INNER
-
-    def full(dft, table, received, home, part, totals, first, last, xh, xl, y, z, dep, dh, dl):
+
+    def body(dft, table, received, absorption, part, beside, totals, xh, xl, y, z, dh, dl):
         def write(b, off, value):
-            alpha = home[b // per, 3 * h + layer : 3 * h + layer + 1, pl.ds((b % per) * INNER, INNER)]
+            alpha = absorption[layer : layer + 1, pl.ds(b * INNER, INNER)]
             deposit = alpha * (value[0] * value[0] + value[1] * value[1])
-            spot = (pl.ds(off, CHUNK), pl.ds(b * INNER, INNER))
-            dep[spot] = deposit
+            lanes = pl.ds(b * INNER, INNER)
+            if isinstance(off, int):
+                beside[:, lanes] = deposit[0:8]
+                return
+            spot = (pl.ds(off, CHUNK), lanes)
             dh[spot], dl[spot] = split(deposit)
 
-        along_cols(functools.partial(plan.flip_b, received), [write], dft, table, xh, xl, y, z)
+        along_cols(h, functools.partial(plan.wide_b, received), [write], dft, table, xh, xl, y, z)
         ones = lower_ones(h)
         dot = functools.partial(jnp.dot, preferred_element_type=F32)
         part[...] = dot(ones, dh[...]) + dot(ones, dl[...])
         for b in range(blocks):
-            lanes = slice(b * INNER, (b + 1) * INNER)
-            at = (b % per) * INNER
-            first[b, 0:8, :] = dep[0:8, lanes]
-            last[b, 0:8, :] = dep[h - 8 : h, lanes]
-            first[b, 8:16, :] = home[b // per, 2 * h : 2 * h + 8, at : at + INNER]
-            last[b, 8:16, :] = home[b // per, 3 * h - 8 : 3 * h, at : at + INNER]
-            total = part[h - 1 : h, lanes]
-            for d in range(plan.devices):
+            total = part[h - 1 : h, b * INNER : (b + 1) * INNER]
+            for d in range(copies):
                 totals[d, b : b + 1, :] = total
 
-    edge = jax.ShapeDtypeStruct((blocks, 16, INNER), F32)
     outs = [
         jax.ShapeDtypeStruct((h, plan.cols), F32),
-        jax.ShapeDtypeStruct((plan.devices, blocks, INNER), F32),
-        edge,
-        edge,
+        jax.ShapeDtypeStruct((8, plan.cols), F32),
+        jax.ShapeDtypeStruct((copies, blocks, INNER), F32),
     ]
-    scratch = plan.work_b() + [pltpu.VMEM((h, plan.cols), F32), pltpu.VMEM((h, plan.cols), BF16), pltpu.VMEM((h, plan.cols), BF16)]
-    return call(full, outs, scratch, name="cols_heat")(dft, table, received, home)
+    scratch = plan.work_b(CHUNK) + [pltpu.VMEM((h, plan.cols), BF16), pltpu.VMEM((h, plan.cols), BF16)]
+    return call(body, outs, scratch, "cols_heat", (0, 1, 2), ())(dft, table, received, absorption)
 
 
 def conducted(mid, up, down, left, right, k_mid, k_up, k_down, k_left, k_right):
@@ -366,38 +482,51 @@
     return mid + (0.5 * conduct_rate) * flux
 
 
-def cols_screen(plan, read_field, dft, table, field, home, part, totals, above, below, me):
+def cols_turn(plan, read_field, dft, table, screen, field):
+    def body(dft, table, screen, field, out, *work):
+        def read(b, off):
+            return screened(read_field(field, b, off), screen[pl.ds(off, CHUNK), pl.ds(b * INNER, INNER)])
+
+        along_cols(plan.height, read, [functools.partial(plan.send_b, out)], dft, table, *work)
+
+    return call(body, [plan.sent], plan.work_b(), "cols_turn", (0, 1, 2), (0,))(dft, table, screen, field)[0]
+
+
+def cols_smooth(plan, kappa, above, below, part, beside, *rest):
     blocks = plan.cols // INNER
     h = plan.height
-    per = plan.cols_here // INNER
     PAD = 16
-
-    def body(dft, table, field, home, part, totals, above, below, me, out, xh, xl, y, z, h0, h1, kx):
-        place = me[0]
+    first, last = 0, plan.devices - 1
+
+    def body(kappa, above, below, part, beside, *refs):
+        sums, (me, screen, h0, h1, kx) = refs[:-5], refs[-5:]
+        place = me[0] * plan.cross + me[1]
         zeros = jnp.zeros((PAD, plan.cols), F32)
         for ref in (h0, kx, h1):
             ref[0:PAD, :] = zeros
             ref[h + PAD : h + 2 * PAD, :] = zeros
+        kx[PAD - 8 : PAD, :] = above[...]
+        kx[PAD : PAD + h, :] = kappa[...]
+        kx[PAD + h : PAD + h + 8, :] = below[...]
         upstream = jnp.zeros((blocks, INNER), F32)
-        for d in range(plan.devices):
-            upstream = upstream + jnp.where(d < place, totals[d], 0.0)
-        inner_low = jnp.where(place < plan.devices - 1, 1.0, 0.0)
+        if len(sums) == 1:
+            for d in range(plan.devices):
+                upstream = upstream + jnp.where(d < place, sums[0][d], 0.0)
+        else:
+            for s in range(1, plan.cross):
+                upstream = upstream + jnp.where(s <= me[1], sums[s - 1][...], 0.0)
+            for t in range(1, plan.wind):
+                upstream = upstream + jnp.where(t <= me[0], sums[plan.cross + t - 2][...], 0.0)
+        has_next = jnp.where(place < last, 1.0, 0.0)
         for b in range(blocks):
             lanes = slice(b * INNER, (b + 1) * INNER)
-            at = (b % per) * INNER
             base = upstream[b : b + 1, :]
             h0[PAD : PAD + h, lanes] = part[:, lanes] + base
-            value = base
-            for j in range(SMOOTH):
-                h0[PAD - 1 - j : PAD - j, lanes] = value
-                value = value - above[b, 7 - j : 8 - j, :]
-            value = base + part[h - 1 : h, lanes]
-            for j in range(SMOOTH):
-                value = value + below[b, j : j + 1, :]
-                h0[PAD + h + j : PAD + h + j + 1, lanes] = value * inner_low
-            kx[PAD - 8 : PAD, lanes] = above[b, 8:16, :]
-            kx[PAD : PAD + h, lanes] = home[b // per, 2 * h : 3 * h, at : at + INNER]
-            kx[PAD + h : PAD + h + 8, lanes] = below[b, 8:16, :]
+            h0[PAD - 1 : PAD, lanes] = base
+            h0[PAD - 2 : PAD - 1, lanes] = base - beside[1:2, lanes]
+            value = base + part[h - 1 : h, lanes] + beside[2:3, lanes]
+            h0[PAD + h : PAD + h + 1, lanes] = value * has_next
+            h0[PAD + h + 1 : PAD + h + 2, lanes] = (value + beside[3:4, lanes]) * has_next
         lane = lax.broadcasted_iota(jnp.int32, (8, plan.cols), 1)
         row = lax.broadcasted_iota(jnp.int32, (8, plan.cols), 0)
 
@@ -419,9 +548,12 @@
                 )
                 if masked:
                     n = row + base
-                    bad = ((n < PAD) & (place == 0)) | ((n >= PAD + h) & (place == plan.devices - 1))
+                    bad = ((n < PAD) & (place == first)) | ((n >= PAD + h) & (place == last))
                     new = jnp.where(bad, 0.0, new)
-                dst[pl.ds(base, 8), :] = new
+                if masked:
+                    dst[pl.ds(base, 8), :] = new
+                else:
+                    screen[pl.ds(base - PAD, 8), :] = -new
                 return carry
 
             lax.fori_loop(0, count, step, 0)
@@ -432,24 +564,16 @@
                 smooth(refs[n % 2], refs[(n + 1) % 2], PAD - 8, (h + 16) // 8, True)
             else:
                 smooth(refs[n % 2], refs[(n + 1) % 2], PAD, h // 8, False)
-        final = refs[SMOOTH % 2]
-
-        def read(b, off):
-            screen = -final[pl.ds(PAD + off, CHUNK), pl.ds(b * INNER, INNER)]
-            return screened(read_field(field, b, off), screen)
-
-        along_cols(read, [functools.partial(plan.send_b, out)], dft, table, xh, xl, y, z)
 
     tall = pltpu.VMEM((h + 2 * PAD, plan.cols), F32)
-    return call(body, [plan.sent], plan.work_b() + [tall] * 3, name="cols_screen")(
-        dft, table, field, home, part, totals, above, below, me
-    )[0]
-
-
-def rows_heat(plan, dft, table, received, alpha, home):
+    out = jax.ShapeDtypeStruct((h, plan.cols), F32)
+    return call(body, [out], [tall] * 3, "cols_smooth", (), (0,))(kappa, above, below, part, beside, *rest)[0]
+
+
+def rows_heat(plan, dft, table, received, alpha, kappa):
     width = plan.width
 
-    def body(dft, table, received, alpha, home, heat, edge_left, edge_right, xh, xl, y, z, dep):
+    def body(dft, table, received, alpha, kappa, heat, edge_left, edge_right, xh, xl, y, z, dep):
         def write(a, off, value):
             deposit = alpha[...] * (value[0] * value[0] + value[1] * value[1])
             rows = pl.ds(a * INNER + off, CHUNK)
@@ -469,29 +593,42 @@
             n = g * INNER
             src, at = n // plan.rows_here, n % plan.rows_here
             value = heat[n : n + INNER, :]
-            kap = home[src, 2, at : at + INNER, :]
-            mixed = jnp.where((lane >= 8) & (lane < 64), pltpu.roll(kap, 8, 1), value)
-            mixed = jnp.where((lane >= 64) & (lane < width - 8), pltpu.roll(kap, width - 8, 1), mixed)
+            kap = kappa[src, at : at + INNER, :]
+            mixed = jnp.where((lane >= 4) & (lane < 64), pltpu.roll(kap, 4, 1), value)
+            mixed = jnp.where((lane >= 64) & (lane < width - 4), pltpu.roll(kap, width - 4, 1), mixed)
             turned = mixed.T
-            edge_left[:, n : n + INNER] = turned[0:16, :]
-            edge_right[:, n : n + INNER] = turned[width - 16 : width, :]
-
-    edge = jax.ShapeDtypeStruct((16, plan.rows), F32)
+            edge_left[:, n : n + INNER] = turned[0:8, :]
+            edge_right[:, n : n + INNER] = turned[width - 8 : width, :]
+
+    edge = jax.ShapeDtypeStruct((8, plan.rows), F32)
     outs = [jax.ShapeDtypeStruct((plan.rows, width), F32), edge, edge]
     scratch = plan.work_a() + [pltpu.VMEM((plan.rows, 2 * width), BF16)]
-    return call(body, outs, scratch, name="rows_heat")(dft, table, received, alpha, home)
-
-
-def rows_screen(plan, read_field, sets, keep, dft, table, field, heat, home, from_left, from_right, me):
+    return call(body, outs, scratch, "rows_heat", (0, 1, 2), ())(dft, table, received, alpha, kappa)
+
+
+def rows_turn(plan, read_field, sets, wide, dft, table, screen, field):
+    def body(dft, table, screen, field, *refs):
+        outs, work = refs[:sets], refs[sets:]
+
+        def read(a, off):
+            return screened(read_field(field, a, off), screen[pl.ds(a * INNER + off, CHUNK), :])
+
+        along_rows(read, [functools.partial(plan.send_a, out) for out in outs], dft, table, *work)
+        if wide:
+            plan.send_edges(outs[0])
+
+    outs = [plan.sent_wide if wide and n == 0 else plan.sent for n in range(sets)]
+    return call(body, outs, plan.work_a(), "rows_turn", (0, 1, 2), range(sets))(dft, table, screen, field)
+
+
+def rows_smooth(plan, keep, heat, kappa, from_left, from_right, me):
     width = plan.width
     PAD = 8
     step_rows = 32
 
-    def body(dft, table, field, heat, home, from_left, from_right, me, *refs):
-        outs, rest = refs[:sets], refs[sets:]
-        screen, rest = (rest[0], rest[1:]) if keep else (rest[-1], rest[:-1])
-        xh, xl, y, z, h0, h1, kx = rest
-        place = me[0]
+    def body(heat, kappa, from_left, from_right, me, screen, *refs):
+        home_parts, h0, h1, kx = (refs[0] if keep else None, *refs[-3:])
+        place = me[1] * plan.wind + plan.local(me[0], me[1])
         zeros = jnp.zeros((PAD, 2 * width), F32)
         for ref in (h0, h1, kx):
             ref[0:PAD, :] = zeros
@@ -502,20 +639,19 @@
             src, at = n // plan.rows_here, n % plan.rows_here
             spot = slice(PAD + n, PAD + n + INNER)
             h0[spot, 0:width] = heat[n : n + INNER, :]
-            kx[spot, 0:width] = home[src, 2, at : at + INNER, :]
+            kx[spot, 0:width] = kappa[src, at : at + INNER, :]
             turned = jnp.concatenate(
-                [from_right[:, n : n + INNER], jnp.zeros((width - 32, INNER), F32), from_left[:, n : n + INNER]], axis=0
+                [from_right[:, n : n + INNER], jnp.zeros((width - 16, INNER), F32), from_left[:, n : n + INNER]], axis=0
             ).T
-            h0[spot, width : 2 * width] = jnp.where((lane < 8) | (lane >= width - 8), turned, 0.0)
-            kap = jnp.where(lane < 8, pltpu.roll(turned, width - 8, 1), 0.0)
-            kx[spot, width : 2 * width] = jnp.where(lane >= width - 8, pltpu.roll(turned, 8, 1), kap)
+            h0[spot, width : 2 * width] = jnp.where((lane < 4) | (lane >= width - 4), turned, 0.0)
+            kap = jnp.where(lane < 4, pltpu.roll(turned, width - 4, 1), 0.0)
+            kx[spot, width : 2 * width] = jnp.where(lane >= width - 4, pltpu.roll(turned, 4, 1), kap)
         wide = lax.broadcasted_iota(jnp.int32, (step_rows, 2 * width), 1)
         bad = (wide >= width) & (wide < width + width // 2) & (place == plan.devices - 1)
         bad = bad | ((wide >= width + width // 2) & (place == 0))
 
         def smooth(src, dst):
-            def step(i, carry):
-                base = pl.multiple_of(i * step_rows, step_rows)
+            def one(base):
                 value = src[pl.ds(base, step_rows + 16), :]
                 kap = kx[pl.ds(base, step_rows + 16), :]
                 mid, k_mid = value[8:-8], kap[8:-8]
@@ -524,9 +660,13 @@
                     k_mid, kap[7:-9], kap[9:-7], pltpu.roll(k_mid, 1, 1), pltpu.roll(k_mid, 2 * width - 1, 1),
                 )
                 dst(base, jnp.where(bad, 0.0, new))
+
+            def step(i, carry):
+                for n in range(4):
+                    one(pl.multiple_of((4 * i + n) * step_rows, step_rows))
                 return carry
 
-            lax.fori_loop(0, plan.rows // step_rows, step, 0)
+            lax.fori_loop(0, plan.rows // (4 * step_rows), step, 0)
 
         def into(ref):
             def put(base, value):
@@ -536,25 +676,20 @@
 
         def into_screen(base, value):
             screen[pl.ds(base, step_rows), :] = -value[:, :width]
+            if keep:
+                block = lax.rem(base // plan.rows_here + plan.wind - me[0], plan.wind)
+                at = pl.multiple_of(lax.rem(base, plan.rows_here), step_rows)
+                home_parts[block, pl.ds(at, step_rows), :] = -value[:, :width]
 
         refs = [h0, h1]
         for n in range(SMOOTH):
             smooth(refs[n % 2], into(refs[(n + 1) % 2]) if n < SMOOTH - 1 else into_screen)
 
-        def read(a, off):
-            return screened(read_field(field, a, off), screen[pl.ds(a * INNER + off, CHUNK), :])
-
-        along_rows(read, [functools.partial(plan.send_a, out) for out in outs], dft, table, xh, xl, y, z)
-
-    outs = [plan.sent] * sets
-    flat = (plan.rows, width)
     tall = pltpu.VMEM((plan.rows + 2 * PAD, 2 * width), F32)
-    scratch = plan.work_a() + [tall] * 3
+    outs = [jax.ShapeDtypeStruct((plan.rows, width), F32)]
     if keep:
-        outs = outs + [jax.ShapeDtypeStruct(flat, F32)]
-    else:
-        scratch = scratch + [pltpu.VMEM(flat, F32)]
-    return call(body, outs, scratch, name="rows_screen")(dft, table, field, heat, home, from_left, from_right, me)
+        outs.append(jax.ShapeDtypeStruct((plan.wind, plan.rows_here, width), F32))
+    return call(body, outs, [tall] * 3, "rows_smooth", (), (0,))(heat, kappa, from_left, from_right, me)
 
 
 def next_prev(value_up, value_down, axes, order):
@@ -751,64 +886,63 @@
         return wide_device(field_real, field_imag, absorb_index, absorb_table, zone_map, zone_conductivity)
     wind, cross = plan.wind, plan.cross
     w, c = lax.axis_index("wind"), lax.axis_index("cross")
-    row_place = jnp.reshape(w * cross + c, (1,)).astype(jnp.int32)
-    col_place = jnp.reshape(c * wind + w, (1,)).astype(jnp.int32)
+    place = jnp.stack([w, c]).astype(jnp.int32)
     grid_axes = ("wind", "cross")
-
-    conductivity = jnp.zeros(field_real.shape, F32)
-    for zone_no in range(zone_conductivity.shape[0]):
-        conductivity = jnp.where(zone_map == zone_no, zone_conductivity[zone_no], conductivity)
+    columns_order = [plan.slot(i) for i in range(plan.devices)]
+
+    def exchange(x, axes):
+        return lax.all_to_all(x, axes, split_axis=0, concat_axis=0, tiled=True)
+
+    def flip(x):
+        return exchange(x, grid_axes)
+
     alpha = jnp.zeros(absorb_index.shape, F32)
     for level in range(absorb_table.shape[1]):
         alpha = jnp.where(absorb_index == level, absorb_table[:, level : level + 1], alpha)
     alpha = alpha * (1.0 / plan.rows)
-    alpha_a = lax.dynamic_slice_in_dim(alpha, w * plan.width, plan.width, axis=1)
-
-    stacked = jnp.stack([field_real, field_imag, conductivity])
-    to_a = stacked.reshape(3, plan.rows_here, wind, plan.width).transpose(2, 0, 1, 3)
-    home_a = lax.all_to_all(to_a, "wind", split_axis=0, concat_axis=0, tiled=True)
-    to_b = [s.reshape(cross, plan.height, plan.cols_here) for s in (field_real, field_imag, conductivity)]
-    alpha_rows = jnp.pad(alpha, ((0, -LAYERS % 8), (0, 0)))
-    to_b.append(jnp.broadcast_to(alpha_rows[None], (cross,) + alpha_rows.shape))
-    home_b = lax.all_to_all(jnp.concatenate(to_b, axis=1), "cross", split_axis=0, concat_axis=0, tiled=True)
+    alpha_a = lax.dynamic_slice_in_dim(alpha, plan.local(w, c) * plan.width, plan.width, axis=1)
+    alpha = jnp.pad(alpha, ((0, 8 - LAYERS), (0, 0)))
+    to_a, *blocks = prepare(plan, field_real, field_imag, zone_map, alpha, zone_conductivity, place)
+    home_a = exchange(to_a, "wind")
+    home_b, kappa_b, alpha_b = home_rows(plan, shifted(blocks[:cross], "cross"), place)
 
     dft = jnp.asarray(dft_matrices())
     tab_a = lambda *shares: jnp.asarray(row_table(plan.rows, shares))
     tab_b = lambda *shares: jnp.asarray(chirp_columns(plan.cols, shares))
 
-    def flip(x):
-        return lax.all_to_all(x, grid_axes, split_axis=0, concat_axis=0, tiled=True)
-
-    def heat_b(layer, share, received):
-        part, totals, first, last = cols_heat(plan, layer, dft, tab_b(share), received, home_b)
-        totals = lax.all_to_all(totals, grid_axes, split_axis=0, concat_axis=0, tiled=True)
-        above, below = next_prev(last, first, grid_axes, list(range(plan.devices)))
-        return part, totals, above, below, row_place
-
-    def heat_a(layer, share, received):
-        heat, left, right = rows_heat(plan, dft, tab_a(share), received, alpha_a[layer : layer + 1], home_a)
-        from_left, from_right = next_prev(right, left, grid_axes, [plan.slot(i) for i in range(plan.devices)])
-        return heat, home_a, from_left, from_right, col_place
-
+    def smooth_a(layer, share, keep, received):
+        heat, left, right = rows_heat(plan, dft, tab_a(share), received, alpha_a[layer : layer + 1], kappa_a)
+        from_left, from_right = next_prev(right, left, grid_axes, columns_order)
+        return rows_smooth(plan, keep, heat, kappa_a, from_left, from_right, place)
+
+    home_a, home_b = lax.optimization_barrier((home_a, home_b))
     sent = rows_send(plan, plan.home_a, dft, tab_a(0.5), home_a)
-    parts = heat_b(0, 0.5, flip(sent))
-    sent = cols_screen(plan, plan.home_b, dft, tab_b(0.5), home_b, home_b, *parts)
-    parts = heat_a(0, 0.5, flip(sent))
-    sent_middle, sent_field = rows_screen(plan, plan.home_a, 2, False, dft, tab_a(1.5, 1.0), home_a, *parts)
+    received, kappa_blocks = lax.optimization_barrier((flip(sent), blocks[cross:]))
+    kappa_blocks = shifted(kappa_blocks, "wind")
+    above, below = next_prev(kappa_b[-8:], kappa_b[:8], grid_axes, list(range(plan.devices)))
+    part, beside, totals = cols_heat(plan, 0, plan.devices, dft, tab_b(0.5), received, alpha_b)
+    screen = cols_smooth(plan, kappa_b, above, below, part, beside, flip(totals), place)
+    sent = cols_turn(plan, plan.home_b, dft, tab_b(0.5), screen, home_b)
+    sent, kappa_blocks = lax.optimization_barrier((sent, kappa_blocks))
+    kappa_a = in_order(kappa_blocks, place, 0, "kappa_a")
+    (screen,) = smooth_a(0, 0.5, False, flip(sent))
+    sent_middle, sent_field = rows_turn(plan, plan.home_a, 2, True, dft, tab_a(1.5, 1.0), screen, home_a)
     middle = flip(sent_middle)
     field_b = cols_send(plan, plan.flip_b, False, dft, tab_b(1.0), flip(sent_field))
     field_a = flip(field_b)
-    parts = heat_b(1, 1.5, middle)
-    sent = cols_screen(plan, plan.flip_b, dft, tab_b(0.5), field_b, home_b, *parts)
-    parts = heat_a(1, 0.5, flip(sent))
-    sent, screen = rows_screen(plan, plan.flip_a, 1, True, dft, tab_a(1.0), field_a, *parts)
-    back = cols_send(plan, plan.flip_b, True, dft, tab_b(1.0), flip(sent))
-    back = lax.all_to_all(back, "cross", split_axis=0, concat_axis=0, tiled=True)
+    part, beside, totals = cols_heat(plan, 1, 1, dft, tab_b(1.5), middle, alpha_b)
+    across = shifted([totals[0]] * cross, "cross")
+    along = shifted([sum(across[1:], across[0])] * wind, "wind")
+    screen = cols_smooth(plan, kappa_b, above, below, part, beside, *across[1:], *along[1:], place)
+    sent = cols_turn(plan, plan.flip_b, dft, tab_b(0.5), screen, field_b)
+    screen, home_parts = smooth_a(1, 0.5, True, flip(sent))
+    (sent,) = rows_turn(plan, plan.flip_a, 1, False, dft, tab_a(1.0), screen, field_a)
+    received, home_parts = lax.optimization_barrier((flip(sent), home_parts))
+    back = cols_send(plan, plan.flip_b, True, dft, tab_b(1.0), received)
+    screen = home_screen(plan, shifted([home_parts[t] for t in range(wind)], "wind"), place)
+    back = exchange(back, "cross")
     out_real = back[:, : plan.height].reshape(field_real.shape)
     out_imag = back[:, plan.height :].reshape(field_real.shape)
-    screen = screen.reshape(wind, plan.rows_here, plan.width)
-    screen = lax.all_to_all(screen, "wind", split_axis=0, concat_axis=0, tiled=True)
-    screen = screen.transpose(1, 0, 2).reshape(field_real.shape)
     return (out_real, out_imag, screen)
 
 

time: 446 us -> 366 us (0.82)
  waiting for transfers between devices: 126 us -> 89.7 us
  Pallas kernels: 98.8 us -> 73.4 us
  other arithmetic: 10.1 us -> 0.85 us
    all_to_all x9 -> x6, waiting for transfers between devices: 121 us -> 37.5 us  [exchange(): return lax.all_to_all(x, axes, split_axis=0, concat_axis=0, tiled=True)]
    ppermute x0 -> x15, waiting for transfers between devices: none -> 28.3 us  [shifted(): lax.ppermute(parts[s], axis, [(i, (i + s) % size) for i in range(size)])]
    pallas_call x11 -> x19, Pallas kernels: 98.8 us -> 73.4 us  [run(): pl.pallas_call(body, out_shape=[pltpu.VMEM(o.shape, o.dtype) if i in near...]
    ppermute x4 -> x3, waiting for transfers between devices: 1.42 us -> 22 us  [next_prev(): lax.ppermute(value_up, axes, up)]
    ppermute x0 -> x15, starting transfers between devices: none -> 15.2 us  [shifted(): lax.ppermute(parts[s], axis, [(i, (i + s) % size) for i in range(size)])]
    all_to_all x9 -> x6, starting transfers between devices: 41.3 us -> 29 us  [exchange(): return lax.all_to_all(x, axes, split_axis=0, concat_axis=0, tiled=True)]
    select_n x1 -> x0, other arithmetic: 5.27 us -> none  [on_device(): jnp.where(zone_map == zone_no, zone_conductivity[zone_no], conductivity)]
    ppermute x4 -> x3, starting transfers between devices: 15.3 us -> 10.9 us  [next_prev(): lax.ppermute(value_down, axes, down)]
  transfers between devices with their start and end apart: 17 -> 27, of which waited for: 11 -> 14; matrix products, arithmetic and copies ran while one was open for 1% -> 0% of each run, Pallas kernels for 7% -> 8%
where the time goes in v2:
time: 366 us; the launch traced here: 362 us
  blocking collectives  124 us (34%)
  waiting for transfers between devices  89.7 us (25%)
  Pallas kernels  73.4 us (20%)
  starting transfers between devices  62.4 us (17%)
  local copies, waits for them, and re-layouts  10.4 us (3%)
    all_to_all x4, blocking collectives, exchange(): return lax.all_to_all(x, axes, split_axis=0, concat_axis=0, tiled=True)  124 us
    pallas_call x19, Pallas kernels, run(): pl.pallas_call(body, out_shape=[pltpu.VMEM(o.shape, o.dtype) if i in near...  73.4 us
    all_to_all x6, waiting for transfers between devices, exchange(): return lax.all_to_all(x, axes, split_axis=0, concat_axis=0, tiled=True)  37.5 us
    all_to_all x6, starting transfers between devices, exchange(): return lax.all_to_all(x, axes, split_axis=0, concat_axis=0, tiled=True)  29 us
    ppermute x15, waiting for transfers between devices, shifted(): lax.ppermute(parts[s], axis, [(i, (i + s) % size) for i in range(size)])  28.3 us
    ppermute x3, waiting for transfers between devices, next_prev(): lax.ppermute(value_up, axes, up)  22 us
    ppermute x15, starting transfers between devices, shifted(): lax.ppermute(parts[s], axis, [(i, (i + s) % size) for i in range(size)])  15.2 us
    ppermute x3, starting transfers between devices, next_prev(): lax.ppermute(value_down, axes, down)  10.9 us
  transfers between devices with their start and end apart: 27, of which 14 were waited for; matrix products, arithmetic and copies ran while one was open for 0% of the time, Pallas kernels for 8%

profile of v2, /device:TPU:16, one launch (start us, length us, event | category | flops | bytes accessed | tf_op | source)
XLA Modules:
  0.0 361.9 jit_solution(15316634215390733494)
XLA Ops:
  7.3 5.2 %all-to-all-start = ((f32[4,512,128]{2,1,0:T(8,128)}), f32[4,512,128]{2,1,0:T(8,128)S(1)}, u32[]{:S(2)}, u32[]{:S(2)}) async-start(f32[4,512,128]{2,1,0:T(8,128)} %get-tuple-element.50), calls=%async_computation | async-start | bytes 2097152 | tf_op jit(solution)/shard_map/all_to_all | solution.py:894
  15.4 8.2 %collective-permute-done.refs_1_ = f32[200,512]{1,0:T(8,128)S(1)} collective-permute-done((f32[200,512]{1,0:T(8,128)S(1)}, f32[200,512]{1,0:T(8,128)S(1)}, u32[]{:S(2)}, u32[]{:S(2)}) %collective-permute-start) | collective-permute-done | bytes 409632 | tf_op jit(solution)/shard_map/ppermute | solution.py:402
  24.9 7.1 %collective-permute-done.2.refs_3_ = f32[200,512]{1,0:T(8,128)S(1)} collective-permute-done((f32[200,512]{1,0:T(8,128)S(1)}, f32[200,512]{1,0:T(8,128)S(1)}, u32[]{:S(2)}, u32[]{:S(2)}) %collective-permute-start.2) | collective-permute-done | bytes 409632 | tf_op jit(solution)/shard_map/ppermute | solution.py:402
  39.1 33.3 %all_to_all.50.received = f32[16,136,128]{2,1,0:T(8,128)S(1)} all-to-all(f32[16,136,128]{2,1,0:T(8,128)S(1)} %rows_send.1), channel_id=1, replica_groups=mesh['beams'=2,'wind'=4,'cross'=4] {'wind','cross'}, dimensions={0} | all-to-all | bytes 2228224 | tf_op jit(solution)/shard_map/all_to_all | solution.py:894
  78.5 5.4 %all-to-all-start.2 = ((f32[16,16,128]{2,1,0:T(8,128)}), f32[16,16,128]{2,1,0:T(8,128)S(1)}, u32[]{:S(2)}, u32[]{:S(2)}) async-start(f32[16,16,128]{2,1,0:T(8,128)} %copy-done.16), calls=%async_computation.2 | async-start | bytes 262144 | tf_op jit(solution)/shard_map/all_to_all | solution.py:894
  89.0 4.5 %collective-permute-start.4 = (f32[8,2048]{1,0:T(8,128)S(1)}, f32[8,2048]{1,0:T(8,128)S(1)}, u32[]{:S(2)}, u32[]{:S(2)}) collective-permute-start(f32[8,2048]{1,0:T(8,128)S(1)} %get-tuple-element.101), channel_id=1, source_target_pairs={{1,0},{2,1},{3,2},{4,3},{5,4},{6,5},{7,6},{8,7},{9,8},{10,9},{11,1... | collective-permute-start | bytes 196616 | tf_op jit(solution)/shard_map/ppermute | solution.py:698
  93.5 7.7 %collective-permute-done.3.above = f32[8,2048]{1,0:T(8,128)S(1)} collective-permute-done((f32[8,2048]{1,0:T(8,128)S(1)}, f32[8,2048]{1,0:T(8,128)S(1)}, u32[]{:S(2)}, u32[]{:S(2)}) %collective-permute-start.3) | collective-permute-done | bytes 65568 | tf_op jit(solution)/shard_map/ppermute | solution.py:698
  106.5 4.9 %cols_turn.2 = f32[16,128,128]{2,1,0:T(8,128)} custom-call(bf16[4,256,256]{2,1,0:T(8,128)(2,1)S(1)} %copy-done, f32[64,128]{1,0:T(8,128)S(1)} %copy-done.11, f32[64,2048]{1,0:T(8,128)S(1)} %cols_smooth.2.screen, f32[4,128,512]{2,1,0:T(8,128)S(1)} %get-tuple-element.62.field), custom_call_target="tpu_custom_call" | custom-call | tf_op jit(solution)/shard_map/cols_turn/pallas_call | solution.py:328
  116.9 24.0 %all-to-all-done.3.received = f32[16,128,128]{2,1,0:T(8,128)S(1)} async-done(((f32[16,128,128]{2,1,0:T(8,128)}), f32[16,128,128]{2,1,0:T(8,128)S(1)}, u32[]{:S(2)}, u32[]{:S(2)}) %all-to-all-start.3) | async-done | bytes 1048608 | tf_op jit(solution)/shard_map/all_to_all | solution.py:894
  140.9 4.8 %rows_heat.2 = (f32[1024,128]{1,0:T(8,128)S(1)}, f32[8,1024]{1,0:T(8,128)S(1)}, f32[8,1024]{1,0:T(8,128)S(1)}) custom-call(bf16[4,256,256]{2,1,0:T(8,128)(2,1)S(1)} %copy-done, f32[128,128]{1,0:T(8,128)S(1)} %copy-done.4, f32[16,128,128]{2,1,0:T(8,128)S(1)} %all-to-all-done.3.received, f32[1,128]{1,0:T(1,128)S(1)} %get-tuple-element.104.alpha, ...), custom_call_target="tpu_custom_call" | custom-call | tf_op jit(solution)/shard_map/rows_heat/pallas_call | solution.py:328
  153.6 4.5 %rows_smooth.2.screen = f32[1024,128]{1,0:T(8,128)S(1)} custom-call(f32[1024,128]{1,0:T(8,128)S(1)} %get-tuple-element.72.heat, f32[4,256,128]{2,1,0:T(8,128)S(1)} %kappa_a.1.kappa, f32[8,1024]{1,0:T(8,128)S(1)} %collective-permute-done.8.from_left, f32[8,1024]{1,0:T(8,128)S(1)} %collective-permute-done.9.from_right, ...), custom_call_target="tpu_custom_call" | custom-call | tf_op jit(solution)/shard_map/rows_smooth/pallas_call | solution.py:328
  158.1 7.0 %rows_turn.2 = (f32[16,136,128]{2,1,0:T(8,128)S(1)}, f32[16,128,128]{2,1,0:T(8,128)S(1)}) custom-call(bf16[4,256,256]{2,1,0:T(8,128)(2,1)S(1)} %copy-done, f32[128,128]{1,0:T(8,128)S(1)} %copy-done.21, f32[1024,128]{1,0:T(8,128)S(1)} %rows_smooth.2.screen, f32[4,512,128]{2,1,0:T(8,128)S(1)} %all-to-all-done.field), custom_call_target="tpu_custom_call" | custom-call | tf_op jit(solution)/shard_map/rows_turn/pallas_call | solution.py:328
  165.2 31.4 %all_to_all.51.received = f32[16,136,128]{2,1,0:T(8,128)S(1)} all-to-all(f32[16,136,128]{2,1,0:T(8,128)S(1)} %get-tuple-element.75), channel_id=1, replica_groups=mesh['beams'=2,'wind'=4,'cross'=4] {'wind','cross'}, dimensions={0} | all-to-all | bytes 2228224 | tf_op jit(solution)/shard_map/all_to_all | solution.py:894
  196.6 5.9 %all-to-all-start.5 = ((f32[16,128,128]{2,1,0:T(8,128)}), f32[16,128,128]{2,1,0:T(8,128)S(1)}, u32[]{:S(2)}, u32[]{:S(2)}) async-start(f32[16,128,128]{2,1,0:T(8,128)} %copy-done.3), calls=%async_computation.5 | async-start | bytes 2097152 | tf_op jit(solution)/shard_map/all_to_all | solution.py:894
  215.8 12.3 %all-to-all-done.5.field = f32[16,128,128]{2,1,0:T(8,128)S(1)} async-done(((f32[16,128,128]{2,1,0:T(8,128)}), f32[16,128,128]{2,1,0:T(8,128)S(1)}, u32[]{:S(2)}, u32[]{:S(2)}) %all-to-all-start.5) | async-done | bytes 1048608 | tf_op jit(solution)/shard_map/all_to_all | solution.py:894
  235.6 5.2 %cols_turn.3 = f32[16,128,128]{2,1,0:T(8,128)S(1)} custom-call(bf16[4,256,256]{2,1,0:T(8,128)(2,1)S(1)} %copy-done, f32[64,128]{1,0:T(8,128)S(1)} %copy-done.11, f32[64,2048]{1,0:T(8,128)S(1)} %cols_smooth.3.screen, f32[16,128,128]{2,1,0:T(8,128)} %cols_send.2.field), custom_call_target="tpu_custom_call" | custom-call | tf_op jit(solution)/shard_map/cols_turn/pallas_call | solution.py:328
  240.8 29.4 %all_to_all.52.received = f32[16,128,128]{2,1,0:T(8,128)S(1)} all-to-all(f32[16,128,128]{2,1,0:T(8,128)S(1)} %cols_turn.3), channel_id=1, replica_groups=mesh['beams'=2,'wind'=4,'cross'=4] {'wind','cross'}, dimensions={0} | all-to-all | bytes 2097152 | tf_op jit(solution)/shard_map/all_to_all | solution.py:894
  270.2 4.6 %all-to-all-start.7 = ((f32[16,128,128]{2,1,0:T(8,128)}), f32[16,128,128]{2,1,0:T(8,128)S(1)}, u32[]{:S(2)}, u32[]{:S(2)}) async-start(f32[16,128,128]{2,1,0:T(8,128)} %cols_send.2.field), calls=%async_computation.7 | async-start | bytes 2097152 | tf_op jit(solution)/shard_map/all_to_all | solution.py:894
  274.8 4.8 %rows_heat.3 = (f32[1024,128]{1,0:T(8,128)S(1)}, f32[8,1024]{1,0:T(8,128)S(1)}, f32[8,1024]{1,0:T(8,128)S(1)}) custom-call(bf16[4,256,256]{2,1,0:T(8,128)(2,1)S(1)} %copy-done, f32[128,128]{1,0:T(8,128)S(1)} %copy-done.4, f32[16,128,128]{2,1,0:T(8,128)S(1)} %all_to_all.52.received, f32[1,128]{1,0:T(1,128)S(1)} %get-tuple-element.103.alpha, ...), custom_call_target="tpu_custom_call" | custom-call | tf_op jit(solution)/shard_map/rows_heat/pallas_call | solution.py:328
  285.5 14.3 %collective-permute-done.16.from_left = f32[8,1024]{1,0:T(8,128)S(1)} collective-permute-done((f32[8,1024]{1,0:T(8,128)S(1)}, f32[8,1024]{1,0:T(8,128)S(1)}, u32[]{:S(2)}, u32[]{:S(2)}) %collective-permute-start.16) | collective-permute-done | bytes 32800 | tf_op jit(solution)/shard_map/ppermute | solution.py:698
  299.8 4.5 %rows_smooth.3 = (f32[1024,128]{1,0:T(8,128)S(1)}, f32[4,256,128]{2,1,0:T(8,128)S(1)}) custom-call(f32[1024,128]{1,0:T(8,128)S(1)} %get-tuple-element.80.heat, f32[4,256,128]{2,1,0:T(8,128)S(1)} %kappa_a.1.kappa, f32[8,1024]{1,0:T(8,128)S(1)} %collective-permute-done.16.from_left, f32[8,1024]{1,0:T(8,128)S(1)} %collective-permute-done.17.from_right, ...), custom_call_target="tpu_custom_call" | custom-call | tf_op jit(solution)/shard_map/rows_smooth/pallas_call | solution.py:328
  304.3 4.4 %rows_turn.3 = f32[16,128,128]{2,1,0:T(8,128)S(1)} custom-call(bf16[4,256,256]{2,1,0:T(8,128)(2,1)S(1)} %copy-done, f32[128,128]{1,0:T(8,128)S(1)} %copy-done.20, f32[1024,128]{1,0:T(8,128)S(1)} %get-tuple-element.83.screen, f32[16,128,128]{2,1,0:T(8,128)S(1)} %all-to-all-done.7.field), custom_call_target="tpu_custom_call" | custom-call | tf_op jit(solution)/shard_map/rows_turn/pallas_call | solution.py:328
  308.7 30.0 %all_to_all.53.field = f32[16,128,128]{2,1,0:T(8,128)S(1)} all-to-all(f32[16,128,128]{2,1,0:T(8,128)S(1)} %rows_turn.3), channel_id=1, replica_groups=mesh['beams'=2,'wind'=4,'cross'=4] {'wind','cross'}, dimensions={0} | all-to-all | bytes 2097152 | tf_op jit(solution)/shard_map/all_to_all | solution.py:894
  349.1 9.4 %collective-permute-done.18.refs_1_ = f32[256,128]{1,0:T(8,128)S(1)} collective-permute-done((f32[256,128]{1,0:T(8,128)S(1)}, f32[256,128]{1,0:T(8,128)S(1)}, u32[]{:S(2)}, u32[]{:S(2)}) %collective-permute-start.18) | collective-permute-done | bytes 131104 | tf_op jit(solution)/shard_map/ppermute | solution.py:402
  (121 shorter events, 88.0 us)
Async XLA Ops:
  7.3 27.7 %all-to-all-start = ((f32[4,512,128]{2,1,0:T(8,128)}), f32[4,512,128]{2,1,0:T(8,128)S(1)}, u32[]{:S(2)}, u32[]{:S(2)}) async-start(f32[4,512,128]{2,1,0:T(8,128)} %get-tuple-element.50), calls=%async_computation | async-start | bytes 2097152 | tf_op jit(solution)/shard_map/all_to_all | solution.py:894
  12.5 11.1 %collective-permute-start = (f32[200,512]{1,0:T(8,128)S(1)}, f32[200,512]{1,0:T(8,128)S(1)}, u32[]{:S(2)}, u32[]{:S(2)}) collective-permute-start(f32[200,512]{1,0:T(8,128)S(1)} %get-tuple-element.46), channel_id=1, source_target_pairs={{0,1},{1,2},{2,3},{3,0},{4,5},{5,6},{6,7},{7,4},{8,9},{9,10},{10,1... | collective-permute-start | bytes 1228808 | tf_op jit(solution)/shard_map/ppermute | solution.py:402
  12.5 12.4 %collective-permute-start.1 = (f32[200,512]{1,0:T(8,128)S(1)}, f32[200,512]{1,0:T(8,128)S(1)}, u32[]{:S(2)}, u32[]{:S(2)}) collective-permute-start(f32[200,512]{1,0:T(8,128)S(1)} %get-tuple-element.47), channel_id=1, source_target_pairs={{0,2},{1,3},{2,0},{3,1},{4,6},{5,7},{6,4},{7,5},{8,10},{9,11},{10,... | collective-permute-start | bytes 1228808 | tf_op jit(solution)/shard_map/ppermute | solution.py:402
  14.0 18.0 %collective-permute-start.2 = (f32[200,512]{1,0:T(8,128)S(1)}, f32[200,512]{1,0:T(8,128)S(1)}, u32[]{:S(2)}, u32[]{:S(2)}) collective-permute-start(f32[200,512]{1,0:T(8,128)S(1)} %get-tuple-element.48), channel_id=1, source_target_pairs={{0,3},{1,0},{2,1},{3,2},{4,7},{5,4},{6,5},{7,6},{8,11},{9,8},{10,9... | collective-permute-start | bytes 1228808 | tf_op jit(solution)/shard_map/ppermute | solution.py:402
  78.5 22.8 %all-to-all-start.2 = ((f32[16,16,128]{2,1,0:T(8,128)}), f32[16,16,128]{2,1,0:T(8,128)S(1)}, u32[]{:S(2)}, u32[]{:S(2)}) async-start(f32[16,16,128]{2,1,0:T(8,128)} %copy-done.16), calls=%async_computation.2 | async-start | bytes 262144 | tf_op jit(solution)/shard_map/all_to_all | solution.py:894
  83.9 27.5 %collective-permute-start.5 = (f32[256,128]{1,0:T(8,128)}, f32[256,128]{1,0:T(8,128)}, u32[]{:S(2)}, u32[]{:S(2)}) collective-permute-start(f32[256,128]{1,0:T(8,128)} %copy-done.28), channel_id=1, source_target_pairs={{0,4},{4,8},{8,12},{12,0},{1,5},{5,9},{9,13},{13,1},{2,6},{6,10},{... | collective-permute-start | bytes 393224 | tf_op jit(solution)/shard_map/ppermute | solution.py:402
  85.4 26.1 %collective-permute-start.6 = (f32[256,128]{1,0:T(8,128)}, f32[256,128]{1,0:T(8,128)}, u32[]{:S(2)}, u32[]{:S(2)}) collective-permute-start(f32[256,128]{1,0:T(8,128)} %copy-done.27), channel_id=1, source_target_pairs={{0,8},{4,12},{8,0},{12,4},{1,9},{5,13},{9,1},{13,5},{2,10},{6,14},... | collective-permute-start | bytes 393224 | tf_op jit(solution)/shard_map/ppermute | solution.py:402
  85.9 25.6 %collective-permute-start.7 = (f32[256,128]{1,0:T(8,128)}, f32[256,128]{1,0:T(8,128)}, u32[]{:S(2)}, u32[]{:S(2)}) collective-permute-start(f32[256,128]{1,0:T(8,128)} %copy-done.26), channel_id=1, source_target_pairs={{0,12},{4,0},{8,4},{12,8},{1,13},{5,1},{9,5},{13,9},{2,14},{6,2},{... | collective-permute-start | bytes 393224 | tf_op jit(solution)/shard_map/ppermute | solution.py:402
  87.0 14.2 %collective-permute-start.3 = (f32[8,2048]{1,0:T(8,128)S(1)}, f32[8,2048]{1,0:T(8,128)S(1)}, u32[]{:S(2)}, u32[]{:S(2)}) collective-permute-start(f32[8,2048]{1,0:T(8,128)S(1)} %get-tuple-element.102), channel_id=1, source_target_pairs={{0,1},{1,2},{2,3},{3,4},{4,5},{5,6},{6,7},{7,8},{8,9},{9,10},{10,1... | collective-permute-start | bytes 196616 | tf_op jit(solution)/shard_map/ppermute | solution.py:698
  89.0 12.3 %collective-permute-start.4 = (f32[8,2048]{1,0:T(8,128)S(1)}, f32[8,2048]{1,0:T(8,128)S(1)}, u32[]{:S(2)}, u32[]{:S(2)}) collective-permute-start(f32[8,2048]{1,0:T(8,128)S(1)} %get-tuple-element.101), channel_id=1, source_target_pairs={{1,0},{2,1},{3,2},{4,3},{5,4},{6,5},{7,6},{8,7},{9,8},{10,9},{11,1... | collective-permute-start | bytes 196616 | tf_op jit(solution)/shard_map/ppermute | solution.py:698
  111.4 29.5 %all-to-all-start.3 = ((f32[16,128,128]{2,1,0:T(8,128)}), f32[16,128,128]{2,1,0:T(8,128)S(1)}, u32[]{:S(2)}, u32[]{:S(2)}) async-start(f32[16,128,128]{2,1,0:T(8,128)} %cols_turn.2), calls=%async_computation.3 | async-start | bytes 2097152 | tf_op jit(solution)/shard_map/all_to_all | solution.py:894
  145.7 6.0 %collective-permute-start.8 = (f32[8,1024]{1,0:T(8,128)S(1)}, f32[8,1024]{1,0:T(8,128)S(1)}, u32[]{:S(2)}, u32[]{:S(2)}) collective-permute-start(f32[8,1024]{1,0:T(8,128)S(1)} %get-tuple-element.73), channel_id=1, source_target_pairs={{0,4},{4,8},{8,12},{12,13},{13,9},{9,5},{5,1},{1,2},{2,6},{6,10},{... | collective-permute-start | bytes 98312 | tf_op jit(solution)/shard_map/ppermute | solution.py:698
  147.8 5.8 %collective-permute-start.9 = (f32[8,1024]{1,0:T(8,128)S(1)}, f32[8,1024]{1,0:T(8,128)S(1)}, u32[]{:S(2)}, u32[]{:S(2)}) collective-permute-start(f32[8,1024]{1,0:T(8,128)S(1)} %get-tuple-element.74), channel_id=1, source_target_pairs={{4,0},{8,4},{12,8},{13,12},{9,13},{5,9},{1,5},{2,1},{6,2},{10,6},{... | collective-permute-start | bytes 98312 | tf_op jit(solution)/shard_map/ppermute | solution.py:698
  196.6 31.5 %all-to-all-start.5 = ((f32[16,128,128]{2,1,0:T(8,128)}), f32[16,128,128]{2,1,0:T(8,128)S(1)}, u32[]{:S(2)}, u32[]{:S(2)}) async-start(f32[16,128,128]{2,1,0:T(8,128)} %copy-done.3), calls=%async_computation.5 | async-start | bytes 2097152 | tf_op jit(solution)/shard_map/all_to_all | solution.py:894
  212.3 19.9 %collective-permute-start.13 = (f32[16,128]{1,0:T(8,128)S(1)}, f32[16,128]{1,0:T(8,128)S(1)}, u32[]{:S(2)}, u32[]{:S(2)}) collective-permute-start(f32[16,128]{1,0:T(8,128)S(1)} %add_add_fusion), channel_id=1, source_target_pairs={{0,4},{4,8},{8,12},{12,0},{1,5},{5,9},{9,13},{13,1},{2,6},{6,10},{... | collective-permute-start | bytes 24584 | tf_op jit(solution)/shard_map/ppermute | solution.py:402
  213.9 18.3 %collective-permute-start.14 = (f32[16,128]{1,0:T(8,128)S(1)}, f32[16,128]{1,0:T(8,128)S(1)}, u32[]{:S(2)}, u32[]{:S(2)}) collective-permute-start(f32[16,128]{1,0:T(8,128)S(1)} %add_add_fusion), channel_id=1, source_target_pairs={{0,8},{4,12},{8,0},{12,4},{1,9},{5,13},{9,1},{13,5},{2,10},{6,14},... | collective-permute-start | bytes 24584 | tf_op jit(solution)/shard_map/ppermute | solution.py:402
  214.4 17.8 %collective-permute-start.15 = (f32[16,128]{1,0:T(8,128)S(1)}, f32[16,128]{1,0:T(8,128)S(1)}, u32[]{:S(2)}, u32[]{:S(2)}) collective-permute-start(f32[16,128]{1,0:T(8,128)S(1)} %add_add_fusion), channel_id=1, source_target_pairs={{0,12},{4,0},{8,4},{12,8},{1,13},{5,1},{9,5},{13,9},{2,14},{6,2},{... | collective-permute-start | bytes 24584 | tf_op jit(solution)/shard_map/ppermute | solution.py:402
  270.2 34.0 %all-to-all-start.7 = ((f32[16,128,128]{2,1,0:T(8,128)}), f32[16,128,128]{2,1,0:T(8,128)S(1)}, u32[]{:S(2)}, u32[]{:S(2)}) async-start(f32[16,128,128]{2,1,0:T(8,128)} %cols_send.2.field), calls=%async_computation.7 | async-start | bytes 2097152 | tf_op jit(solution)/shard_map/all_to_all | solution.py:894
  279.6 20.1 %collective-permute-start.16 = (f32[8,1024]{1,0:T(8,128)S(1)}, f32[8,1024]{1,0:T(8,128)S(1)}, u32[]{:S(2)}, u32[]{:S(2)}) collective-permute-start(f32[8,1024]{1,0:T(8,128)S(1)} %get-tuple-element.81), channel_id=1, source_target_pairs={{0,4},{4,8},{8,12},{12,13},{13,9},{9,5},{5,1},{1,2},{2,6},{6,10},{... | collective-permute-start | bytes 98312 | tf_op jit(solution)/shard_map/ppermute | solution.py:698
  283.0 16.8 %collective-permute-start.17 = (f32[8,1024]{1,0:T(8,128)S(1)}, f32[8,1024]{1,0:T(8,128)S(1)}, u32[]{:S(2)}, u32[]{:S(2)}) collective-permute-start(f32[8,1024]{1,0:T(8,128)S(1)} %get-tuple-element.82), channel_id=1, source_target_pairs={{4,0},{8,4},{12,8},{13,12},{9,13},{5,9},{1,5},{2,1},{6,2},{10,6},{... | collective-permute-start | bytes 98312 | tf_op jit(solution)/shard_map/ppermute | solution.py:698
  342.9 18.0 %all-to-all-start.9 = ((f32[4,128,512]{2,1,0:T(8,128)}), f32[4,128,512]{2,1,0:T(8,128)S(1)}, u32[]{:S(2)}, u32[]{:S(2)}) async-start(f32[4,128,512]{2,1,0:T(8,128)} %cols_send.3), calls=%async_computation.9 | async-start | bytes 2097152 | tf_op jit(solution)/shard_map/all_to_all | solution.py:894
  346.4 12.0 %collective-permute-start.18 = (f32[256,128]{1,0:T(8,128)S(1)}, f32[256,128]{1,0:T(8,128)S(1)}, u32[]{:S(2)}, u32[]{:S(2)}) collective-permute-start(f32[256,128]{1,0:T(8,128)S(1)} %get-tuple-element.99), channel_id=1, source_target_pairs={{0,4},{4,8},{8,12},{12,0},{1,5},{5,9},{9,13},{13,1},{2,6},{6,10},{... | collective-permute-start | bytes 393224 | tf_op jit(solution)/shard_map/ppermute | solution.py:402
  346.5 12.0 %collective-permute-start.19 = (f32[256,128]{1,0:T(8,128)S(1)}, f32[256,128]{1,0:T(8,128)S(1)}, u32[]{:S(2)}, u32[]{:S(2)}) collective-permute-start(f32[256,128]{1,0:T(8,128)S(1)} %get-tuple-element.98), channel_id=1, source_target_pairs={{0,8},{4,12},{8,0},{12,4},{1,9},{5,13},{9,1},{13,5},{2,10},{6,14},... | collective-permute-start | bytes 393224 | tf_op jit(solution)/shard_map/ppermute | solution.py:402
  348.2 11.3 %collective-permute-start.20 = (f32[256,128]{1,0:T(8,128)S(1)}, f32[256,128]{1,0:T(8,128)S(1)}, u32[]{:S(2)}, u32[]{:S(2)}) collective-permute-start(f32[256,128]{1,0:T(8,128)S(1)} %get-tuple-element.97), channel_id=1, source_target_pairs={{0,12},{4,0},{8,4},{12,8},{1,13},{5,1},{9,5},{13,9},{2,14},{6,2},{... | collective-permute-start | bytes 393224 | tf_op jit(solution)/shard_map/ppermute | solution.py:402
  (32 other events, 457.8 us)

commit v3 on v2

--- a/solution.py
+++ b/solution.py
@@ -8,6 +8,7 @@
 from jax.experimental import pallas as pl
 from jax.experimental.pallas import tpu as pltpu
 from jax.sharding import PartitionSpec as P
+
 
 LAYERS = 2
 ITERS = 2
@@ -52,9 +53,22 @@
     return np.concatenate(tables, axis=0).astype(np.float32)
 
 
-def row_table(length, shares):
-    cols = chirp_columns(length, shares).T
+def row_table(length):
+    cols = chirp_columns(length, ()).T
     return np.pad(cols, ((0, 0), (0, -cols.shape[1] % 128)))
+
+
+def row_blocks(length, share):
+    outer = length // INNER
+    ids = np.arange(INNER)
+    forward = np.exp(-2j * np.pi * (np.outer(ids, ids) % INNER) / INNER)
+    blocks = []
+    for k in range(outer):
+        p = k + outer * ids
+        freq = np.where(p < length // 2, p, p - length) / length
+        block = forward.conj() @ (np.exp(-1j * share * diffraction * freq * freq)[:, None] / length * forward)
+        blocks.append(np.stack(split_np(np.block([[block.real, -block.imag], [block.imag, block.real]]))))
+    return np.stack(blocks)
 
 
 def split(x):
@@ -133,45 +147,38 @@
     lax.fori_loop(0, count // CHUNK, step, 0)
 
 
-def along_rows(read, writes, dft, table, xh, xl, y, z):
-    outer = xh.shape[1] // 128
-    rows = lambda k: pl.ds(k * 128, 128)
+def along_rows(read, write, matrices, table, xh, z):
+    outer = matrices.shape[0]
+    width = z.shape[1] // outer
+    lanes = lambda k: pl.ds(k * width, width)
     col = lambda part, off: table[pl.ds(off, CHUNK), part : part + 1]
-
-    def put(k, off, value):
-        for at, v in ((0, value[0]), (INNER, value[1])):
-            xh[pl.ds(at + off, CHUNK), rows(k)], xl[pl.ds(at + off, CHUNK), rows(k)] = split(v)
 
     def first(off):
         for k, value in enumerate(small_fft([read(a, off) for a in range(outer)], -1)):
             if k:
                 value = times(value, (col(k, off), col(outer + k, off)))
-            put(k, off, value)
+            for at, v in ((0, value[0]), (INNER, value[1])):
+                high, low = split(v)
+                xh[pl.ds(at + off, CHUNK), pl.ds(2 * k * width, width)] = high
+                xh[pl.ds(at + off, CHUNK), pl.ds((2 * k + 1) * width, width)] = low
+
+    def last(off):
+        values = []
+        for k in range(outer):
+            value = (z[pl.ds(off, CHUNK), lanes(k)], z[pl.ds(INNER + off, CHUNK), lanes(k)])
+            if k:
+                value = times(value, (col(k, off), -col(outer + k, off)))
+            values.append(value)
+        for a, value in enumerate(small_fft(values, 1)):
+            write(a, off, value)
 
     chunks(INNER, first)
-    y[...] = triple(dft[0], dft[1], xh[...], xl[...])
-    for n, write in enumerate(writes):
-
-        def middle(off, n=n):
-            for k in range(outer):
-                value = (y[pl.ds(off, CHUNK), rows(k)], y[pl.ds(INNER + off, CHUNK), rows(k)])
-                base = (2 + 2 * n) * outer + k
-                put(k, off, times(value, (col(base, off), col(base + outer, off))))
-
-        chunks(INNER, middle)
-        z[...] = triple(dft[2], dft[3], xh[...], xl[...])
-
-        def last(off, write=write):
-            values = []
-            for k in range(outer):
-                value = (z[pl.ds(off, CHUNK), rows(k)], z[pl.ds(INNER + off, CHUNK), rows(k)])
-                if k:
-                    value = times(value, (col(k, off), -col(outer + k, off)))
-                values.append(value)
-            for a, value in enumerate(small_fft(values, 1)):
-                write(a, off, value)
-
-        chunks(INNER, last)
+    dot = functools.partial(jnp.dot, preferred_element_type=F32)
+    for k in range(outer):
+        both = dot(matrices[k, 0], xh[:, 2 * k * width : (2 * k + 2) * width])
+        low = dot(matrices[k, 1], xh[:, 2 * k * width : (2 * k + 1) * width])
+        z[:, k * width : (k + 1) * width] = both[:, :width] + both[:, width:] + low
+    chunks(INNER, last)
 
 
 def along_cols(main, read, writes, dft, table, xh, xl, y, z):
@@ -270,6 +277,11 @@
                 ref[d, at : at + 2, :] = before
                 ref[d, at + 2 : at + 4, :] = after
 
+    def edges(self, value, left, right, at):
+        turned = value.T
+        left[:, at : at + INNER] = turned[0:8, :]
+        right[:, at : at + INNER] = turned[self.width - 8 : self.width, :]
+
     def home_b(self, ref, b, off):
         per = self.cols_here // INNER
         return tuple(ref[b // per, pl.ds(p * self.height + off, CHUNK), pl.ds((b % per) * INNER, INNER)] for p in (0, 1))
@@ -300,9 +312,7 @@
     def work_a(self):
         wide = (self.rows // INNER) * self.width
         return [
-            pltpu.VMEM((2 * INNER, wide), BF16),
-            pltpu.VMEM((2 * INNER, wide), BF16),
-            pltpu.VMEM((2 * INNER, wide), F32),
+            pltpu.VMEM((2 * INNER, 2 * wide), BF16),
             pltpu.VMEM((2 * INNER, wide), F32),
         ]
 
@@ -320,9 +330,9 @@
         ]
 
 
-def call(body, outs, scratch, name, near=(), near_outs=(), far=()):
+def call(body, outs, scratch, near=(), near_outs=(), far=()):
     def run(*args):
-        specs = [SCALAR if a.size <= 8 else WHOLE for a in args]
+        specs = [SCALAR if a.size <= 16 else WHOLE for a in args]
         spaces = [pltpu.VMEM if i in near else pltpu.HBM if i in far else None for i in range(len(args))]
         args = [pltpu.with_memory_space_constraint(a, space) if space else a for a, space in zip(args, spaces)]
         return pl.pallas_call(
@@ -331,70 +341,80 @@
             in_specs=specs,
             out_specs=[WHOLE] * len(outs),
             scratch_shapes=scratch,
-            name=name,
             compiler_params=pltpu.CompilerParams(vmem_limit_bytes=24 * 1024 * 1024),
         )(*args)
 
     return run
 
 
-def prepare(plan, field_real, field_imag, zone_map, alpha, zone_conductivity, place):
+def prepare_field(plan, field_real, field_imag, place):
     h = plan.height
 
-    def body(real, imag, zones, alpha, levels, place, field_a, *refs):
-        to_b, to_a, kappa = refs[: plan.cross], refs[plan.cross : -1], refs[-1]
+    def body(real, imag, place, to_b, *to_a):
+        for c in range(plan.cross):
+            to_b[c, 0:h, :] = real[c * h : (c + 1) * h, :]
+            to_b[c, h : 2 * h, :] = imag[c * h : (c + 1) * h, :]
+        for t, out in enumerate(to_a):
+            n = lax.rem(place[0] + t, plan.wind)
+            lanes = pl.ds(pl.multiple_of(plan.local(n, place[1]) * plan.width, plan.width), plan.width)
+            out[0 : plan.rows_here, :] = real[:, lanes]
+            out[plan.rows_here : 2 * plan.rows_here, :] = imag[:, lanes]
+
+    outs = [jax.ShapeDtypeStruct((plan.cross, 2 * h, plan.cols_here), F32)]
+    outs += [jax.ShapeDtypeStruct((2 * plan.rows_here, plan.width), F32)] * plan.wind
+    return call(body, outs, [], (), (), (0, 1))(field_real, field_imag, place)
+
+
+def prepare(plan, zone_map, absorb_index, absorb_table, zone_conductivity, place):
+    h = plan.height
+
+    def picked(ids, count, level):
+        value = jnp.zeros(ids.shape, F32)
+        for n in range(count):
+            value = jnp.where(ids == n, level(n), value)
+        return value
+
+    def body(zones, index, table, levels, place, *refs):
+        to_b, to_a, alpha_a, kappa, alpha = refs[: plan.cross], refs[plan.cross : -3], refs[-3], refs[-2], refs[-1]
         w, c = place[0], place[1]
-        for n in range(plan.wind):
-            lanes = pl.ds(pl.multiple_of(plan.local(n, c) * plan.width, plan.width), plan.width)
-            field_a[n, 0 : plan.rows_here, :] = real[:, lanes]
-            field_a[n, plan.rows_here : 2 * plan.rows_here, :] = imag[:, lanes]
 
         def step(off):
-            ids = zones[pl.ds(off, CHUNK), :]
-            value = jnp.zeros(ids.shape, F32)
-            for n in range(levels.shape[0]):
-                value = jnp.where(ids == n, levels[n], value)
-            kappa[pl.ds(off, CHUNK), :] = value
+            kappa[pl.ds(off, CHUNK), :] = picked(zones[pl.ds(off, CHUNK), :], levels.shape[0], lambda n: levels[n])
 
         chunks(plan.rows_here, step)
+        alpha[...] = jnp.zeros_like(alpha)
+        for layer in range(LAYERS):
+            value = picked(index[layer : layer + 1, :], table.shape[1], lambda n: table[layer, n])
+            alpha[layer : layer + 1, :] = value * (1.0 / plan.rows)
+        alpha_a[...] = alpha[:, pl.ds(pl.multiple_of(plan.local(w, c) * plan.width, plan.width), plan.width)]
         for s, out in enumerate(to_b):
-            at = pl.multiple_of(lax.rem(c + s, plan.cross) * h, h)
-            out[0:h, :] = real[pl.ds(at, h), :]
-            out[h : 2 * h, :] = imag[pl.ds(at, h), :]
-            out[2 * h : 3 * h, :] = kappa[pl.ds(at, h), :]
-            out[3 * h :, :] = alpha[...]
+            out[0:h, :] = kappa[pl.ds(pl.multiple_of(lax.rem(c + s, plan.cross) * h, h), h), :]
+            out[h:, :] = alpha[...]
         for t, out in enumerate(to_a):
             n = lax.rem(w + t, plan.wind)
             lanes = pl.ds(pl.multiple_of(plan.local(n, c) * plan.width, plan.width), plan.width)
             out[...] = kappa[:, lanes]
 
-    outs = [jax.ShapeDtypeStruct((plan.wind, 2 * plan.rows_here, plan.width), F32)]
-    outs += [jax.ShapeDtypeStruct((3 * h + 8, plan.cols_here), F32)] * plan.cross
+    outs = [jax.ShapeDtypeStruct((h + 8, plan.cols_here), F32)] * plan.cross
     outs += [jax.ShapeDtypeStruct((plan.rows_here, plan.width), F32)] * plan.wind
-    scratch = [pltpu.VMEM(field_real.shape, F32)]
-    return call(body, outs, scratch, "prepare", (), (0,), (0, 1, 2))(
-        field_real, field_imag, zone_map, alpha, zone_conductivity, place
-    )
+    outs.append(jax.ShapeDtypeStruct((8, plan.width), F32))
+    scratch = [pltpu.VMEM(zone_map.shape, F32), pltpu.VMEM((8, plan.cols_here), F32)]
+    return call(body, outs, scratch, (), (), (0,))(zone_map, absorb_index, absorb_table, zone_conductivity, place)
 
 
 def home_rows(plan, parts, place):
     h = plan.height
 
     def body(*refs):
-        place, field, kappa, alpha = refs[plan.cross :]
+        place, kappa, alpha = refs[plan.cross :]
         for s, ref in enumerate(refs[: plan.cross]):
             c = lax.rem(place[1] + plan.cross - s, plan.cross)
             lanes = pl.ds(pl.multiple_of(c * plan.cols_here, plan.cols_here), plan.cols_here)
-            field[c] = ref[0 : 2 * h, :]
-            kappa[:, lanes] = ref[2 * h : 3 * h, :]
-            alpha[:, lanes] = ref[3 * h :, :]
-
-    outs = [
-        jax.ShapeDtypeStruct((plan.cross, 2 * h, plan.cols_here), F32),
-        jax.ShapeDtypeStruct((h, plan.cols), F32),
-        jax.ShapeDtypeStruct((8, plan.cols), F32),
-    ]
-    return call(body, outs, [], "home_rows", range(plan.cross))(*parts, place)
+            kappa[:, lanes] = ref[0:h, :]
+            alpha[:, lanes] = ref[h:, :]
+
+    outs = [jax.ShapeDtypeStruct((h, plan.cols), F32), jax.ShapeDtypeStruct((8, plan.cols), F32)]
+    return call(body, outs, [])(*parts, place)
 
 
 def shifted(parts, axis):
@@ -402,7 +422,7 @@
     return [parts[0]] + [lax.ppermute(parts[s], axis, [(i, (i + s) % size) for i in range(size)]) for s in range(1, size)]
 
 
-def in_order(parts, place, which, name):
+def in_order(parts, place, which):
     size = len(parts)
 
     def body(*refs):
@@ -411,26 +431,41 @@
             out[lax.rem(place[which] + size - s, size)] = ref[...]
 
     out = jax.ShapeDtypeStruct((size,) + parts[0].shape, F32)
-    return call(body, [out], [], name, range(size))(*parts, place)[0]
+    return call(body, [out], [], range(size))(*parts, place)[0]
 
 
 def home_screen(plan, parts, place):
+    h = plan.height
+
     def body(*refs):
-        place, out = refs[plan.wind], refs[-1]
+        place, out = refs[plan.cross], refs[-1]
+        for s, ref in enumerate(refs[: plan.cross]):
+            c = lax.rem(place[1] + plan.cross - s, plan.cross)
+            out[pl.ds(pl.multiple_of(c * h, h), h), :] = ref[...]
+
+    out = jax.ShapeDtypeStruct((plan.rows_here, plan.cols_here), F32)
+    return call(body, [out], [])(*parts, place)[0]
+
+
+def rows_kappa(plan, parts, place):
+    def body(*refs):
+        place, out, left, right = refs[plan.wind :]
         for t, ref in enumerate(refs[: plan.wind]):
             w = lax.rem(place[0] + plan.wind - t, plan.wind)
-            out[:, pl.ds(pl.multiple_of(plan.local(w, place[1]) * plan.width, plan.width), plan.width)] = ref[...]
-
-    out = jax.ShapeDtypeStruct((plan.rows_here, plan.cols_here), F32)
-    return call(body, [out], [], "home_screen", range(plan.wind))(*parts, place)[0]
-
-
-def rows_send(plan, read_field, dft, table, field):
+            out[pl.ds(pl.multiple_of(w * plan.rows_here, plan.rows_here), plan.rows_here), :] = ref[...]
+        for g in range(plan.rows // INNER):
+            plan.edges(out[g * INNER : (g + 1) * INNER, :], left, right, g * INNER)
+
+    edge = jax.ShapeDtypeStruct((8, plan.rows), F32)
+    outs = [jax.ShapeDtypeStruct((plan.rows, plan.width), F32), edge, edge]
+    return call(body, outs, [], range(plan.wind))(*parts, place)
+
+
+def rows_field(plan, read_field, dft, table, field):
     def body(dft, table, field, out, *work):
-        along_rows(functools.partial(read_field, field), [functools.partial(plan.send_a, out)], dft, table, *work)
-        plan.send_edges(out)
-
-    return call(body, [plan.sent_wide], plan.work_a(), "rows_send", (0, 1, 2), (0,))(dft, table, field)[0]
+        along_rows(functools.partial(read_field, field), functools.partial(plan.send_a, out), dft, table, *work)
+
+    return call(body, [plan.sent], plan.work_a(), (0, 1, 2), (0,))(dft, table, field)[0]
 
 
 def cols_send(plan, read_field, back, dft, table, field):
@@ -440,7 +475,7 @@
         put = plan.back_b if back else plan.send_b
         along_cols(plan.height, functools.partial(read_field, field), [functools.partial(put, out)], dft, table, *work)
 
-    return call(body, [out], plan.work_b(), "cols_send", (0, 1, 2), () if back else (0,))(dft, table, field)[0]
+    return call(body, [out], plan.work_b(), (0, 1, 2), () if back else (0,))(dft, table, field)[0]
 
 
 def cols_heat(plan, layer, copies, dft, table, received, absorption):
@@ -473,7 +508,7 @@
         jax.ShapeDtypeStruct((copies, blocks, INNER), F32),
     ]
     scratch = plan.work_b(CHUNK) + [pltpu.VMEM((h, plan.cols), BF16), pltpu.VMEM((h, plan.cols), BF16)]
-    return call(body, outs, scratch, "cols_heat", (0, 1, 2), ())(dft, table, received, absorption)
+    return call(body, outs, scratch, (0, 1, 2), ())(dft, table, received, absorption)
 
 
 def conducted(mid, up, down, left, right, k_mid, k_up, k_down, k_left, k_right):
@@ -482,24 +517,29 @@
     return mid + (0.5 * conduct_rate) * flux
 
 
-def cols_turn(plan, read_field, dft, table, screen, field):
-    def body(dft, table, screen, field, out, *work):
+def cols_turn(plan, read_field, sets, dft, table, screen, field):
+    def body(dft, table, screen, field, *refs):
+        outs, work = refs[:sets], refs[sets:]
+
         def read(b, off):
             return screened(read_field(field, b, off), screen[pl.ds(off, CHUNK), pl.ds(b * INNER, INNER)])
 
-        along_cols(plan.height, read, [functools.partial(plan.send_b, out)], dft, table, *work)
-
-    return call(body, [plan.sent], plan.work_b(), "cols_turn", (0, 1, 2), (0,))(dft, table, screen, field)[0]
-
-
-def cols_smooth(plan, kappa, above, below, part, beside, *rest):
+        along_cols(plan.height, read, [functools.partial(plan.send_b, out) for out in outs], dft, table, *work)
+
+    return call(body, [plan.sent] * sets, plan.work_b(), (0, 1, 2), range(sets))(
+        dft, table, screen, field
+    )
+
+
+def cols_smooth(plan, keep, kappa, above, below, part, beside, *rest):
     blocks = plan.cols // INNER
     h = plan.height
     PAD = 16
     first, last = 0, plan.devices - 1
 
     def body(kappa, above, below, part, beside, *refs):
-        sums, (me, screen, h0, h1, kx) = refs[:-5], refs[-5:]
+        count = plan.cross + 1 if keep else 1
+        sums, me, outs, (h0, h1, kx, kept) = refs[: -5 - count], refs[-5 - count], refs[-4 - count : -4], refs[-4:]
         place = me[0] * plan.cross + me[1]
         zeros = jnp.zeros((PAD, plan.cols), F32)
         for ref in (h0, kx, h1):
@@ -553,7 +593,13 @@
                 if masked:
                     dst[pl.ds(base, 8), :] = new
                 else:
-                    screen[pl.ds(base - PAD, 8), :] = -new
+                    at = pl.ds(base - PAD, 8)
+                    if not keep:
+                        outs[0][at, :] = -new
+                        return carry
+                    for b in range(blocks):
+                        outs[0][plan.slot(b), at, :] = -new[:, b * INNER : (b + 1) * INNER]
+                    kept[pl.ds(base - PAD, 8), :] = -new
                 return carry
 
             lax.fori_loop(0, count, step, 0)
@@ -564,22 +610,34 @@
                 smooth(refs[n % 2], refs[(n + 1) % 2], PAD - 8, (h + 16) // 8, True)
             else:
                 smooth(refs[n % 2], refs[(n + 1) % 2], PAD, h // 8, False)
+        if keep:
+            for s, out in enumerate(outs[1:]):
+                c = lax.rem(me[1] + s, plan.cross)
+                lanes = pl.ds(pl.multiple_of(c * plan.cols_here, plan.cols_here), plan.cols_here)
+                out[...] = kept[:, lanes]
 
     tall = pltpu.VMEM((h + 2 * PAD, plan.cols), F32)
-    out = jax.ShapeDtypeStruct((h, plan.cols), F32)
-    return call(body, [out], [tall] * 3, "cols_smooth", (), (0,))(kappa, above, below, part, beside, *rest)[0]
-
-
-def rows_heat(plan, dft, table, received, alpha, kappa):
+    flat = (h, plan.cols)
+    if keep:
+        outs = [jax.ShapeDtypeStruct((plan.devices, h, plan.width), F32)]
+        outs += [jax.ShapeDtypeStruct((h, plan.cols_here), F32)] * plan.cross
+    else:
+        outs = [jax.ShapeDtypeStruct(flat, F32)]
+    return call(body, outs, [tall] * 3 + [pltpu.VMEM(flat, F32)], (), () if keep else (0,))(
+        kappa, above, below, part, beside, *rest
+    )
+
+
+def rows_heat(plan, dft, table, received, alpha):
     width = plan.width
 
-    def body(dft, table, received, alpha, kappa, heat, edge_left, edge_right, xh, xl, y, z, dep):
+    def body(dft, table, received, alpha, heat, edge_left, edge_right, xh, z, dep):
         def write(a, off, value):
             deposit = alpha[...] * (value[0] * value[0] + value[1] * value[1])
             rows = pl.ds(a * INNER + off, CHUNK)
             dep[rows, 0:width], dep[rows, width : 2 * width] = split(deposit)
 
-        along_rows(functools.partial(plan.flip_a, received), [write], dft, table, xh, xl, y, z)
+        along_rows(functools.partial(plan.flip_a, received), write, dft, table, xh, z)
         tile = 2 * INNER
         ones = lower_ones(tile)
         carry = jnp.zeros((1, width), F32)
@@ -588,64 +646,46 @@
             value = both[:, :width] + both[:, width:] + carry
             heat[g * tile : (g + 1) * tile, :] = value
             carry = value[tile - 1 : tile, :]
-        lane = lax.broadcasted_iota(jnp.int32, (INNER, width), 1)
         for g in range(plan.rows // INNER):
-            n = g * INNER
-            src, at = n // plan.rows_here, n % plan.rows_here
-            value = heat[n : n + INNER, :]
-            kap = kappa[src, at : at + INNER, :]
-            mixed = jnp.where((lane >= 4) & (lane < 64), pltpu.roll(kap, 4, 1), value)
-            mixed = jnp.where((lane >= 64) & (lane < width - 4), pltpu.roll(kap, width - 4, 1), mixed)
-            turned = mixed.T
-            edge_left[:, n : n + INNER] = turned[0:8, :]
-            edge_right[:, n : n + INNER] = turned[width - 8 : width, :]
+            plan.edges(heat[g * INNER : (g + 1) * INNER, :], edge_left, edge_right, g * INNER)
 
     edge = jax.ShapeDtypeStruct((8, plan.rows), F32)
     outs = [jax.ShapeDtypeStruct((plan.rows, width), F32), edge, edge]
     scratch = plan.work_a() + [pltpu.VMEM((plan.rows, 2 * width), BF16)]
-    return call(body, outs, scratch, "rows_heat", (0, 1, 2), ())(dft, table, received, alpha, kappa)
-
-
-def rows_turn(plan, read_field, sets, wide, dft, table, screen, field):
-    def body(dft, table, screen, field, *refs):
-        outs, work = refs[:sets], refs[sets:]
-
+    return call(body, outs, scratch, (0, 1, 2), ())(dft, table, received, alpha)
+
+
+def rows_turn(plan, read_field, wide, dft, table, screen, field):
+    def body(dft, table, screen, field, out, *work):
         def read(a, off):
             return screened(read_field(field, a, off), screen[pl.ds(a * INNER + off, CHUNK), :])
 
-        along_rows(read, [functools.partial(plan.send_a, out) for out in outs], dft, table, *work)
+        along_rows(read, functools.partial(plan.send_a, out), dft, table, *work)
         if wide:
-            plan.send_edges(outs[0])
-
-    outs = [plan.sent_wide if wide and n == 0 else plan.sent for n in range(sets)]
-    return call(body, outs, plan.work_a(), "rows_turn", (0, 1, 2), range(sets))(dft, table, screen, field)
-
-
-def rows_smooth(plan, keep, heat, kappa, from_left, from_right, me):
+            plan.send_edges(out)
+
+    out = plan.sent_wide if wide else plan.sent
+    return call(body, [out], plan.work_a(), (0, 1, 2), (0,))(dft, table, screen, field)[0]
+
+
+def rows_smooth(plan, heat, from_left, from_right, kappa, kappa_left, kappa_right, me):
     width = plan.width
     PAD = 8
     step_rows = 32
 
-    def body(heat, kappa, from_left, from_right, me, screen, *refs):
-        home_parts, h0, h1, kx = (refs[0] if keep else None, *refs[-3:])
+    def body(heat, from_left, from_right, kappa, kappa_left, kappa_right, me, screen, h0, h1, kx):
         place = me[1] * plan.wind + plan.local(me[0], me[1])
         zeros = jnp.zeros((PAD, 2 * width), F32)
         for ref in (h0, h1, kx):
             ref[0:PAD, :] = zeros
             ref[plan.rows + PAD : plan.rows + 2 * PAD, :] = zeros
-        lane = lax.broadcasted_iota(jnp.int32, (INNER, width), 1)
         for g in range(plan.rows // INNER):
-            n = g * INNER
-            src, at = n // plan.rows_here, n % plan.rows_here
-            spot = slice(PAD + n, PAD + n + INNER)
-            h0[spot, 0:width] = heat[n : n + INNER, :]
-            kx[spot, 0:width] = kappa[src, at : at + INNER, :]
-            turned = jnp.concatenate(
-                [from_right[:, n : n + INNER], jnp.zeros((width - 16, INNER), F32), from_left[:, n : n + INNER]], axis=0
-            ).T
-            h0[spot, width : 2 * width] = jnp.where((lane < 4) | (lane >= width - 4), turned, 0.0)
-            kap = jnp.where(lane < 4, pltpu.roll(turned, width - 4, 1), 0.0)
-            kx[spot, width : 2 * width] = jnp.where(lane >= width - 4, pltpu.roll(turned, 4, 1), kap)
+            n = slice(g * INNER, (g + 1) * INNER)
+            spot = slice(PAD + g * INNER, PAD + (g + 1) * INNER)
+            for ref, value, left, right in ((h0, heat, from_left, from_right), (kx, kappa, kappa_left, kappa_right)):
+                ref[spot, 0:width] = value[n, :]
+                beside = [right[:, n], jnp.zeros((width - 16, INNER), F32), left[:, n]]
+                ref[spot, width : 2 * width] = jnp.concatenate(beside, axis=0).T
         wide = lax.broadcasted_iota(jnp.int32, (step_rows, 2 * width), 1)
         bad = (wide >= width) & (wide < width + width // 2) & (place == plan.devices - 1)
         bad = bad | ((wide >= width + width // 2) & (place == 0))
@@ -676,10 +716,6 @@
 
         def into_screen(base, value):
             screen[pl.ds(base, step_rows), :] = -value[:, :width]
-            if keep:
-                block = lax.rem(base // plan.rows_here + plan.wind - me[0], plan.wind)
-                at = pl.multiple_of(lax.rem(base, plan.rows_here), step_rows)
-                home_parts[block, pl.ds(at, step_rows), :] = -value[:, :width]
 
         refs = [h0, h1]
         for n in range(SMOOTH):
@@ -687,9 +723,7 @@
 
     tall = pltpu.VMEM((plan.rows + 2 * PAD, 2 * width), F32)
     outs = [jax.ShapeDtypeStruct((plan.rows, width), F32)]
-    if keep:
-        outs.append(jax.ShapeDtypeStruct((plan.wind, plan.rows_here, width), F32))
-    return call(body, outs, [tall] * 3, "rows_smooth", (), (0,))(heat, kappa, from_left, from_right, me)
+    return call(body, outs, [tall] * 3, (), (0,))(heat, from_left, from_right, kappa, kappa_left, kappa_right, me)[0]
 
 
 def next_prev(value_up, value_down, axes, order):
@@ -855,7 +889,7 @@
     for layer_no in range(LAYERS):
         absorption = layer_absorption(index_full[layer_no], absorb_table[layer_no], level_ids)
         screen_phase = jnp.zeros((slab_rows, slab_pair.shape[2]), jnp.float32)
-        for round_no in range(ITERS):
+        for _ in range(ITERS):
             middle = propagate_slab(apply_phase(slab_pair, screen_phase), 0.5)
             intensity = middle[0] * middle[0] + middle[1] * middle[1]
             deposit = absorption[None, :] * intensity * (1.0 / rows_total)
@@ -863,7 +897,7 @@
             totals = partial_heat[-1]
             upstream = carried_in(totals, ("wind", "cross"), add_terms, jnp.zeros_like(totals))
             heat_field = partial_heat + upstream[None, :]
-            for smooth_no in range(SMOOTH):
+            for _ in range(SMOOTH):
                 padded = extended(heat_field, ((("wind", "cross"), 0),), 1)
                 padded = jnp.pad(padded, ((0, 0), (1, 1)))
                 heat_field = conduct_core(padded, kappa_pad)
@@ -884,7 +918,11 @@
     fits = plan.width == INNER and INNER % plan.height == 0 and plan.height % CHUNK == 0
     if not fits or plan.rows_here % INNER or plan.rows % (2 * INNER):
         return wide_device(field_real, field_imag, absorb_index, absorb_table, zone_map, zone_conductivity)
-    wind, cross = plan.wind, plan.cross
+    return tiled_device(plan, field_real, field_imag, absorb_index, absorb_table, zone_map, zone_conductivity)
+
+
+def tiled_device(plan, field_real, field_imag, absorb_index, absorb_table, zone_map, zone_conductivity):
+    cross = plan.cross
     w, c = lax.axis_index("wind"), lax.axis_index("cross")
     place = jnp.stack([w, c]).astype(jnp.int32)
     grid_axes = ("wind", "cross")
@@ -896,50 +934,50 @@
     def flip(x):
         return exchange(x, grid_axes)
 
-    alpha = jnp.zeros(absorb_index.shape, F32)
-    for level in range(absorb_table.shape[1]):
-        alpha = jnp.where(absorb_index == level, absorb_table[:, level : level + 1], alpha)
-    alpha = alpha * (1.0 / plan.rows)
-    alpha_a = lax.dynamic_slice_in_dim(alpha, plan.local(w, c) * plan.width, plan.width, axis=1)
-    alpha = jnp.pad(alpha, ((0, 8 - LAYERS), (0, 0)))
-    to_a, *blocks = prepare(plan, field_real, field_imag, zone_map, alpha, zone_conductivity, place)
-    home_a = exchange(to_a, "wind")
-    home_b, kappa_b, alpha_b = home_rows(plan, shifted(blocks[:cross], "cross"), place)
+    to_b, *field_blocks = prepare_field(plan, field_real, field_imag, place)
+    home_b = exchange(to_b, "cross")
+    field_blocks = shifted(field_blocks, "wind")
+    *blocks, alpha_a = prepare(plan, zone_map, absorb_index, absorb_table, zone_conductivity, place)
 
     dft = jnp.asarray(dft_matrices())
-    tab_a = lambda *shares: jnp.asarray(row_table(plan.rows, shares))
+    tab_a = lambda share: (jnp.asarray(row_blocks(plan.rows, share)), jnp.asarray(row_table(plan.rows)))
     tab_b = lambda *shares: jnp.asarray(chirp_columns(plan.cols, shares))
 
-    def smooth_a(layer, share, keep, received):
-        heat, left, right = rows_heat(plan, dft, tab_a(share), received, alpha_a[layer : layer + 1], kappa_a)
+    def smooth_a(layer, share, received):
+        heat, left, right = rows_heat(plan, *tab_a(share), received, alpha_a[layer : layer + 1])
         from_left, from_right = next_prev(right, left, grid_axes, columns_order)
-        return rows_smooth(plan, keep, heat, kappa_a, from_left, from_right, place)
-
-    home_a, home_b = lax.optimization_barrier((home_a, home_b))
-    sent = rows_send(plan, plan.home_a, dft, tab_a(0.5), home_a)
-    received, kappa_blocks = lax.optimization_barrier((flip(sent), blocks[cross:]))
-    kappa_blocks = shifted(kappa_blocks, "wind")
+        return rows_smooth(plan, heat, from_left, from_right, *kappas, place)
+
+    def smooth_b(layer, keep, received):
+        part, beside, totals = cols_heat(plan, layer, plan.devices, dft, tab_b(0.5), received, alpha_b)
+        return cols_smooth(plan, keep, kappa_b, above, below, part, beside, flip(totals), place)
+
+    home_b, across = lax.optimization_barrier((home_b, blocks[:cross]))
+    sent = cols_send(plan, plan.home_b, False, dft, tab_b(0.5), home_b)
+    kappa_b, alpha_b = home_rows(plan, shifted(across, "cross"), place)
     above, below = next_prev(kappa_b[-8:], kappa_b[:8], grid_axes, list(range(plan.devices)))
-    part, beside, totals = cols_heat(plan, 0, plan.devices, dft, tab_b(0.5), received, alpha_b)
-    screen = cols_smooth(plan, kappa_b, above, below, part, beside, flip(totals), place)
-    sent = cols_turn(plan, plan.home_b, dft, tab_b(0.5), screen, home_b)
-    sent, kappa_blocks = lax.optimization_barrier((sent, kappa_blocks))
-    kappa_a = in_order(kappa_blocks, place, 0, "kappa_a")
-    (screen,) = smooth_a(0, 0.5, False, flip(sent))
-    sent_middle, sent_field = rows_turn(plan, plan.home_a, 2, True, dft, tab_a(1.5, 1.0), screen, home_a)
+    received, along = lax.optimization_barrier((flip(sent), blocks[cross:]))
+    along = shifted(along, "wind")
+    kappa_a, left, right = rows_kappa(plan, along, place)
+    kappas = (kappa_a, *next_prev(right, left, grid_axes, columns_order))
+    home_a = in_order(field_blocks, place, 0)
+    screen = smooth_a(0, 0.5, received)
+    sent = rows_turn(plan, plan.home_a, True, *tab_a(0.5), screen, home_a)
+    received, above, below = lax.optimization_barrier((flip(sent), above, below))
+    (screen,) = smooth_b(0, False, received)
+    sent_middle, sent_field = cols_turn(plan, plan.home_b, 2, dft, tab_b(1.5, 1.0), screen, home_b)
     middle = flip(sent_middle)
-    field_b = cols_send(plan, plan.flip_b, False, dft, tab_b(1.0), flip(sent_field))
-    field_a = flip(field_b)
-    part, beside, totals = cols_heat(plan, 1, 1, dft, tab_b(1.5), middle, alpha_b)
-    across = shifted([totals[0]] * cross, "cross")
-    along = shifted([sum(across[1:], across[0])] * wind, "wind")
-    screen = cols_smooth(plan, kappa_b, above, below, part, beside, *across[1:], *along[1:], place)
-    sent = cols_turn(plan, plan.flip_b, dft, tab_b(0.5), screen, field_b)
-    screen, home_parts = smooth_a(1, 0.5, True, flip(sent))
-    (sent,) = rows_turn(plan, plan.flip_a, 1, False, dft, tab_a(1.0), screen, field_a)
-    received, home_parts = lax.optimization_barrier((flip(sent), home_parts))
-    back = cols_send(plan, plan.flip_b, True, dft, tab_b(1.0), received)
-    screen = home_screen(plan, shifted([home_parts[t] for t in range(wind)], "wind"), place)
+    field = flip(sent_field)
+    screen = smooth_a(1, 1.5, middle)
+    field, screen = lax.optimization_barrier((field, screen))
+    field = rows_field(plan, plan.flip_a, *tab_a(1.0), field)
+    sent = rows_turn(plan, plan.flip_a, True, *tab_a(0.5), screen, field)
+    screen, *home_parts = smooth_b(1, True, flip(sent))
+    screen, home_parts = lax.optimization_barrier((flip(screen), home_parts))
+    screen = screen.reshape(plan.rows, plan.width)
+    sent = rows_turn(plan, plan.flip_a, False, *tab_a(1.0), screen, field)
+    back = cols_send(plan, plan.flip_b, True, dft, tab_b(1.0), flip(sent))
+    screen = home_screen(plan, shifted(home_parts, "cross"), place)
     back = exchange(back, "cross")
     out_real = back[:, : plan.height].reshape(field_real.shape)
     out_imag = back[:, plan.height :].reshape(field_real.shape)
@@ -960,6 +998,4 @@
         P(("beams", "wind"), "cross"),
         P(("beams", "wind"), "cross"),
     )
-    return jax.shard_map(
-        on_device, mesh=mesh, in_specs=in_specs, out_specs=out_specs, check_vma=False
-    )
+    return jax.shard_map(on_device, mesh=mesh, in_specs=in_specs, out_specs=out_specs, check_vma=False)

time: 366 us -> 380 us (1.038)
  blocking collectives: 124 us -> 162 us
  waiting for transfers between devices: 89.7 us -> 78.3 us
  Pallas kernels: 73.4 us -> 62.6 us
  starting transfers between devices: 62.4 us -> 55.7 us
  local copies, waits for them, and re-layouts: 10.4 us -> 16.2 us
    all_to_all x4 -> x7, blocking collectives: 124 us -> 162 us  [exchange(): return lax.all_to_all(x, axes, split_axis=0, concat_axis=0, tiled=True)]
    all_to_all x6 -> x4, waiting for transfers between devices: 37.5 us -> 8.19 us  [exchange(): return lax.all_to_all(x, axes, split_axis=0, concat_axis=0, tiled=True)]
    ppermute x15 -> x12, waiting for transfers between devices: 28.3 us -> 49.1 us  [shifted(): lax.ppermute(parts[s], axis, [(i, (i + s) % size) for i in range(size)])]
    all_to_all x6 -> x4, starting transfers between devices: 29 us -> 16.4 us  [exchange(): return lax.all_to_all(x, axes, split_axis=0, concat_axis=0, tiled=True)]
    pallas_call x19 -> x21, Pallas kernels: 73.4 us -> 62.6 us  [run(): pl.pallas_call(body, out_shape=[pltpu.VMEM(o.shape, o.dtype) if i in near...]
    ppermute x3 -> x4, starting transfers between devices: 7.37 us -> 17.9 us  [next_prev(): lax.ppermute(value_up, axes, up)]
    unnamed x58 -> x96, local copies, waits for them, and re-layouts: 7.99 us -> 15.2 us
    ppermute x3 -> x4, waiting for transfers between devices: 22 us -> 17.7 us  [next_prev(): lax.ppermute(value_up, axes, up)]
  transfers between devices with their start and end apart: 27 -> 24, of which waited for: 14 -> 12; matrix products, arithmetic and copies ran while one was open for 0% -> 0% of each run, Pallas kernels for 8% -> 4%
where the time goes in v3:
time: 380 us; the launch traced here: 376 us
  blocking collectives  162 us (43%)
  waiting for transfers between devices  78.3 us (21%)
  Pallas kernels  62.6 us (16%)
  starting transfers between devices  55.7 us (15%)
  local copies, waits for them, and re-layouts  16.2 us (4%)
    all_to_all x7, blocking collectives, exchange(): return lax.all_to_all(x, axes, split_axis=0, concat_axis=0, tiled=True)  162 us
    pallas_call x21, Pallas kernels, run(): pl.pallas_call(body, out_shape=[pltpu.VMEM(o.shape, o.dtype) if i in near...  62.6 us
    ppermute x12, waiting for transfers between devices, shifted(): lax.ppermute(parts[s], axis, [(i, (i + s) % size) for i in range(size)])  49.1 us
    ppermute x4, starting transfers between devices, next_prev(): lax.ppermute(value_up, axes, up)  17.9 us
    ppermute x4, waiting for transfers between devices, next_prev(): lax.ppermute(value_up, axes, up)  17.7 us
    all_to_all x4, starting transfers between devices, exchange(): return lax.all_to_all(x, axes, split_axis=0, concat_axis=0, tiled=True)  16.4 us
    unnamed x96, local copies, waits for them, and re-layouts  15.2 us
    ppermute x12, starting transfers between devices, shifted(): lax.ppermute(parts[s], axis, [(i, (i + s) % size) for i in range(size)])  13 us
  transfers between devices with their start and end apart: 24, of which 12 were waited for; matrix products, arithmetic and copies ran while one was open for 0% of the time, Pallas kernels for 4%

profile of v3, /device:TPU:16, one launch (start us, length us, event | category | flops | bytes accessed | tf_op | source)
XLA Modules:
  0.0 376.2 jit_solution(11046364502860090402)
XLA Ops:
  14.4 8.2 %all-to-all-done.field = f32[4,128,512]{2,1,0:T(8,128)S(1)} async-done(((f32[4,128,512]{2,1,0:T(8,128)}), f32[4,128,512]{2,1,0:T(8,128)S(1)}, u32[]{:S(2)}, u32[]{:S(2)}) %all-to-all-start) | async-done | bytes 1048608 | tf_op jit(solution)/shard_map/all_to_all | solution.py:932
  26.8 30.2 %all_to_all.55.received = f32[16,128,128]{2,1,0:T(8,128)S(1)} all-to-all(f32[16,128,128]{2,1,0:T(8,128)S(1)} %shard_map.250), channel_id=1, replica_groups=mesh['beams'=2,'wind'=4,'cross'=4] {'wind','cross'}, dimensions={0} | all-to-all | bytes 2097152 | tf_op jit(solution)/shard_map/all_to_all | solution.py:932
  67.3 22.5 %collective-permute-done.6.refs_2_ = f32[256,128]{1,0:T(8,128)S(1)} collective-permute-done((f32[256,128]{1,0:T(8,128)S(1)}, f32[256,128]{1,0:T(8,128)S(1)}, u32[]{:S(2)}, u32[]{:S(2)}) %collective-permute-start.6) | collective-permute-done | bytes 131104 | tf_op jit(solution)/shard_map/ppermute | solution.py:422
  89.8 6.3 %collective-permute-start.3 = (f32[8,1024]{1,0:T(8,128)S(1)}, f32[8,1024]{1,0:T(8,128)S(1)}, u32[]{:S(2)}, u32[]{:S(2)}) collective-permute-start(f32[8,1024]{1,0:T(8,128)S(1)} %get-tuple-element.79), channel_id=1, source_target_pairs={{0,4},{4,8},{8,12},{12,13},{13,9},{9,5},{5,1},{1,2},{2,6},{6,10},{... | collective-permute-start | bytes 98312 | tf_op jit(solution)/shard_map/ppermute | solution.py:732
  108.6 4.3 %shard_map.253.screen = f32[1024,128]{1,0:T(8,128)S(1)} custom-call(f32[1024,128]{1,0:T(8,128)S(1)} %get-tuple-element.78.heat, f32[8,1024]{1,0:T(8,128)S(1)} %collective-permute-done.3.from_left, f32[8,1024]{1,0:T(8,128)S(1)} %collective-permute-done.4.from_right, f32[1024,128]{1,0:T(8,128)S(1)} %get-tuple-element.85.kappa, ...), custom_call_target="tpu_custom_call" | custom-call | tf_op jit(solution)/shard_map/pallas_call | solution.py:338
  116.9 4.5 %all-to-all-start.2 = ((f32[16,136,128]{2,1,0:T(8,128)}), f32[16,136,128]{2,1,0:T(8,128)}, u32[]{:S(2)}, u32[]{:S(2)}) async-start(f32[16,136,128]{2,1,0:T(8,128)} %copy-done.6), calls=%async_computation.2 | async-start | bytes 2228224 | tf_op jit(solution)/shard_map/all_to_all | solution.py:932
  124.4 8.2 %collective-permute-done.refs_1_ = f32[72,512]{1,0:T(8,128)S(1)} collective-permute-done((f32[72,512]{1,0:T(8,128)S(1)}, f32[72,512]{1,0:T(8,128)S(1)}, u32[]{:S(2)}, u32[]{:S(2)}) %collective-permute-start) | collective-permute-done | bytes 147488 | tf_op jit(solution)/shard_map/ppermute | solution.py:422
  137.7 4.4 %collective-permute-start.13 = (f32[8,2048]{1,0:T(8,128)S(1)}, f32[8,2048]{1,0:T(8,128)S(1)}, u32[]{:S(2)}, u32[]{:S(2)}) collective-permute-start(f32[8,2048]{1,0:T(8,128)S(1)} %get-tuple-element.122), channel_id=1, source_target_pairs={{0,1},{1,2},{2,3},{3,4},{4,5},{5,6},{6,7},{7,8},{8,9},{9,10},{10,1... | collective-permute-start | bytes 196616 | tf_op jit(solution)/shard_map/ppermute | solution.py:732
  144.1 4.6 %collective-permute-done.13.above = f32[8,2048]{1,0:T(8,128)S(1)} collective-permute-done((f32[8,2048]{1,0:T(8,128)S(1)}, f32[8,2048]{1,0:T(8,128)S(1)}, u32[]{:S(2)}, u32[]{:S(2)}) %collective-permute-start.13) | collective-permute-done | bytes 65568 | tf_op jit(solution)/shard_map/ppermute | solution.py:732
  148.8 5.3 %shard_map.256 = (f32[64,2048]{1,0:T(8,128)S(1)}, f32[8,2048]{1,0:T(8,128)S(1)}, f32[16,16,128]{2,1,0:T(8,128)S(1)}) custom-call(bf16[4,256,256]{2,1,0:T(8,128)(2,1)S(1)} %copy-done.1, f32[64,128]{1,0:T(8,128)S(1)} %copy-done.16, f32[16,136,128]{2,1,0:T(8,128)} %all-to-all-done.2.received, f32[8,2048]{1,0:T(8,128)S(1)} %get-tuple-element.95.absorption), custom_call_target="tpu_custom_call" | custom-call | tf_op jit(solution)/shard_map/pallas_call | solution.py:338
  154.1 11.0 %all_to_all.56.refs_0_ = f32[16,16,128]{2,1,0:T(8,128)S(1)} all-to-all(f32[16,16,128]{2,1,0:T(8,128)S(1)} %get-tuple-element.98), channel_id=1, replica_groups=mesh['beams'=2,'wind'=4,'cross'=4] {'wind','cross'}, dimensions={0} | all-to-all | bytes 262144 | tf_op jit(solution)/shard_map/all_to_all | solution.py:932
  168.5 5.2 %shard_map.258 = (f32[16,128,128]{2,1,0:T(8,128)S(1)}, f32[16,128,128]{2,1,0:T(8,128)S(1)}) custom-call(bf16[4,256,256]{2,1,0:T(8,128)(2,1)S(1)} %copy-done.1, f32[96,128]{1,0:T(8,128)S(1)} %copy-done.19, f32[64,2048]{1,0:T(8,128)S(1)} %shard_map.257.screen, f32[4,128,512]{2,1,0:T(8,128)S(1)} %copy-done.3), custom_call_target="tpu_custom_call" | custom-call | tf_op jit(solution)/shard_map/pallas_call | solution.py:338
  173.7 30.8 %all_to_all.57.received = f32[16,128,128]{2,1,0:T(8,128)} all-to-all(f32[16,128,128]{2,1,0:T(8,128)S(1)} %get-tuple-element.100), channel_id=1, replica_groups=mesh['beams'=2,'wind'=4,'cross'=4] {'wind','cross'}, dimensions={0} | all-to-all | bytes 2097152 | tf_op jit(solution)/shard_map/all_to_all | solution.py:932
  204.5 4.6 %all-to-all-start.4 = ((f32[16,128,128]{2,1,0:T(8,128)}), f32[16,128,128]{2,1,0:T(8,128)}, u32[]{:S(2)}, u32[]{:S(2)}) async-start(f32[16,128,128]{2,1,0:T(8,128)} %copy-done.14), calls=%async_computation.4 | async-start | bytes 2097152 | tf_op jit(solution)/shard_map/all_to_all | solution.py:932
  220.9 13.1 %collective-permute-done.15.from_left = f32[8,1024]{1,0:T(8,128)S(1)} collective-permute-done((f32[8,1024]{1,0:T(8,128)S(1)}, f32[8,1024]{1,0:T(8,128)S(1)}, u32[]{:S(2)}, u32[]{:S(2)}) %collective-permute-start.15) | collective-permute-done | bytes 32800 | tf_op jit(solution)/shard_map/ppermute | solution.py:732
  234.0 4.3 %shard_map.260.screen = f32[1024,128]{1,0:T(8,128)S(1)} custom-call(f32[1024,128]{1,0:T(8,128)S(1)} %get-tuple-element.101.heat, f32[8,1024]{1,0:T(8,128)S(1)} %collective-permute-done.15.from_left, f32[8,1024]{1,0:T(8,128)S(1)} %collective-permute-done.16.from_right, f32[1024,128]{1,0:T(8,128)S(1)} %copy-done.13, ...), custom_call_target="tpu_custom_call" | custom-call | tf_op jit(solution)/shard_map/pallas_call | solution.py:338
  240.7 4.0 %shard_map.261.field = f32[16,128,128]{2,1,0:T(8,128)S(1)} custom-call(bf16[8,2,256,256]{3,2,1,0:T(8,128)(2,1)S(1)} %copy-done.4, f32[128,128]{1,0:T(8,128)S(1)} %copy-done.8, f32[16,128,128]{2,1,0:T(8,128)} %all-to-all-done.4.field), custom_call_target="tpu_custom_call" | custom-call | tf_op jit(solution)/shard_map/pallas_call | solution.py:338
  247.6 31.4 %all_to_all.58.received = f32[16,136,128]{2,1,0:T(8,128)S(1)} all-to-all(f32[16,136,128]{2,1,0:T(8,128)S(1)} %shard_map.262), channel_id=1, replica_groups=mesh['beams'=2,'wind'=4,'cross'=4] {'wind','cross'}, dimensions={0} | all-to-all | bytes 2228224 | tf_op jit(solution)/shard_map/all_to_all | solution.py:932
  279.0 4.1 %shard_map.263 = (f32[64,2048]{1,0:T(8,128)S(1)}, f32[8,2048]{1,0:T(8,128)S(1)}, f32[16,16,128]{2,1,0:T(8,128)S(1)}) custom-call(bf16[4,256,256]{2,1,0:T(8,128)(2,1)S(1)} %copy-done.1, f32[64,128]{1,0:T(8,128)S(1)} %copy-done.16, f32[16,136,128]{2,1,0:T(8,128)S(1)} %all_to_all.58.received, f32[8,2048]{1,0:T(8,128)S(1)} %get-tuple-element.95.absorption), custom_call_target="tpu_custom_call" | custom-call | tf_op jit(solution)/shard_map/pallas_call | solution.py:338
  283.1 10.3 %all_to_all.59.refs_0_ = f32[16,16,128]{2,1,0:T(8,128)S(1)} all-to-all(f32[16,16,128]{2,1,0:T(8,128)S(1)} %get-tuple-element.108), channel_id=1, replica_groups=mesh['beams'=2,'wind'=4,'cross'=4] {'wind','cross'}, dimensions={0} | all-to-all | bytes 262144 | tf_op jit(solution)/shard_map/all_to_all | solution.py:932
  296.8 18.8 %all_to_all.60 = f32[16,64,128]{2,1,0:T(8,128)S(1)} all-to-all(f32[16,64,128]{2,1,0:T(8,128)S(1)} %get-tuple-element.109), channel_id=1, replica_groups=mesh['beams'=2,'wind'=4,'cross'=4] {'wind','cross'}, dimensions={0} | all-to-all | bytes 1048576 | tf_op jit(solution)/shard_map/all_to_all | solution.py:932
  318.6 29.4 %all_to_all.61.field = f32[16,128,128]{2,1,0:T(8,128)S(1)} all-to-all(f32[16,128,128]{2,1,0:T(8,128)S(1)} %shard_map.265), channel_id=1, replica_groups=mesh['beams'=2,'wind'=4,'cross'=4] {'wind','cross'}, dimensions={0} | all-to-all | bytes 2097152 | tf_op jit(solution)/shard_map/all_to_all | solution.py:932
  348.1 4.1 %shard_map.266 = f32[4,128,512]{2,1,0:T(8,128)} custom-call(bf16[4,256,256]{2,1,0:T(8,128)(2,1)S(1)} %copy-done.1, f32[64,128]{1,0:T(8,128)S(1)} %copy-done.20, f32[16,128,128]{2,1,0:T(8,128)S(1)} %all_to_all.61.field), custom_call_target="tpu_custom_call" | custom-call | tf_op jit(solution)/shard_map/pallas_call | solution.py:338
  359.3 13.2 %collective-permute-done.17.refs_1_ = f32[64,512]{1,0:T(8,128)S(1)} collective-permute-done((f32[64,512]{1,0:T(8,128)S(1)}, f32[64,512]{1,0:T(8,128)S(1)}, u32[]{:S(2)}, u32[]{:S(2)}) %collective-permute-start.17) | collective-permute-done | bytes 131104 | tf_op jit(solution)/shard_map/ppermute | solution.py:422
  (152 shorter events, 92.2 us)
Async XLA Ops:
  4.5 18.1 %all-to-all-start = ((f32[4,128,512]{2,1,0:T(8,128)}), f32[4,128,512]{2,1,0:T(8,128)S(1)}, u32[]{:S(2)}, u32[]{:S(2)}) async-start(f32[4,128,512]{2,1,0:T(8,128)} %copy-done.15), calls=%async_computation | async-start | bytes 2097152 | tf_op jit(solution)/shard_map/all_to_all | solution.py:932
  57.1 6.4 %collective-permute-start.5 = (f32[256,128]{1,0:T(8,128)S(1)}, f32[256,128]{1,0:T(8,128)S(1)}, u32[]{:S(2)}, u32[]{:S(2)}) collective-permute-start(f32[256,128]{1,0:T(8,128)S(1)} %copy-done.47), channel_id=1, source_target_pairs={{0,4},{4,8},{8,12},{12,0},{1,5},{5,9},{9,13},{13,1},{2,6},{6,10},{... | collective-permute-start | bytes 393224 | tf_op jit(solution)/shard_map/ppermute | solution.py:422
  57.1 41.8 %collective-permute-start.10 = (f32[512,128]{1,0:T(8,128)S(1)}, f32[512,128]{1,0:T(8,128)S(1)}, u32[]{:S(2)}, u32[]{:S(2)}) collective-permute-start(f32[512,128]{1,0:T(8,128)S(1)} %copy-done.29), channel_id=1, source_target_pairs={{0,4},{4,8},{8,12},{12,0},{1,5},{5,9},{9,13},{13,1},{2,6},{6,10},{... | collective-permute-start | bytes 786440 | tf_op jit(solution)/shard_map/ppermute | solution.py:422
  58.2 44.6 %collective-permute-start.11 = (f32[512,128]{1,0:T(8,128)S(1)}, f32[512,128]{1,0:T(8,128)S(1)}, u32[]{:S(2)}, u32[]{:S(2)}) collective-permute-start(f32[512,128]{1,0:T(8,128)S(1)} %copy-done.27), channel_id=1, source_target_pairs={{0,8},{4,12},{8,0},{12,4},{1,9},{5,13},{9,1},{13,5},{2,10},{6,14},... | collective-permute-start | bytes 786440 | tf_op jit(solution)/shard_map/ppermute | solution.py:422
  60.6 44.2 %collective-permute-start.12 = (f32[512,128]{1,0:T(8,128)S(1)}, f32[512,128]{1,0:T(8,128)S(1)}, u32[]{:S(2)}, u32[]{:S(2)}) collective-permute-start(f32[512,128]{1,0:T(8,128)S(1)} %copy-done.25), channel_id=1, source_target_pairs={{0,12},{4,0},{8,4},{12,8},{1,13},{5,1},{9,5},{13,9},{2,14},{6,2},{... | collective-permute-start | bytes 786440 | tf_op jit(solution)/shard_map/ppermute | solution.py:422
  61.6 28.2 %collective-permute-start.6 = (f32[256,128]{1,0:T(8,128)S(1)}, f32[256,128]{1,0:T(8,128)S(1)}, u32[]{:S(2)}, u32[]{:S(2)}) collective-permute-start(f32[256,128]{1,0:T(8,128)S(1)} %copy-done.39), channel_id=1, source_target_pairs={{0,8},{4,12},{8,0},{12,4},{1,9},{5,13},{9,1},{13,5},{2,10},{6,14},... | collective-permute-start | bytes 393224 | tf_op jit(solution)/shard_map/ppermute | solution.py:422
  63.4 32.7 %collective-permute-start.7 = (f32[256,128]{1,0:T(8,128)S(1)}, f32[256,128]{1,0:T(8,128)S(1)}, u32[]{:S(2)}, u32[]{:S(2)}) collective-permute-start(f32[256,128]{1,0:T(8,128)S(1)} %copy-done.37), channel_id=1, source_target_pairs={{0,12},{4,0},{8,4},{12,8},{1,13},{5,1},{9,5},{13,9},{2,14},{6,2},{... | collective-permute-start | bytes 393224 | tf_op jit(solution)/shard_map/ppermute | solution.py:422
  89.8 15.6 %collective-permute-start.3 = (f32[8,1024]{1,0:T(8,128)S(1)}, f32[8,1024]{1,0:T(8,128)S(1)}, u32[]{:S(2)}, u32[]{:S(2)}) collective-permute-start(f32[8,1024]{1,0:T(8,128)S(1)} %get-tuple-element.79), channel_id=1, source_target_pairs={{0,4},{4,8},{8,12},{12,13},{13,9},{9,5},{5,1},{1,2},{2,6},{6,10},{... | collective-permute-start | bytes 98312 | tf_op jit(solution)/shard_map/ppermute | solution.py:732
  96.1 9.3 %collective-permute-start.4 = (f32[8,1024]{1,0:T(8,128)S(1)}, f32[8,1024]{1,0:T(8,128)S(1)}, u32[]{:S(2)}, u32[]{:S(2)}) collective-permute-start(f32[8,1024]{1,0:T(8,128)S(1)} %get-tuple-element.80), channel_id=1, source_target_pairs={{4,0},{8,4},{12,8},{13,12},{9,13},{5,9},{1,5},{2,1},{6,2},{10,6},{... | collective-permute-start | bytes 98312 | tf_op jit(solution)/shard_map/ppermute | solution.py:732
  98.9 6.5 %collective-permute-start.8 = (f32[8,1024]{1,0:T(8,128)S(1)}, f32[8,1024]{1,0:T(8,128)S(1)}, u32[]{:S(2)}, u32[]{:S(2)}) collective-permute-start(f32[8,1024]{1,0:T(8,128)S(1)} %get-tuple-element.86), channel_id=1, source_target_pairs={{0,4},{4,8},{8,12},{12,13},{13,9},{9,5},{5,1},{1,2},{2,6},{6,10},{... | collective-permute-start | bytes 98312 | tf_op jit(solution)/shard_map/ppermute | solution.py:732
  102.8 5.8 %collective-permute-start.9 = (f32[8,1024]{1,0:T(8,128)S(1)}, f32[8,1024]{1,0:T(8,128)S(1)}, u32[]{:S(2)}, u32[]{:S(2)}) collective-permute-start(f32[8,1024]{1,0:T(8,128)S(1)} %get-tuple-element.87), channel_id=1, source_target_pairs={{4,0},{8,4},{12,8},{13,12},{9,13},{5,9},{1,5},{2,1},{6,2},{10,6},{... | collective-permute-start | bytes 98312 | tf_op jit(solution)/shard_map/ppermute | solution.py:732
  116.9 31.9 %all-to-all-start.2 = ((f32[16,136,128]{2,1,0:T(8,128)}), f32[16,136,128]{2,1,0:T(8,128)}, u32[]{:S(2)}, u32[]{:S(2)}) async-start(f32[16,136,128]{2,1,0:T(8,128)} %copy-done.6), calls=%async_computation.2 | async-start | bytes 2228224 | tf_op jit(solution)/shard_map/all_to_all | solution.py:932
  121.4 11.2 %collective-permute-start = (f32[72,512]{1,0:T(8,128)S(1)}, f32[72,512]{1,0:T(8,128)S(1)}, u32[]{:S(2)}, u32[]{:S(2)}) collective-permute-start(f32[72,512]{1,0:T(8,128)S(1)} %copy-done.35), channel_id=1, source_target_pairs={{0,1},{1,2},{2,3},{3,0},{4,5},{5,6},{6,7},{7,4},{8,9},{9,10},{10,1... | collective-permute-start | bytes 442376 | tf_op jit(solution)/shard_map/ppermute | solution.py:422
  121.6 12.2 %collective-permute-start.1 = (f32[72,512]{1,0:T(8,128)S(1)}, f32[72,512]{1,0:T(8,128)S(1)}, u32[]{:S(2)}, u32[]{:S(2)}) collective-permute-start(f32[72,512]{1,0:T(8,128)S(1)} %copy-done.33), channel_id=1, source_target_pairs={{0,2},{1,3},{2,0},{3,1},{4,6},{5,7},{6,4},{7,5},{8,10},{9,11},{10,... | collective-permute-start | bytes 442376 | tf_op jit(solution)/shard_map/ppermute | solution.py:422
  123.1 13.1 %collective-permute-start.2 = (f32[72,512]{1,0:T(8,128)S(1)}, f32[72,512]{1,0:T(8,128)S(1)}, u32[]{:S(2)}, u32[]{:S(2)}) collective-permute-start(f32[72,512]{1,0:T(8,128)S(1)} %copy-done.31), channel_id=1, source_target_pairs={{0,3},{1,0},{2,1},{3,2},{4,7},{5,4},{6,5},{7,6},{8,11},{9,8},{10,9... | collective-permute-start | bytes 442376 | tf_op jit(solution)/shard_map/ppermute | solution.py:422
  137.7 11.1 %collective-permute-start.13 = (f32[8,2048]{1,0:T(8,128)S(1)}, f32[8,2048]{1,0:T(8,128)S(1)}, u32[]{:S(2)}, u32[]{:S(2)}) collective-permute-start(f32[8,2048]{1,0:T(8,128)S(1)} %get-tuple-element.122), channel_id=1, source_target_pairs={{0,1},{1,2},{2,3},{3,4},{4,5},{5,6},{6,7},{7,8},{8,9},{9,10},{10,1... | collective-permute-start | bytes 196616 | tf_op jit(solution)/shard_map/ppermute | solution.py:732
  142.0 6.7 %collective-permute-start.14 = (f32[8,2048]{1,0:T(8,128)S(1)}, f32[8,2048]{1,0:T(8,128)S(1)}, u32[]{:S(2)}, u32[]{:S(2)}) collective-permute-start(f32[8,2048]{1,0:T(8,128)S(1)} %get-tuple-element.121), channel_id=1, source_target_pairs={{1,0},{2,1},{3,2},{4,3},{5,4},{6,5},{7,6},{8,7},{9,8},{10,9},{11,1... | collective-permute-start | bytes 196616 | tf_op jit(solution)/shard_map/ppermute | solution.py:732
  204.5 34.6 %all-to-all-start.4 = ((f32[16,128,128]{2,1,0:T(8,128)}), f32[16,128,128]{2,1,0:T(8,128)}, u32[]{:S(2)}, u32[]{:S(2)}) async-start(f32[16,128,128]{2,1,0:T(8,128)} %copy-done.14), calls=%async_computation.4 | async-start | bytes 2097152 | tf_op jit(solution)/shard_map/all_to_all | solution.py:932
  215.0 18.9 %collective-permute-start.15 = (f32[8,1024]{1,0:T(8,128)S(1)}, f32[8,1024]{1,0:T(8,128)S(1)}, u32[]{:S(2)}, u32[]{:S(2)}) collective-permute-start(f32[8,1024]{1,0:T(8,128)S(1)} %get-tuple-element.102), channel_id=1, source_target_pairs={{0,4},{4,8},{8,12},{12,13},{13,9},{9,5},{5,1},{1,2},{2,6},{6,10},{... | collective-permute-start | bytes 98312 | tf_op jit(solution)/shard_map/ppermute | solution.py:732
  218.4 15.5 %collective-permute-start.16 = (f32[8,1024]{1,0:T(8,128)S(1)}, f32[8,1024]{1,0:T(8,128)S(1)}, u32[]{:S(2)}, u32[]{:S(2)}) collective-permute-start(f32[8,1024]{1,0:T(8,128)S(1)} %get-tuple-element.103), channel_id=1, source_target_pairs={{4,0},{8,4},{12,8},{13,12},{9,13},{5,9},{1,5},{2,1},{6,2},{10,6},{... | collective-permute-start | bytes 98312 | tf_op jit(solution)/shard_map/ppermute | solution.py:732
  352.2 23.0 %all-to-all-start.10 = ((f32[4,128,512]{2,1,0:T(8,128)}), f32[4,128,512]{2,1,0:T(8,128)S(1)}, u32[]{:S(2)}, u32[]{:S(2)}) async-start(f32[4,128,512]{2,1,0:T(8,128)} %shard_map.266), calls=%async_computation.10 | async-start | bytes 2097152 | tf_op jit(solution)/shard_map/all_to_all | solution.py:932
  355.9 16.6 %collective-permute-start.17 = (f32[64,512]{1,0:T(8,128)S(1)}, f32[64,512]{1,0:T(8,128)S(1)}, u32[]{:S(2)}, u32[]{:S(2)}) collective-permute-start(f32[64,512]{1,0:T(8,128)S(1)} %copy-done.45), channel_id=1, source_target_pairs={{0,1},{1,2},{2,3},{3,0},{4,5},{5,6},{6,7},{7,4},{8,9},{9,10},{10,1... | collective-permute-start | bytes 393224 | tf_op jit(solution)/shard_map/ppermute | solution.py:422
  356.3 17.3 %collective-permute-start.18 = (f32[64,512]{1,0:T(8,128)S(1)}, f32[64,512]{1,0:T(8,128)S(1)}, u32[]{:S(2)}, u32[]{:S(2)}) collective-permute-start(f32[64,512]{1,0:T(8,128)S(1)} %copy-done.43), channel_id=1, source_target_pairs={{0,2},{1,3},{2,0},{3,1},{4,6},{5,7},{6,4},{7,5},{8,10},{9,11},{10,... | collective-permute-start | bytes 393224 | tf_op jit(solution)/shard_map/ppermute | solution.py:422
  358.0 15.8 %collective-permute-start.19 = (f32[64,512]{1,0:T(8,128)S(1)}, f32[64,512]{1,0:T(8,128)S(1)}, u32[]{:S(2)}, u32[]{:S(2)}) collective-permute-start(f32[64,512]{1,0:T(8,128)S(1)} %copy-done.41), channel_id=1, source_target_pairs={{0,3},{1,0},{2,1},{3,2},{4,7},{5,4},{6,5},{7,6},{8,11},{9,8},{10,9... | collective-permute-start | bytes 393224 | tf_op jit(solution)/shard_map/ppermute | solution.py:422
  (48 other events, 608.4 us)

commit v4 on v3

--- a/solution.py
+++ b/solution.py
@@ -341,7 +341,7 @@
             in_specs=specs,
             out_specs=[WHOLE] * len(outs),
             scratch_shapes=scratch,
-            compiler_params=pltpu.CompilerParams(vmem_limit_bytes=24 * 1024 * 1024),
+            compiler_params=pltpu.CompilerParams(vmem_limit_bytes=14 * 1024 * 1024),
         )(*args)
 
     return run
@@ -375,7 +375,7 @@
         return value
 
     def body(zones, index, table, levels, place, *refs):
-        to_b, to_a, alpha_a, kappa, alpha = refs[: plan.cross], refs[plan.cross : -3], refs[-3], refs[-2], refs[-1]
+        to_b, (kappa, left, right, alpha_a, alpha) = refs[: plan.cross], refs[plan.cross :]
         w, c = place[0], place[1]
 
         def step(off):
@@ -390,16 +390,40 @@
         for s, out in enumerate(to_b):
             out[0:h, :] = kappa[pl.ds(pl.multiple_of(lax.rem(c + s, plan.cross) * h, h), h), :]
             out[h:, :] = alpha[...]
-        for t, out in enumerate(to_a):
-            n = lax.rem(w + t, plan.wind)
-            lanes = pl.ds(pl.multiple_of(plan.local(n, c) * plan.width, plan.width), plan.width)
-            out[...] = kappa[:, lanes]
-
+        for at in range(0, plan.rows_here, INNER):
+            left[:, at : at + INNER] = kappa[at : at + INNER, 0 : plan.width].T[0:8, :]
+            right[:, at : at + INNER] = kappa[at : at + INNER, plan.cols_here - plan.width :].T[plan.width - 8 :, :]
+
+    edge = jax.ShapeDtypeStruct((8, plan.rows_here), F32)
     outs = [jax.ShapeDtypeStruct((h + 8, plan.cols_here), F32)] * plan.cross
-    outs += [jax.ShapeDtypeStruct((plan.rows_here, plan.width), F32)] * plan.wind
-    outs.append(jax.ShapeDtypeStruct((8, plan.width), F32))
-    scratch = [pltpu.VMEM(zone_map.shape, F32), pltpu.VMEM((8, plan.cols_here), F32)]
+    outs += [jax.ShapeDtypeStruct(zone_map.shape, F32), edge, edge, jax.ShapeDtypeStruct((8, plan.width), F32)]
+    scratch = [pltpu.VMEM((8, plan.cols_here), F32)]
     return call(body, outs, scratch, (), (), (0,))(zone_map, absorb_index, absorb_table, zone_conductivity, place)
+
+
+def home_kappa(plan, kappa, from_left, from_right, place):
+    per = plan.rows_here // INNER
+
+    def body(kappa, from_left, from_right, place, *refs):
+        outs, edges = refs[: plan.wind], refs[-1]
+        for at in range(per):
+            n = slice(at * INNER, (at + 1) * INNER)
+            edges[0, 8 * at : 8 * at + 8, :] = from_left[:, n]
+            edges[plan.wind - 1, 8 * (per + at) : 8 * (per + at) + 8, :] = from_right[:, n]
+            for i in range(plan.wind):
+                turned = kappa[n, i * plan.width : (i + 1) * plan.width].T
+                if i + 1 < plan.wind:
+                    edges[i + 1, 8 * at : 8 * at + 8, :] = turned[plan.width - 8 :, :]
+                if i:
+                    edges[i - 1, 8 * (per + at) : 8 * (per + at) + 8, :] = turned[0:8, :]
+        for t, out in enumerate(outs):
+            i = plan.local(lax.rem(place[0] + t, plan.wind), place[1])
+            out[0 : plan.rows_here, :] = kappa[:, pl.ds(pl.multiple_of(i * plan.width, plan.width), plan.width)]
+            out[plan.rows_here :, :] = edges[i]
+
+    outs = [jax.ShapeDtypeStruct((plan.rows_here + 16 * per, plan.width), F32)] * plan.wind
+    scratch = [pltpu.VMEM((plan.wind, 16 * per, INNER), F32)]
+    return call(body, outs, scratch)(kappa, from_left, from_right, place)
 
 
 def home_rows(plan, parts, place):
@@ -448,13 +472,18 @@
 
 
 def rows_kappa(plan, parts, place):
+    per = plan.rows_here // INNER
+
     def body(*refs):
         place, out, left, right = refs[plan.wind :]
         for t, ref in enumerate(refs[: plan.wind]):
-            w = lax.rem(place[0] + plan.wind - t, plan.wind)
-            out[pl.ds(pl.multiple_of(w * plan.rows_here, plan.rows_here), plan.rows_here), :] = ref[...]
-        for g in range(plan.rows // INNER):
-            plan.edges(out[g * INNER : (g + 1) * INNER, :], left, right, g * INNER)
+            first = lax.rem(place[0] + plan.wind - t, plan.wind) * plan.rows_here
+            out[pl.ds(pl.multiple_of(first, plan.rows_here), plan.rows_here), :] = ref[0 : plan.rows_here, :]
+            for at in range(per):
+                n = pl.ds(pl.multiple_of(first + at * INNER, INNER), INNER)
+                line = plan.rows_here + 8 * at
+                left[:, n] = ref[line : line + 8, :]
+                right[:, n] = ref[line + 8 * per : line + 8 * per + 8, :]
 
     edge = jax.ShapeDtypeStruct((8, plan.rows), F32)
     outs = [jax.ShapeDtypeStruct((plan.rows, plan.width), F32), edge, edge]
@@ -937,7 +966,8 @@
     to_b, *field_blocks = prepare_field(plan, field_real, field_imag, place)
     home_b = exchange(to_b, "cross")
     field_blocks = shifted(field_blocks, "wind")
-    *blocks, alpha_a = prepare(plan, zone_map, absorb_index, absorb_table, zone_conductivity, place)
+    *across, kappa, left, right, alpha_a = prepare(plan, zone_map, absorb_index, absorb_table, zone_conductivity, place)
+    along = home_kappa(plan, kappa, *next_prev(right, left, "cross", list(range(cross))), place)
 
     dft = jnp.asarray(dft_matrices())
     tab_a = lambda share: (jnp.asarray(row_blocks(plan.rows, share)), jnp.asarray(row_table(plan.rows)))
@@ -952,14 +982,13 @@
         part, beside, totals = cols_heat(plan, layer, plan.devices, dft, tab_b(0.5), received, alpha_b)
         return cols_smooth(plan, keep, kappa_b, above, below, part, beside, flip(totals), place)
 
-    home_b, across = lax.optimization_barrier((home_b, blocks[:cross]))
+    home_b, across = lax.optimization_barrier((home_b, across))
     sent = cols_send(plan, plan.home_b, False, dft, tab_b(0.5), home_b)
     kappa_b, alpha_b = home_rows(plan, shifted(across, "cross"), place)
     above, below = next_prev(kappa_b[-8:], kappa_b[:8], grid_axes, list(range(plan.devices)))
-    received, along = lax.optimization_barrier((flip(sent), blocks[cross:]))
+    received, along = lax.optimization_barrier((flip(sent), along))
     along = shifted(along, "wind")
-    kappa_a, left, right = rows_kappa(plan, along, place)
-    kappas = (kappa_a, *next_prev(right, left, grid_axes, columns_order))
+    kappas = rows_kappa(plan, along, place)
     home_a = in_order(field_blocks, place, 0)
     screen = smooth_a(0, 0.5, received)
     sent = rows_turn(plan, plan.home_a, True, *tab_a(0.5), screen, home_a)
@@ -973,11 +1002,11 @@
     field = rows_field(plan, plan.flip_a, *tab_a(1.0), field)
     sent = rows_turn(plan, plan.flip_a, True, *tab_a(0.5), screen, field)
     screen, *home_parts = smooth_b(1, True, flip(sent))
-    screen, home_parts = lax.optimization_barrier((flip(screen), home_parts))
-    screen = screen.reshape(plan.rows, plan.width)
+    home_parts = shifted(home_parts, "cross")
+    screen = flip(screen).reshape(plan.rows, plan.width)
     sent = rows_turn(plan, plan.flip_a, False, *tab_a(1.0), screen, field)
     back = cols_send(plan, plan.flip_b, True, dft, tab_b(1.0), flip(sent))
-    screen = home_screen(plan, shifted(home_parts, "cross"), place)
+    screen = home_screen(plan, home_parts, place)
     back = exchange(back, "cross")
     out_real = back[:, : plan.height].reshape(field_real.shape)
     out_imag = back[:, plan.height :].reshape(field_real.shape)

time: 380 us -> 370 us (0.974)
  blocking collectives: 162 us -> 132 us
  waiting for transfers between devices: 78.3 us -> 89.3 us
  Pallas kernels: 62.6 us -> 66.4 us
    all_to_all x7 -> x6, blocking collectives: 162 us -> 132 us  [exchange(): return lax.all_to_all(x, axes, split_axis=0, concat_axis=0, tiled=True)]
    all_to_all x4 -> x5, waiting for transfers between devices: 8.19 us -> 34.4 us  [exchange(): return lax.all_to_all(x, axes, split_axis=0, concat_axis=0, tiled=True)]
    ppermute x12, waiting for transfers between devices: 49.1 us -> 31.5 us  [shifted(): lax.ppermute(parts[s], axis, [(i, (i + s) % size) for i in range(size)])]
    all_to_all x4 -> x5, starting transfers between devices: 16.4 us -> 22.4 us  [exchange(): return lax.all_to_all(x, axes, split_axis=0, concat_axis=0, tiled=True)]
    pallas_call x21 -> x22, Pallas kernels: 62.6 us -> 66.4 us  [run(): pl.pallas_call(body, out_shape=[pltpu.VMEM(o.shape, o.dtype) if i in near...]
    unnamed x96 -> x76, local copies, waits for them, and re-layouts: 15.2 us -> 17.2 us
  transfers between devices with their start and end apart: 24 -> 25, of which waited for: 12 -> 14; matrix products, arithmetic and copies ran while one was open for 0% -> 0% of each run, Pallas kernels for 4% -> 5%
where the time goes in v4:
time: 370 us; the launch traced here: 366 us
  blocking collectives  132 us (36%)
  waiting for transfers between devices  89.3 us (24%)
  Pallas kernels  66.4 us (18%)
  starting transfers between devices  59.1 us (16%)
  local copies, waits for them, and re-layouts  18.3 us (5%)
    all_to_all x6, blocking collectives, exchange(): return lax.all_to_all(x, axes, split_axis=0, concat_axis=0, tiled=True)  132 us
    pallas_call x22, Pallas kernels, run(): pl.pallas_call(body, out_shape=[pltpu.VMEM(o.shape, o.dtype) if i in near...  66.4 us
    all_to_all x5, waiting for transfers between devices, exchange(): return lax.all_to_all(x, axes, split_axis=0, concat_axis=0, tiled=True)  34.4 us
    ppermute x12, waiting for transfers between devices, shifted(): lax.ppermute(parts[s], axis, [(i, (i + s) % size) for i in range(size)])  31.5 us
    all_to_all x5, starting transfers between devices, exchange(): return lax.all_to_all(x, axes, split_axis=0, concat_axis=0, tiled=True)  22.4 us
    ppermute x4, starting transfers between devices, next_prev(): lax.ppermute(value_up, axes, up)  19 us
    ppermute x4, waiting for transfers between devices, next_prev(): lax.ppermute(value_up, axes, up)  17.7 us
    unnamed x76, local copies, waits for them, and re-layouts  17.2 us
  transfers between devices with their start and end apart: 25, of which 14 were waited for; matrix products, arithmetic and copies ran while one was open for 0% of the time, Pallas kernels for 5%

profile of v4, /device:TPU:16, one launch (start us, length us, event | category | flops | bytes accessed | tf_op | source)
XLA Modules:
  0.0 366.1 jit_solution(3102468551478796729)
XLA Ops:
  13.1 10.2 %all-to-all-done.field = f32[4,128,512]{2,1,0:T(8,128)S(1)} async-done(((f32[4,128,512]{2,1,0:T(8,128)}), f32[4,128,512]{2,1,0:T(8,128)S(1)}, u32[]{:S(2)}, u32[]{:S(2)}) %all-to-all-start) | async-done | bytes 1048608 | tf_op jit(solution)/shard_map/all_to_all | solution.py:961
  28.4 5.4 %all-to-all-start.1 = ((f32[16,128,128]{2,1,0:T(8,128)}), f32[16,128,128]{2,1,0:T(8,128)}, u32[]{:S(2)}, u32[]{:S(2)}) async-start(f32[16,128,128]{2,1,0:T(8,128)} %copy-done.8), calls=%async_computation.1 | async-start | bytes 2097152 | tf_op jit(solution)/shard_map/all_to_all | solution.py:961
  46.6 24.2 %all-to-all-done.1.received = f32[16,128,128]{2,1,0:T(8,128)} async-done(((f32[16,128,128]{2,1,0:T(8,128)}), f32[16,128,128]{2,1,0:T(8,128)}, u32[]{:S(2)}, u32[]{:S(2)}) %all-to-all-start.1) | async-done | bytes 1048608 | tf_op jit(solution)/shard_map/all_to_all | solution.py:961
  71.2 4.4 %collective-permute-done.10.refs_1_ = f32[512,128]{1,0:T(8,128)} collective-permute-done((f32[512,128]{1,0:T(8,128)}, f32[512,128]{1,0:T(8,128)}, u32[]{:S(2)}, u32[]{:S(2)}) %collective-permute-start.10) | collective-permute-done | bytes 262176 | tf_op jit(solution)/shard_map/ppermute | solution.py:446
  75.6 4.4 %shard_map.252 = (f32[1024,128]{1,0:T(8,128)S(1)}, f32[8,1024]{1,0:T(8,128)S(1)}, f32[8,1024]{1,0:T(8,128)S(1)}) custom-call(bf16[8,2,256,256]{3,2,1,0:T(8,128)(2,1)S(1)} %copy-done, f32[128,128]{1,0:T(8,128)S(1)} %copy-done.9, f32[16,128,128]{2,1,0:T(8,128)} %all-to-all-done.1.received, f32[1,128]{1,0:T(1,128)S(1)} %get-tuple-element.120.alpha), custom_call_target="tpu_custom_call" | custom-call | tf_op jit(solution)/shard_map/pallas_call | solution.py:338
  80.9 9.9 %collective-permute-start.5 = (f32[8,1024]{1,0:T(8,128)S(1)}, f32[8,1024]{1,0:T(8,128)S(1)}, u32[]{:S(2)}, u32[]{:S(2)}) collective-permute-start(f32[8,1024]{1,0:T(8,128)S(1)} %get-tuple-element.80), channel_id=1, source_target_pairs={{0,4},{4,8},{8,12},{12,13},{13,9},{9,5},{5,1},{1,2},{2,6},{6,10},{... | collective-permute-start | bytes 98312 | tf_op jit(solution)/shard_map/ppermute | solution.py:761
  96.7 4.4 %shard_map.254.screen = f32[1024,128]{1,0:T(8,128)S(1)} custom-call(f32[1024,128]{1,0:T(8,128)S(1)} %get-tuple-element.79.heat, f32[8,1024]{1,0:T(8,128)S(1)} %collective-permute-done.5.from_left, f32[8,1024]{1,0:T(8,128)S(1)} %collective-permute-done.6.from_right, f32[1024,128]{1,0:T(8,128)S(1)} %get-tuple-element.86.kappa, ...), custom_call_target="tpu_custom_call" | custom-call | tf_op jit(solution)/shard_map/pallas_call | solution.py:338
  105.8 5.3 %all-to-all-start.2 = ((f32[16,136,128]{2,1,0:T(8,128)}), f32[16,136,128]{2,1,0:T(8,128)}, u32[]{:S(2)}, u32[]{:S(2)}) async-start(f32[16,136,128]{2,1,0:T(8,128)} %copy-done.6), calls=%async_computation.2 | async-start | bytes 2228224 | tf_op jit(solution)/shard_map/all_to_all | solution.py:961
  114.1 8.2 %collective-permute-done.refs_1_ = f32[72,512]{1,0:T(8,128)S(1)} collective-permute-done((f32[72,512]{1,0:T(8,128)S(1)}, f32[72,512]{1,0:T(8,128)S(1)}, u32[]{:S(2)}, u32[]{:S(2)}) %collective-permute-start) | collective-permute-done | bytes 147488 | tf_op jit(solution)/shard_map/ppermute | solution.py:446
  127.3 4.4 %collective-permute-start.13 = (f32[8,2048]{1,0:T(8,128)S(1)}, f32[8,2048]{1,0:T(8,128)S(1)}, u32[]{:S(2)}, u32[]{:S(2)}) collective-permute-start(f32[8,2048]{1,0:T(8,128)S(1)} %get-tuple-element.118), channel_id=1, source_target_pairs={{0,1},{1,2},{2,3},{3,4},{4,5},{5,6},{6,7},{7,8},{8,9},{9,10},{10,1... | collective-permute-start | bytes 196616 | tf_op jit(solution)/shard_map/ppermute | solution.py:761
  133.8 4.6 %collective-permute-done.13.above = f32[8,2048]{1,0:T(8,128)S(1)} collective-permute-done((f32[8,2048]{1,0:T(8,128)S(1)}, f32[8,2048]{1,0:T(8,128)S(1)}, u32[]{:S(2)}, u32[]{:S(2)}) %collective-permute-start.13) | collective-permute-done | bytes 65568 | tf_op jit(solution)/shard_map/ppermute | solution.py:761
  138.5 5.3 %shard_map.257 = (f32[64,2048]{1,0:T(8,128)S(1)}, f32[8,2048]{1,0:T(8,128)S(1)}, f32[16,16,128]{2,1,0:T(8,128)S(1)}) custom-call(bf16[4,256,256]{2,1,0:T(8,128)(2,1)S(1)} %copy-done.1, f32[64,128]{1,0:T(8,128)S(1)} %copy-done.16, f32[16,136,128]{2,1,0:T(8,128)} %all-to-all-done.2.received, f32[8,2048]{1,0:T(8,128)S(1)} %get-tuple-element.96.absorption), custom_call_target="tpu_custom_call" | custom-call | tf_op jit(solution)/shard_map/pallas_call | solution.py:338
  143.8 11.0 %all_to_all.55.refs_0_ = f32[16,16,128]{2,1,0:T(8,128)S(1)} all-to-all(f32[16,16,128]{2,1,0:T(8,128)S(1)} %get-tuple-element.99), channel_id=1, replica_groups=mesh['beams'=2,'wind'=4,'cross'=4] {'wind','cross'}, dimensions={0} | all-to-all | bytes 262144 | tf_op jit(solution)/shard_map/all_to_all | solution.py:961
  158.3 5.2 %shard_map.259 = (f32[16,128,128]{2,1,0:T(8,128)S(1)}, f32[16,128,128]{2,1,0:T(8,128)S(1)}) custom-call(bf16[4,256,256]{2,1,0:T(8,128)(2,1)S(1)} %copy-done.1, f32[96,128]{1,0:T(8,128)S(1)} %copy-done.21, f32[64,2048]{1,0:T(8,128)S(1)} %shard_map.258.screen, f32[4,128,512]{2,1,0:T(8,128)S(1)} %copy-done.3), custom_call_target="tpu_custom_call" | custom-call | tf_op jit(solution)/shard_map/pallas_call | solution.py:338
  163.5 30.8 %all_to_all.56.received = f32[16,128,128]{2,1,0:T(8,128)} all-to-all(f32[16,128,128]{2,1,0:T(8,128)S(1)} %get-tuple-element.101), channel_id=1, replica_groups=mesh['beams'=2,'wind'=4,'cross'=4] {'wind','cross'}, dimensions={0} | all-to-all | bytes 2097152 | tf_op jit(solution)/shard_map/all_to_all | solution.py:961
  194.3 4.6 %all-to-all-start.4 = ((f32[16,128,128]{2,1,0:T(8,128)}), f32[16,128,128]{2,1,0:T(8,128)}, u32[]{:S(2)}, u32[]{:S(2)}) async-start(f32[16,128,128]{2,1,0:T(8,128)} %copy-done.15), calls=%async_computation.4 | async-start | bytes 2097152 | tf_op jit(solution)/shard_map/all_to_all | solution.py:961
  210.7 13.1 %collective-permute-done.15.from_left = f32[8,1024]{1,0:T(8,128)S(1)} collective-permute-done((f32[8,1024]{1,0:T(8,128)S(1)}, f32[8,1024]{1,0:T(8,128)S(1)}, u32[]{:S(2)}, u32[]{:S(2)}) %collective-permute-start.15) | collective-permute-done | bytes 32800 | tf_op jit(solution)/shard_map/ppermute | solution.py:761
  223.8 4.4 %shard_map.261.screen = f32[1024,128]{1,0:T(8,128)S(1)} custom-call(f32[1024,128]{1,0:T(8,128)S(1)} %get-tuple-element.102.heat, f32[8,1024]{1,0:T(8,128)S(1)} %collective-permute-done.15.from_left, f32[8,1024]{1,0:T(8,128)S(1)} %collective-permute-done.16.from_right, f32[1024,128]{1,0:T(8,128)S(1)} %copy-done.14, ...), custom_call_target="tpu_custom_call" | custom-call | tf_op jit(solution)/shard_map/pallas_call | solution.py:338
  237.5 31.4 %all_to_all.57.received = f32[16,136,128]{2,1,0:T(8,128)S(1)} all-to-all(f32[16,136,128]{2,1,0:T(8,128)S(1)} %shard_map.263), channel_id=1, replica_groups=mesh['beams'=2,'wind'=4,'cross'=4] {'wind','cross'}, dimensions={0} | all-to-all | bytes 2228224 | tf_op jit(solution)/shard_map/all_to_all | solution.py:961
  273.0 10.3 %all_to_all.58.refs_0_ = f32[16,16,128]{2,1,0:T(8,128)S(1)} all-to-all(f32[16,16,128]{2,1,0:T(8,128)S(1)} %get-tuple-element.109), channel_id=1, replica_groups=mesh['beams'=2,'wind'=4,'cross'=4] {'wind','cross'}, dimensions={0} | all-to-all | bytes 262144 | tf_op jit(solution)/shard_map/all_to_all | solution.py:961
  286.8 18.8 %all_to_all.59 = f32[16,64,128]{2,1,0:T(8,128)S(1)} all-to-all(f32[16,64,128]{2,1,0:T(8,128)S(1)} %get-tuple-element.110), channel_id=1, replica_groups=mesh['beams'=2,'wind'=4,'cross'=4] {'wind','cross'}, dimensions={0} | all-to-all | bytes 1048576 | tf_op jit(solution)/shard_map/all_to_all | solution.py:961
  308.6 29.4 %all_to_all.60.field = f32[16,128,128]{2,1,0:T(8,128)S(1)} all-to-all(f32[16,128,128]{2,1,0:T(8,128)S(1)} %shard_map.266), channel_id=1, replica_groups=mesh['beams'=2,'wind'=4,'cross'=4] {'wind','cross'}, dimensions={0} | all-to-all | bytes 2097152 | tf_op jit(solution)/shard_map/all_to_all | solution.py:961
  338.0 4.2 %shard_map.267 = f32[4,128,512]{2,1,0:T(8,128)} custom-call(bf16[4,256,256]{2,1,0:T(8,128)(2,1)S(1)} %copy-done.1, f32[64,128]{1,0:T(8,128)S(1)} %copy-done.22, f32[16,128,128]{2,1,0:T(8,128)S(1)} %all_to_all.60.field), custom_call_target="tpu_custom_call" | custom-call | tf_op jit(solution)/shard_map/pallas_call | solution.py:338
  349.2 13.2 %collective-permute-done.17.refs_1_ = f32[64,512]{1,0:T(8,128)S(1)} collective-permute-done((f32[64,512]{1,0:T(8,128)S(1)}, f32[64,512]{1,0:T(8,128)S(1)}, u32[]{:S(2)}, u32[]{:S(2)}) %collective-permute-start.17) | collective-permute-done | bytes 131104 | tf_op jit(solution)/shard_map/ppermute | solution.py:446
  (134 shorter events, 97.9 us)
Async XLA Ops:
  5.2 18.1 %all-to-all-start = ((f32[4,128,512]{2,1,0:T(8,128)}), f32[4,128,512]{2,1,0:T(8,128)S(1)}, u32[]{:S(2)}, u32[]{:S(2)}) async-start(f32[4,128,512]{2,1,0:T(8,128)} %get-tuple-element.59), calls=%async_computation | async-start | bytes 2097152 | tf_op jit(solution)/shard_map/all_to_all | solution.py:961
  28.4 42.5 %all-to-all-start.1 = ((f32[16,128,128]{2,1,0:T(8,128)}), f32[16,128,128]{2,1,0:T(8,128)}, u32[]{:S(2)}, u32[]{:S(2)}) async-start(f32[16,128,128]{2,1,0:T(8,128)} %copy-done.8), calls=%async_computation.1 | async-start | bytes 2097152 | tf_op jit(solution)/shard_map/all_to_all | solution.py:961
  33.7 41.8 %collective-permute-start.10 = (f32[512,128]{1,0:T(8,128)}, f32[512,128]{1,0:T(8,128)}, u32[]{:S(2)}, u32[]{:S(2)}) collective-permute-start(f32[512,128]{1,0:T(8,128)} %copy-done.28), channel_id=1, source_target_pairs={{0,4},{4,8},{8,12},{12,0},{1,5},{5,9},{9,13},{13,1},{2,6},{6,10},{... | collective-permute-start | bytes 786440 | tf_op jit(solution)/shard_map/ppermute | solution.py:446
  35.2 45.7 %collective-permute-start.11 = (f32[512,128]{1,0:T(8,128)}, f32[512,128]{1,0:T(8,128)}, u32[]{:S(2)}, u32[]{:S(2)}) collective-permute-start(f32[512,128]{1,0:T(8,128)} %copy-done.27), channel_id=1, source_target_pairs={{0,8},{4,12},{8,0},{12,4},{1,9},{5,13},{9,1},{13,5},{2,10},{6,14},... | collective-permute-start | bytes 786440 | tf_op jit(solution)/shard_map/ppermute | solution.py:446
  35.8 55.1 %collective-permute-start.12 = (f32[512,128]{1,0:T(8,128)}, f32[512,128]{1,0:T(8,128)}, u32[]{:S(2)}, u32[]{:S(2)}) collective-permute-start(f32[512,128]{1,0:T(8,128)} %copy-done.26), channel_id=1, source_target_pairs={{0,12},{4,0},{8,4},{12,8},{1,13},{5,1},{9,5},{13,9},{2,14},{6,2},{... | collective-permute-start | bytes 786440 | tf_op jit(solution)/shard_map/ppermute | solution.py:446
  38.2 5.0 %collective-permute-start.4 = (f32[8,256]{1,0:T(8,128)S(1)}, f32[8,256]{1,0:T(8,128)S(1)}, u32[]{:S(2)}, u32[]{:S(2)}) collective-permute-start(f32[8,256]{1,0:T(8,128)S(1)} %get-tuple-element.72), channel_id=1, source_target_pairs={{1,0},{2,1},{3,2},{5,4},{6,5},{7,6},{9,8},{10,9},{11,10},{13,12},{... | collective-permute-start | bytes 24584 | tf_op jit(solution)/shard_map/ppermute | solution.py:761
  70.9 23.1 %collective-permute-start.7 = (f32[288,128]{1,0:T(8,128)}, f32[288,128]{1,0:T(8,128)S(1)}, u32[]{:S(2)}, u32[]{:S(2)}) collective-permute-start(f32[288,128]{1,0:T(8,128)} %copy-done.37), channel_id=1, source_target_pairs={{0,4},{4,8},{8,12},{12,0},{1,5},{5,9},{9,13},{13,1},{2,6},{6,10},{... | collective-permute-start | bytes 442376 | tf_op jit(solution)/shard_map/ppermute | solution.py:446
  70.9 23.1 %collective-permute-start.8 = (f32[288,128]{1,0:T(8,128)}, f32[288,128]{1,0:T(8,128)S(1)}, u32[]{:S(2)}, u32[]{:S(2)}) collective-permute-start(f32[288,128]{1,0:T(8,128)} %copy-done.36), channel_id=1, source_target_pairs={{0,8},{4,12},{8,0},{12,4},{1,9},{5,13},{9,1},{13,5},{2,10},{6,14},... | collective-permute-start | bytes 442376 | tf_op jit(solution)/shard_map/ppermute | solution.py:446
  75.5 18.5 %collective-permute-start.9 = (f32[288,128]{1,0:T(8,128)}, f32[288,128]{1,0:T(8,128)S(1)}, u32[]{:S(2)}, u32[]{:S(2)}) collective-permute-start(f32[288,128]{1,0:T(8,128)} %copy-done.35), channel_id=1, source_target_pairs={{0,12},{4,0},{8,4},{12,8},{1,13},{5,1},{9,5},{13,9},{2,14},{6,2},{... | collective-permute-start | bytes 442376 | tf_op jit(solution)/shard_map/ppermute | solution.py:446
  80.9 13.7 %collective-permute-start.5 = (f32[8,1024]{1,0:T(8,128)S(1)}, f32[8,1024]{1,0:T(8,128)S(1)}, u32[]{:S(2)}, u32[]{:S(2)}) collective-permute-start(f32[8,1024]{1,0:T(8,128)S(1)} %get-tuple-element.80), channel_id=1, source_target_pairs={{0,4},{4,8},{8,12},{12,13},{13,9},{9,5},{5,1},{1,2},{2,6},{6,10},{... | collective-permute-start | bytes 98312 | tf_op jit(solution)/shard_map/ppermute | solution.py:761
  90.9 5.8 %collective-permute-start.6 = (f32[8,1024]{1,0:T(8,128)S(1)}, f32[8,1024]{1,0:T(8,128)S(1)}, u32[]{:S(2)}, u32[]{:S(2)}) collective-permute-start(f32[8,1024]{1,0:T(8,128)S(1)} %get-tuple-element.81), channel_id=1, source_target_pairs={{4,0},{8,4},{12,8},{13,12},{9,13},{5,9},{1,5},{2,1},{6,2},{10,6},{... | collective-permute-start | bytes 98312 | tf_op jit(solution)/shard_map/ppermute | solution.py:761
  105.8 32.6 %all-to-all-start.2 = ((f32[16,136,128]{2,1,0:T(8,128)}), f32[16,136,128]{2,1,0:T(8,128)}, u32[]{:S(2)}, u32[]{:S(2)}) async-start(f32[16,136,128]{2,1,0:T(8,128)} %copy-done.6), calls=%async_computation.2 | async-start | bytes 2228224 | tf_op jit(solution)/shard_map/all_to_all | solution.py:961
  111.1 11.2 %collective-permute-start = (f32[72,512]{1,0:T(8,128)S(1)}, f32[72,512]{1,0:T(8,128)S(1)}, u32[]{:S(2)}, u32[]{:S(2)}) collective-permute-start(f32[72,512]{1,0:T(8,128)S(1)} %copy-done.34), channel_id=1, source_target_pairs={{0,1},{1,2},{2,3},{3,0},{4,5},{5,6},{6,7},{7,4},{8,9},{9,10},{10,1... | collective-permute-start | bytes 442376 | tf_op jit(solution)/shard_map/ppermute | solution.py:446
  111.3 12.2 %collective-permute-start.1 = (f32[72,512]{1,0:T(8,128)S(1)}, f32[72,512]{1,0:T(8,128)S(1)}, u32[]{:S(2)}, u32[]{:S(2)}) collective-permute-start(f32[72,512]{1,0:T(8,128)S(1)} %copy-done.32), channel_id=1, source_target_pairs={{0,2},{1,3},{2,0},{3,1},{4,6},{5,7},{6,4},{7,5},{8,10},{9,11},{10,... | collective-permute-start | bytes 442376 | tf_op jit(solution)/shard_map/ppermute | solution.py:446
  112.7 13.1 %collective-permute-start.2 = (f32[72,512]{1,0:T(8,128)S(1)}, f32[72,512]{1,0:T(8,128)S(1)}, u32[]{:S(2)}, u32[]{:S(2)}) collective-permute-start(f32[72,512]{1,0:T(8,128)S(1)} %copy-done.30), channel_id=1, source_target_pairs={{0,3},{1,0},{2,1},{3,2},{4,7},{5,4},{6,5},{7,6},{8,11},{9,8},{10,9... | collective-permute-start | bytes 442376 | tf_op jit(solution)/shard_map/ppermute | solution.py:446
  127.3 11.1 %collective-permute-start.13 = (f32[8,2048]{1,0:T(8,128)S(1)}, f32[8,2048]{1,0:T(8,128)S(1)}, u32[]{:S(2)}, u32[]{:S(2)}) collective-permute-start(f32[8,2048]{1,0:T(8,128)S(1)} %get-tuple-element.118), channel_id=1, source_target_pairs={{0,1},{1,2},{2,3},{3,4},{4,5},{5,6},{6,7},{7,8},{8,9},{9,10},{10,1... | collective-permute-start | bytes 196616 | tf_op jit(solution)/shard_map/ppermute | solution.py:761
  131.7 6.7 %collective-permute-start.14 = (f32[8,2048]{1,0:T(8,128)S(1)}, f32[8,2048]{1,0:T(8,128)S(1)}, u32[]{:S(2)}, u32[]{:S(2)}) collective-permute-start(f32[8,2048]{1,0:T(8,128)S(1)} %get-tuple-element.117), channel_id=1, source_target_pairs={{1,0},{2,1},{3,2},{4,3},{5,4},{6,5},{7,6},{8,7},{9,8},{10,9},{11,1... | collective-permute-start | bytes 196616 | tf_op jit(solution)/shard_map/ppermute | solution.py:761
  194.3 34.7 %all-to-all-start.4 = ((f32[16,128,128]{2,1,0:T(8,128)}), f32[16,128,128]{2,1,0:T(8,128)}, u32[]{:S(2)}, u32[]{:S(2)}) async-start(f32[16,128,128]{2,1,0:T(8,128)} %copy-done.15), calls=%async_computation.4 | async-start | bytes 2097152 | tf_op jit(solution)/shard_map/all_to_all | solution.py:961
  204.9 18.9 %collective-permute-start.15 = (f32[8,1024]{1,0:T(8,128)S(1)}, f32[8,1024]{1,0:T(8,128)S(1)}, u32[]{:S(2)}, u32[]{:S(2)}) collective-permute-start(f32[8,1024]{1,0:T(8,128)S(1)} %get-tuple-element.103), channel_id=1, source_target_pairs={{0,4},{4,8},{8,12},{12,13},{13,9},{9,5},{5,1},{1,2},{2,6},{6,10},{... | collective-permute-start | bytes 98312 | tf_op jit(solution)/shard_map/ppermute | solution.py:761
  208.3 15.5 %collective-permute-start.16 = (f32[8,1024]{1,0:T(8,128)S(1)}, f32[8,1024]{1,0:T(8,128)S(1)}, u32[]{:S(2)}, u32[]{:S(2)}) collective-permute-start(f32[8,1024]{1,0:T(8,128)S(1)} %get-tuple-element.104), channel_id=1, source_target_pairs={{4,0},{8,4},{12,8},{13,12},{9,13},{5,9},{1,5},{2,1},{6,2},{10,6},{... | collective-permute-start | bytes 98312 | tf_op jit(solution)/shard_map/ppermute | solution.py:761
  342.2 22.8 %all-to-all-start.10 = ((f32[4,128,512]{2,1,0:T(8,128)}), f32[4,128,512]{2,1,0:T(8,128)S(1)}, u32[]{:S(2)}, u32[]{:S(2)}) async-start(f32[4,128,512]{2,1,0:T(8,128)} %shard_map.267), calls=%async_computation.10 | async-start | bytes 2097152 | tf_op jit(solution)/shard_map/all_to_all | solution.py:961
  345.7 16.6 %collective-permute-start.17 = (f32[64,512]{1,0:T(8,128)S(1)}, f32[64,512]{1,0:T(8,128)S(1)}, u32[]{:S(2)}, u32[]{:S(2)}) collective-permute-start(f32[64,512]{1,0:T(8,128)S(1)} %get-tuple-element.112), channel_id=1, source_target_pairs={{0,1},{1,2},{2,3},{3,0},{4,5},{5,6},{6,7},{7,4},{8,9},{9,10},{10,1... | collective-permute-start | bytes 393224 | tf_op jit(solution)/shard_map/ppermute | solution.py:446
  346.2 17.3 %collective-permute-start.18 = (f32[64,512]{1,0:T(8,128)S(1)}, f32[64,512]{1,0:T(8,128)S(1)}, u32[]{:S(2)}, u32[]{:S(2)}) collective-permute-start(f32[64,512]{1,0:T(8,128)S(1)} %get-tuple-element.113), channel_id=1, source_target_pairs={{0,2},{1,3},{2,0},{3,1},{4,6},{5,7},{6,4},{7,5},{8,10},{9,11},{10,... | collective-permute-start | bytes 393224 | tf_op jit(solution)/shard_map/ppermute | solution.py:446
  347.8 15.8 %collective-permute-start.19 = (f32[64,512]{1,0:T(8,128)S(1)}, f32[64,512]{1,0:T(8,128)S(1)}, u32[]{:S(2)}, u32[]{:S(2)}) collective-permute-start(f32[64,512]{1,0:T(8,128)S(1)} %get-tuple-element.114), channel_id=1, source_target_pairs={{0,3},{1,0},{2,1},{3,2},{4,7},{5,4},{6,5},{7,6},{8,11},{9,8},{10,9... | collective-permute-start | bytes 393224 | tf_op jit(solution)/shard_map/ppermute | solution.py:446
  (39 other events, 330.8 us)

commit v5 on v4

--- a/solution.py
+++ b/solution.py
@@ -141,10 +141,12 @@
 
 def chunks(count, body):
     def step(i, carry):
-        body(pl.multiple_of(i * CHUNK, CHUNK))
+        for n in range(side):
+            body(pl.multiple_of((side * i + n) * CHUNK, CHUNK))
         return carry
 
-    lax.fori_loop(0, count // CHUNK, step, 0)
+    side = 2 if count % (2 * CHUNK) == 0 else 1
+    lax.fori_loop(0, count // (side * CHUNK), step, 0)
 
 
 def along_rows(read, write, matrices, table, xh, z):
@@ -281,6 +283,19 @@
         turned = value.T
         left[:, at : at + INNER] = turned[0:8, :]
         right[:, at : at + INNER] = turned[self.width - 8 : self.width, :]
+
+    def send_sides(self, ref):
+        h, w = self.height, self.width
+        last = self.devices - 1
+        for b in range(self.devices):
+            turned = ref[self.slot(b), 0 : 2 * h, :].T
+            if b < last:
+                ref[self.slot(b + 1), 2 * h : 2 * h + 2, :] = turned[w - 2 : w, :]
+            if b:
+                ref[self.slot(b - 1), 2 * h + 2 : 2 * h + 4, :] = turned[0:2, :]
+        none = jnp.zeros((2, w), F32)
+        ref[self.slot(0), 2 * h : 2 * h + 2, :] = none
+        ref[self.slot(last), 2 * h + 2 : 2 * h + 4, :] = none
 
     def home_b(self, ref, b, off):
         per = self.cols_here // INNER
@@ -391,25 +406,45 @@
             out[0:h, :] = kappa[pl.ds(pl.multiple_of(lax.rem(c + s, plan.cross) * h, h), h), :]
             out[h:, :] = alpha[...]
         for at in range(0, plan.rows_here, INNER):
-            left[:, at : at + INNER] = kappa[at : at + INNER, 0 : plan.width].T[0:8, :]
-            right[:, at : at + INNER] = kappa[at : at + INNER, plan.cols_here - plan.width :].T[plan.width - 8 :, :]
-
-    edge = jax.ShapeDtypeStruct((8, plan.rows_here), F32)
+            left[0:8, at : at + INNER] = kappa[at : at + INNER, 0 : plan.width].T[0:8, :]
+            right[0:8, at : at + INNER] = kappa[at : at + INNER, plan.cols_here - plan.width :].T[plan.width - 8 :, :]
+        left[8:16, :] = jnp.zeros((8, plan.rows_here), F32)
+        right[8:16, :] = jnp.zeros((8, plan.rows_here), F32)
+        left[8:16, 0:INNER] = alpha[:, 0 : plan.width]
+        right[8:16, 0:INNER] = alpha[:, plan.cols_here - plan.width :]
+
+    edge = jax.ShapeDtypeStruct((16, plan.rows_here), F32)
     outs = [jax.ShapeDtypeStruct((h + 8, plan.cols_here), F32)] * plan.cross
     outs += [jax.ShapeDtypeStruct(zone_map.shape, F32), edge, edge, jax.ShapeDtypeStruct((8, plan.width), F32)]
-    scratch = [pltpu.VMEM((8, plan.cols_here), F32)]
-    return call(body, outs, scratch, (), (), (0,))(zone_map, absorb_index, absorb_table, zone_conductivity, place)
-
-
-def home_kappa(plan, kappa, from_left, from_right, place):
+    outs.append(jax.ShapeDtypeStruct((8, plan.cols_here), F32))
+    return call(body, outs, [], (), (), (0,))(
+        zone_map, absorb_index, absorb_table, zone_conductivity, place
+    )
+
+
+def home_kappa(plan, kappa, from_left, from_right, alpha, place):
     per = plan.rows_here // INNER
 
-    def body(kappa, from_left, from_right, place, *refs):
+    def body(kappa, from_left, from_right, alpha, place, side_alpha, *refs):
         outs, edges = refs[: plan.wind], refs[-1]
+        mine = plan.local(place[0], place[1])
+        side_alpha[...] = jnp.zeros_like(side_alpha)
+        for i in range(plan.wind):
+
+            @pl.when(mine == i)
+            def _():
+                for layer in range(LAYERS):
+                    line = slice(layer, layer + 1)
+                    before = alpha[line, (i - 1) * plan.width : i * plan.width] if i else from_left[8 + layer : 9 + layer, 0:INNER]
+                    last = i + 1 == plan.wind
+                    after = from_right[8 + layer : 9 + layer, 0:INNER] if last else alpha[line, (i + 1) * plan.width : (i + 2) * plan.width]
+                    for n, value in enumerate((before[:, -2:-1], before[:, -1:], after[:, 0:1], after[:, 1:2])):
+                        side_alpha[layer, n : n + 1, :] = jnp.broadcast_to(value, (1, INNER))
+
         for at in range(per):
             n = slice(at * INNER, (at + 1) * INNER)
-            edges[0, 8 * at : 8 * at + 8, :] = from_left[:, n]
-            edges[plan.wind - 1, 8 * (per + at) : 8 * (per + at) + 8, :] = from_right[:, n]
+            edges[0, 8 * at : 8 * at + 8, :] = from_left[0:8, n]
+            edges[plan.wind - 1, 8 * (per + at) : 8 * (per + at) + 8, :] = from_right[0:8, n]
             for i in range(plan.wind):
                 turned = kappa[n, i * plan.width : (i + 1) * plan.width].T
                 if i + 1 < plan.wind:
@@ -421,9 +456,12 @@
             out[0 : plan.rows_here, :] = kappa[:, pl.ds(pl.multiple_of(i * plan.width, plan.width), plan.width)]
             out[plan.rows_here :, :] = edges[i]
 
-    outs = [jax.ShapeDtypeStruct((plan.rows_here + 16 * per, plan.width), F32)] * plan.wind
+    outs = [jax.ShapeDtypeStruct((LAYERS, 8, INNER), F32)]
+    outs += [jax.ShapeDtypeStruct((plan.rows_here + 16 * per, plan.width), F32)] * plan.wind
     scratch = [pltpu.VMEM((plan.wind, 16 * per, INNER), F32)]
-    return call(body, outs, scratch)(kappa, from_left, from_right, place)
+    return call(body, outs, scratch)(
+        kappa, from_left, from_right, alpha, place
+    )
 
 
 def home_rows(plan, parts, place):
@@ -497,12 +535,16 @@
     return call(body, [plan.sent], plan.work_a(), (0, 1, 2), (0,))(dft, table, field)[0]
 
 
-def cols_send(plan, read_field, back, dft, table, field):
-    out = jax.ShapeDtypeStruct((plan.cross, 2 * plan.height, plan.cols_here), F32) if back else plan.sent
+def cols_send(plan, read_field, back, dft, table, field, sides=False):
+    out = plan.sent_wide if sides else plan.sent
+    if back:
+        out = jax.ShapeDtypeStruct((plan.cross, 2 * plan.height, plan.cols_here), F32)
 
     def body(dft, table, field, out, *work):
         put = plan.back_b if back else plan.send_b
         along_cols(plan.height, functools.partial(read_field, field), [functools.partial(put, out)], dft, table, *work)
+        if sides:
+            plan.send_sides(out)
 
     return call(body, [out], plan.work_b(), (0, 1, 2), () if back else (0,))(dft, table, field)[0]
 
@@ -554,8 +596,10 @@
             return screened(read_field(field, b, off), screen[pl.ds(off, CHUNK), pl.ds(b * INNER, INNER)])
 
         along_cols(plan.height, read, [functools.partial(plan.send_b, out) for out in outs], dft, table, *work)
-
-    return call(body, [plan.sent] * sets, plan.work_b(), (0, 1, 2), range(sets))(
+        if sets > 1:
+            plan.send_sides(outs[0])
+
+    return call(body, [plan.sent_wide if sets > 1 and n == 0 else plan.sent for n in range(sets)], plan.work_b(), (0, 1, 2), range(sets))(
         dft, table, screen, field
     )
 
@@ -657,16 +701,58 @@
     )
 
 
-def rows_heat(plan, dft, table, received, alpha):
+def rows_heat(plan, matrices, table, received, alpha, side_table, side_alpha):
     width = plan.width
-
-    def body(dft, table, received, alpha, heat, edge_left, edge_right, xh, z, dep):
+    outer = plan.rows // INNER
+    per = INNER // plan.height
+    two_rows = lambda a, b: lax.dot_general(a, b, (((1,), (1,)), ((), ())), preferred_element_type=F32)
+
+    def sides(matrices, received, side_table, side_alpha, from_left, from_right):
+        h = plan.height
+        lane = lax.broadcasted_iota(jnp.int32, (8, INNER), 1)
+        row = lambda part: side_table[part : part + 1, :]
+        points = []
+        for a in range(outer):
+            re = jnp.zeros((8, INNER), F32)
+            im = re
+            for j in range(per):
+                part = received[a * per + j, 2 * h : 2 * h + 8, :]
+                here = (lane >= j * h) & (lane < (j + 1) * h)
+                re = jnp.where(here, pltpu.roll(part, j * h, 1) if j else part, re)
+                im = jnp.where(here, pltpu.roll(part, (j * h + INNER - h) % INNER, 1), im)
+            points.append((re, im))
+        values = []
+        for k, value in enumerate(small_fft(points, -1)):
+            if k:
+                value = times(value, (row(k), row(outer + k)))
+            high, low = split(jnp.concatenate(value, axis=1))
+            both = two_rows(jnp.concatenate([high, low], axis=0), matrices[k, 0])
+            value = both[0:8] + both[8:16] + two_rows(jnp.concatenate([high, high], axis=0), matrices[k, 1])[0:8]
+            value = (value[:, :INNER], value[:, INNER:])
+            if k:
+                value = times(value, (row(k), -row(outer + k)))
+            values.append(value)
+        deposits = [side_alpha[...] * (re * re + im * im) for re, im in small_fft(values, 1)]
+        high, low = split(jnp.concatenate(deposits, axis=0))
+        ones = lower_ones(INNER)
+        sums = two_rows(high, ones) + two_rows(low, ones)
+        carry = jnp.zeros((8, 1), F32)
+        none = jnp.zeros((6, INNER), F32)
+        for a in range(outer):
+            part = sums[8 * a : 8 * a + 8] + carry
+            carry = part[:, INNER - 1 : INNER]
+            n = slice(a * INNER, (a + 1) * INNER)
+            from_left[:, n] = jnp.concatenate([none, part[0:2]], axis=0)
+            from_right[:, n] = jnp.concatenate([part[2:4], none], axis=0)
+
+    def body(matrices, table, received, alpha, side_table, side_alpha, heat, from_left, from_right, xh, z, dep):
         def write(a, off, value):
             deposit = alpha[...] * (value[0] * value[0] + value[1] * value[1])
             rows = pl.ds(a * INNER + off, CHUNK)
             dep[rows, 0:width], dep[rows, width : 2 * width] = split(deposit)
 
-        along_rows(functools.partial(plan.flip_a, received), write, dft, table, xh, z)
+        sides(matrices, received, side_table, side_alpha, from_left, from_right)
+        along_rows(functools.partial(plan.flip_a, received), write, matrices, table, xh, z)
         tile = 2 * INNER
         ones = lower_ones(tile)
         carry = jnp.zeros((1, width), F32)
@@ -675,13 +761,11 @@
             value = both[:, :width] + both[:, width:] + carry
             heat[g * tile : (g + 1) * tile, :] = value
             carry = value[tile - 1 : tile, :]
-        for g in range(plan.rows // INNER):
-            plan.edges(heat[g * INNER : (g + 1) * INNER, :], edge_left, edge_right, g * INNER)
 
     edge = jax.ShapeDtypeStruct((8, plan.rows), F32)
     outs = [jax.ShapeDtypeStruct((plan.rows, width), F32), edge, edge]
     scratch = plan.work_a() + [pltpu.VMEM((plan.rows, 2 * width), BF16)]
-    return call(body, outs, scratch, (0, 1, 2), ())(dft, table, received, alpha)
+    return call(body, outs, scratch, (0, 1, 2), ())(matrices, table, received, alpha, side_table, side_alpha)
 
 
 def rows_turn(plan, read_field, wide, dft, table, screen, field):
@@ -955,7 +1039,6 @@
     w, c = lax.axis_index("wind"), lax.axis_index("cross")
     place = jnp.stack([w, c]).astype(jnp.int32)
     grid_axes = ("wind", "cross")
-    columns_order = [plan.slot(i) for i in range(plan.devices)]
 
     def exchange(x, axes):
         return lax.all_to_all(x, axes, split_axis=0, concat_axis=0, tiled=True)
@@ -966,16 +1049,20 @@
     to_b, *field_blocks = prepare_field(plan, field_real, field_imag, place)
     home_b = exchange(to_b, "cross")
     field_blocks = shifted(field_blocks, "wind")
-    *across, kappa, left, right, alpha_a = prepare(plan, zone_map, absorb_index, absorb_table, zone_conductivity, place)
-    along = home_kappa(plan, kappa, *next_prev(right, left, "cross", list(range(cross))), place)
+    *across, kappa, left, right, alpha_a, alpha = prepare(
+        plan, zone_map, absorb_index, absorb_table, zone_conductivity, place
+    )
+    side_alpha, *along = home_kappa(plan, kappa, *next_prev(right, left, "cross", list(range(cross))), alpha, place)
 
     dft = jnp.asarray(dft_matrices())
     tab_a = lambda share: (jnp.asarray(row_blocks(plan.rows, share)), jnp.asarray(row_table(plan.rows)))
+    tab_b_of = lambda length: jnp.asarray(chirp_columns(length, ()))
     tab_b = lambda *shares: jnp.asarray(chirp_columns(plan.cols, shares))
 
     def smooth_a(layer, share, received):
-        heat, left, right = rows_heat(plan, *tab_a(share), received, alpha_a[layer : layer + 1])
-        from_left, from_right = next_prev(right, left, grid_axes, columns_order)
+        heat, from_left, from_right = rows_heat(
+            plan, *tab_a(share), received, alpha_a[layer : layer + 1], tab_b_of(plan.rows), side_alpha[layer]
+        )
         return rows_smooth(plan, heat, from_left, from_right, *kappas, place)
 
     def smooth_b(layer, keep, received):
@@ -983,7 +1070,7 @@
         return cols_smooth(plan, keep, kappa_b, above, below, part, beside, flip(totals), place)
 
     home_b, across = lax.optimization_barrier((home_b, across))
-    sent = cols_send(plan, plan.home_b, False, dft, tab_b(0.5), home_b)
+    sent = cols_send(plan, plan.home_b, False, dft, tab_b(0.5), home_b, True)
     kappa_b, alpha_b = home_rows(plan, shifted(across, "cross"), place)
     above, below = next_prev(kappa_b[-8:], kappa_b[:8], grid_axes, list(range(plan.devices)))
     received, along = lax.optimization_barrier((flip(sent), along))

time: 370 us -> 364 us (0.984)
  starting transfers between devices: 59.1 us -> 48.6 us
  waiting for transfers between devices: 89.3 us -> 97.1 us
  local copies, waits for them, and re-layouts: 18.3 us -> 13.1 us
    all_to_all x5, waiting for transfers between devices: 34.4 us -> 53 us  [exchange(): return lax.all_to_all(x, axes, split_axis=0, concat_axis=0, tiled=True)]
    ppermute x4 -> x2, waiting for transfers between devices: 17.7 us -> 3.41 us  [next_prev(): lax.ppermute(value_up, axes, up)]
    ppermute x4 -> x2, starting transfers between devices: 19 us -> 4.85 us  [next_prev(): lax.ppermute(value_up, axes, up)]
    ppermute x12, waiting for transfers between devices: 31.5 us -> 40.7 us  [shifted(): lax.ppermute(parts[s], axis, [(i, (i + s) % size) for i in range(size)])]
    ppermute x4 -> x2, waiting for transfers between devices: 5.77 us -> 0.01 us  [next_prev(): lax.ppermute(value_down, axes, down)]
    unnamed x76 -> x70, local copies, waits for them, and re-layouts: 17.2 us -> 12 us
    all_to_all x5, starting transfers between devices: 22.4 us -> 26.3 us  [exchange(): return lax.all_to_all(x, axes, split_axis=0, concat_axis=0, tiled=True)]
    ppermute x4 -> x2, starting transfers between devices: 7.78 us -> 4.63 us  [next_prev(): lax.ppermute(value_down, axes, down)]
  transfers between devices with their start and end apart: 25 -> 21, of which waited for: 14 -> 12; matrix products, arithmetic and copies ran while one was open for 0% -> 0% of each run, Pallas kernels for 5% -> 5%
where the time goes in v5:
time: 364 us; the launch traced here: 360 us
  blocking collectives  133 us (37%)
  waiting for transfers between devices  97.1 us (27%)
  Pallas kernels  67.2 us (18%)
  starting transfers between devices  48.6 us (13%)
  local copies, waits for them, and re-layouts  13.1 us (4%)
    all_to_all x6, blocking collectives, exchange(): return lax.all_to_all(x, axes, split_axis=0, concat_axis=0, tiled=True)  133 us
    pallas_call x22, Pallas kernels, run(): pl.pallas_call(body, out_shape=[pltpu.VMEM(o.shape, o.dtype) if i in near...  67.2 us
    all_to_all x5, waiting for transfers between devices, exchange(): return lax.all_to_all(x, axes, split_axis=0, concat_axis=0, tiled=True)  53 us
    ppermute x12, waiting for transfers between devices, shifted(): lax.ppermute(parts[s], axis, [(i, (i + s) % size) for i in range(size)])  40.7 us
    all_to_all x5, starting transfers between devices, exchange(): return lax.all_to_all(x, axes, split_axis=0, concat_axis=0, tiled=True)  26.3 us
    ppermute x12, starting transfers between devices, shifted(): lax.ppermute(parts[s], axis, [(i, (i + s) % size) for i in range(size)])  12.8 us
    unnamed x70, local copies, waits for them, and re-layouts  12 us
  transfers between devices with their start and end apart: 21, of which 12 were waited for; matrix products, arithmetic and copies ran while one was open for 0% of the time, Pallas kernels for 5%

profile of v5, /device:TPU:16, one launch (start us, length us, event | category | flops | bytes accessed | tf_op | source)
XLA Modules:
  0.0 360.1 jit_solution(11510431469526376958)
XLA Ops:
  9.8 11.5 %all-to-all-done.field = f32[4,128,512]{2,1,0:T(8,128)S(1)} async-done(((f32[4,128,512]{2,1,0:T(8,128)}), f32[4,128,512]{2,1,0:T(8,128)S(1)}, u32[]{:S(2)}, u32[]{:S(2)}) %all-to-all-start) | async-done | bytes 1048608 | tf_op jit(solution)/shard_map/all_to_all | solution.py:1044
  21.4 4.5 %shard_map.268 = f32[16,136,128]{2,1,0:T(8,128)} custom-call(bf16[4,256,256]{2,1,0:T(8,128)(2,1)S(1)} %copy-done.1, f32[64,128]{1,0:T(8,128)S(1)} %copy-done.15, f32[4,128,512]{2,1,0:T(8,128)S(1)} %all-to-all-done.field), custom_call_target="tpu_custom_call" | custom-call | tf_op jit(solution)/shard_map/pallas_call | solution.py:353
  25.8 5.2 %all-to-all-start.1 = ((f32[16,136,128]{2,1,0:T(8,128)}), f32[16,136,128]{2,1,0:T(8,128)}, u32[]{:S(2)}, u32[]{:S(2)}) async-start(f32[16,136,128]{2,1,0:T(8,128)} %shard_map.268), calls=%async_computation.1 | async-start | bytes 2228224 | tf_op jit(solution)/shard_map/all_to_all | solution.py:1044
  41.6 27.9 %all-to-all-done.1.received = f32[16,136,128]{2,1,0:T(8,128)} async-done(((f32[16,136,128]{2,1,0:T(8,128)}), f32[16,136,128]{2,1,0:T(8,128)}, u32[]{:S(2)}, u32[]{:S(2)}) %all-to-all-start.1) | async-done | bytes 1114144 | tf_op jit(solution)/shard_map/all_to_all | solution.py:1044
  69.6 10.0 %collective-permute-done.10.refs_3_ = f32[512,128]{1,0:T(8,128)S(1)} collective-permute-done((f32[512,128]{1,0:T(8,128)}, f32[512,128]{1,0:T(8,128)S(1)}, u32[]{:S(2)}, u32[]{:S(2)}) %collective-permute-start.10) | collective-permute-done | bytes 262176 | tf_op jit(solution)/shard_map/ppermute | solution.py:484
  86.3 5.1 %shard_map.270 = (f32[1024,128]{1,0:T(8,128)S(1)}, f32[8,1024]{1,0:T(8,128)S(1)}, f32[8,1024]{1,0:T(8,128)S(1)}) custom-call(bf16[8,2,256,256]{3,2,1,0:T(8,128)(2,1)S(1)} %copy-done, f32[128,128]{1,0:T(8,128)S(1)} %copy-done.8, f32[16,136,128]{2,1,0:T(8,128)} %all-to-all-done.1.received, f32[1,128]{1,0:T(1,128)S(1)} %get-tuple-element.126.alpha, ...), custom_call_target="tpu_custom_call" | custom-call | tf_op jit(solution)/shard_map/pallas_call | solution.py:353
  92.0 4.3 %shard_map.272.screen = f32[1024,128]{1,0:T(8,128)S(1)} custom-call(f32[1024,128]{1,0:T(8,128)S(1)} %get-tuple-element.83.heat, f32[8,1024]{1,0:T(8,128)S(1)} %get-tuple-element.84.from_left, f32[8,1024]{1,0:T(8,128)S(1)} %get-tuple-element.85.from_right, f32[1024,128]{1,0:T(8,128)S(1)} %get-tuple-element.90.kappa, ...), custom_call_target="tpu_custom_call" | custom-call | tf_op jit(solution)/shard_map/pallas_call | solution.py:353
  100.8 7.7 %all-to-all-start.2 = ((f32[16,136,128]{2,1,0:T(8,128)}), f32[16,136,128]{2,1,0:T(8,128)}, u32[]{:S(2)}, u32[]{:S(2)}) async-start(f32[16,136,128]{2,1,0:T(8,128)} %copy-done.6), calls=%async_computation.2 | async-start | bytes 2228224 | tf_op jit(solution)/shard_map/all_to_all | solution.py:1044
  111.5 8.2 %collective-permute-done.refs_1_ = f32[72,512]{1,0:T(8,128)S(1)} collective-permute-done((f32[72,512]{1,0:T(8,128)S(1)}, f32[72,512]{1,0:T(8,128)S(1)}, u32[]{:S(2)}, u32[]{:S(2)}) %collective-permute-start) | collective-permute-done | bytes 147488 | tf_op jit(solution)/shard_map/ppermute | solution.py:484
  135.8 5.3 %shard_map.275 = (f32[64,2048]{1,0:T(8,128)S(1)}, f32[8,2048]{1,0:T(8,128)S(1)}, f32[16,16,128]{2,1,0:T(8,128)S(1)}) custom-call(bf16[4,256,256]{2,1,0:T(8,128)(2,1)S(1)} %copy-done.1, f32[64,128]{1,0:T(8,128)S(1)} %copy-done.15, f32[16,136,128]{2,1,0:T(8,128)} %all-to-all-done.2.received, f32[8,2048]{1,0:T(8,128)S(1)} %get-tuple-element.100.absorption), custom_call_target="tpu_custom_call" | custom-call | tf_op jit(solution)/shard_map/pallas_call | solution.py:353
  141.2 11.1 %all_to_all.55.refs_0_ = f32[16,16,128]{2,1,0:T(8,128)S(1)} all-to-all(f32[16,16,128]{2,1,0:T(8,128)S(1)} %get-tuple-element.103), channel_id=1, replica_groups=mesh['beams'=2,'wind'=4,'cross'=4] {'wind','cross'}, dimensions={0} | all-to-all | bytes 262144 | tf_op jit(solution)/shard_map/all_to_all | solution.py:1044
  155.6 5.5 %shard_map.277 = (f32[16,136,128]{2,1,0:T(8,128)S(1)}, f32[16,128,128]{2,1,0:T(8,128)S(1)}) custom-call(bf16[4,256,256]{2,1,0:T(8,128)(2,1)S(1)} %copy-done.1, f32[96,128]{1,0:T(8,128)S(1)} %copy-done.20, f32[64,2048]{1,0:T(8,128)S(1)} %shard_map.276.screen, f32[4,128,512]{2,1,0:T(8,128)S(1)} %copy-done.3), custom_call_target="tpu_custom_call" | custom-call | tf_op jit(solution)/shard_map/pallas_call | solution.py:353
  161.1 32.2 %all_to_all.56.received = f32[16,136,128]{2,1,0:T(8,128)} all-to-all(f32[16,136,128]{2,1,0:T(8,128)S(1)} %get-tuple-element.105), channel_id=1, replica_groups=mesh['beams'=2,'wind'=4,'cross'=4] {'wind','cross'}, dimensions={0} | all-to-all | bytes 2228224 | tf_op jit(solution)/shard_map/all_to_all | solution.py:1044
  193.3 6.2 %all-to-all-start.4 = ((f32[16,128,128]{2,1,0:T(8,128)}), f32[16,128,128]{2,1,0:T(8,128)}, u32[]{:S(2)}, u32[]{:S(2)}) async-start(f32[16,128,128]{2,1,0:T(8,128)} %copy-done.14), calls=%async_computation.4 | async-start | bytes 2097152 | tf_op jit(solution)/shard_map/all_to_all | solution.py:1044
  202.3 3.8 %shard_map.278 = (f32[1024,128]{1,0:T(8,128)S(1)}, f32[8,1024]{1,0:T(8,128)S(1)}, f32[8,1024]{1,0:T(8,128)S(1)}) custom-call(bf16[8,2,256,256]{3,2,1,0:T(8,128)(2,1)S(1)} %copy-done.11, f32[128,128]{1,0:T(8,128)S(1)} %copy-done.8, f32[16,136,128]{2,1,0:T(8,128)S(1)} %copy-done.7, f32[1,128]{1,0:T(1,128)S(1)} %get-tuple-element.125.alpha, ...), custom_call_target="tpu_custom_call" | custom-call | tf_op jit(solution)/shard_map/pallas_call | solution.py:353
  206.1 4.3 %shard_map.279.screen = f32[1024,128]{1,0:T(8,128)S(1)} custom-call(f32[1024,128]{1,0:T(8,128)S(1)} %get-tuple-element.106.heat, f32[8,1024]{1,0:T(8,128)S(1)} %get-tuple-element.107.from_left, f32[8,1024]{1,0:T(8,128)S(1)} %get-tuple-element.108.from_right, f32[1024,128]{1,0:T(8,128)S(1)} %copy-done.13, f32[8,1024]{1,0:T(8,128)S(1)} %get-tuple-element.91.kappa_left, ...), custom_call_target="tpu_custom_call" | custom-call | tf_op jit(solution)/shard_map/pallas_call | solution.py:353
  211.2 13.5 %all-to-all-done.4.field = f32[16,128,128]{2,1,0:T(8,128)} async-done(((f32[16,128,128]{2,1,0:T(8,128)}), f32[16,128,128]{2,1,0:T(8,128)}, u32[]{:S(2)}, u32[]{:S(2)}) %all-to-all-start.4) | async-done | bytes 1048608 | tf_op jit(solution)/shard_map/all_to_all | solution.py:1044
  232.3 30.8 %all_to_all.57.received = f32[16,136,128]{2,1,0:T(8,128)S(1)} all-to-all(f32[16,136,128]{2,1,0:T(8,128)S(1)} %shard_map.281), channel_id=1, replica_groups=mesh['beams'=2,'wind'=4,'cross'=4] {'wind','cross'}, dimensions={0} | all-to-all | bytes 2228224 | tf_op jit(solution)/shard_map/all_to_all | solution.py:1044
  263.2 4.1 %shard_map.282 = (f32[64,2048]{1,0:T(8,128)S(1)}, f32[8,2048]{1,0:T(8,128)S(1)}, f32[16,16,128]{2,1,0:T(8,128)S(1)}) custom-call(bf16[4,256,256]{2,1,0:T(8,128)(2,1)S(1)} %copy-done.1, f32[64,128]{1,0:T(8,128)S(1)} %copy-done.15, f32[16,136,128]{2,1,0:T(8,128)S(1)} %all_to_all.57.received, f32[8,2048]{1,0:T(8,128)S(1)} %get-tuple-element.100.absorption), custom_call_target="tpu_custom_call" | custom-call | tf_op jit(solution)/shard_map/pallas_call | solution.py:353
  267.2 10.3 %all_to_all.58.refs_0_ = f32[16,16,128]{2,1,0:T(8,128)S(1)} all-to-all(f32[16,16,128]{2,1,0:T(8,128)S(1)} %get-tuple-element.113), channel_id=1, replica_groups=mesh['beams'=2,'wind'=4,'cross'=4] {'wind','cross'}, dimensions={0} | all-to-all | bytes 262144 | tf_op jit(solution)/shard_map/all_to_all | solution.py:1044
  280.9 19.1 %all_to_all.59 = f32[16,64,128]{2,1,0:T(8,128)S(1)} all-to-all(f32[16,64,128]{2,1,0:T(8,128)S(1)} %get-tuple-element.114), channel_id=1, replica_groups=mesh['beams'=2,'wind'=4,'cross'=4] {'wind','cross'}, dimensions={0} | all-to-all | bytes 1048576 | tf_op jit(solution)/shard_map/all_to_all | solution.py:1044
  302.6 29.4 %all_to_all.60.field = f32[16,128,128]{2,1,0:T(8,128)S(1)} all-to-all(f32[16,128,128]{2,1,0:T(8,128)S(1)} %shard_map.284), channel_id=1, replica_groups=mesh['beams'=2,'wind'=4,'cross'=4] {'wind','cross'}, dimensions={0} | all-to-all | bytes 2097152 | tf_op jit(solution)/shard_map/all_to_all | solution.py:1044
  332.1 4.1 %shard_map.285 = f32[4,128,512]{2,1,0:T(8,128)} custom-call(bf16[4,256,256]{2,1,0:T(8,128)(2,1)S(1)} %copy-done.1, f32[64,128]{1,0:T(8,128)S(1)} %copy-done.22, f32[16,128,128]{2,1,0:T(8,128)S(1)} %all_to_all.60.field), custom_call_target="tpu_custom_call" | custom-call | tf_op jit(solution)/shard_map/pallas_call | solution.py:353
  343.2 13.2 %collective-permute-done.13.refs_1_ = f32[64,512]{1,0:T(8,128)S(1)} collective-permute-done((f32[64,512]{1,0:T(8,128)S(1)}, f32[64,512]{1,0:T(8,128)S(1)}, u32[]{:S(2)}, u32[]{:S(2)}) %collective-permute-start.13) | collective-permute-done | bytes 131104 | tf_op jit(solution)/shard_map/ppermute | solution.py:484
  (121 shorter events, 81.7 us)
Async XLA Ops:
  3.3 18.1 %all-to-all-start = ((f32[4,128,512]{2,1,0:T(8,128)}), f32[4,128,512]{2,1,0:T(8,128)S(1)}, u32[]{:S(2)}, u32[]{:S(2)}) async-start(f32[4,128,512]{2,1,0:T(8,128)} %get-tuple-element.61), calls=%async_computation | async-start | bytes 2097152 | tf_op jit(solution)/shard_map/all_to_all | solution.py:1044
  25.8 43.7 %all-to-all-start.1 = ((f32[16,136,128]{2,1,0:T(8,128)}), f32[16,136,128]{2,1,0:T(8,128)}, u32[]{:S(2)}, u32[]{:S(2)}) async-start(f32[16,136,128]{2,1,0:T(8,128)} %shard_map.268), calls=%async_computation.1 | async-start | bytes 2228224 | tf_op jit(solution)/shard_map/all_to_all | solution.py:1044
  31.0 48.5 %collective-permute-start.10 = (f32[512,128]{1,0:T(8,128)}, f32[512,128]{1,0:T(8,128)S(1)}, u32[]{:S(2)}, u32[]{:S(2)}) collective-permute-start(f32[512,128]{1,0:T(8,128)} %get-tuple-element.96), channel_id=1, source_target_pairs={{0,12},{4,0},{8,4},{12,8},{1,13},{5,1},{9,5},{13,9},{2,14},{6,2},{... | collective-permute-start | bytes 786440 | tf_op jit(solution)/shard_map/ppermute | solution.py:484
  31.6 6.4 %collective-permute-start.3 = (f32[16,256]{1,0:T(8,128)S(1)}, f32[16,256]{1,0:T(8,128)S(1)}, u32[]{:S(2)}, u32[]{:S(2)}) collective-permute-start(f32[16,256]{1,0:T(8,128)S(1)} %get-tuple-element.73), channel_id=1, source_target_pairs={{0,1},{1,2},{2,3},{4,5},{5,6},{6,7},{8,9},{9,10},{10,11},{12,13},{... | collective-permute-start | bytes 49160 | tf_op jit(solution)/shard_map/ppermute | solution.py:845
  33.3 4.7 %collective-permute-start.4 = (f32[16,256]{1,0:T(8,128)S(1)}, f32[16,256]{1,0:T(8,128)S(1)}, u32[]{:S(2)}, u32[]{:S(2)}) collective-permute-start(f32[16,256]{1,0:T(8,128)S(1)} %get-tuple-element.74), channel_id=1, source_target_pairs={{1,0},{2,1},{3,2},{5,4},{6,5},{7,6},{9,8},{10,9},{11,10},{13,12},{... | collective-permute-start | bytes 49160 | tf_op jit(solution)/shard_map/ppermute | solution.py:845
  34.6 47.3 %collective-permute-start.8 = (f32[512,128]{1,0:T(8,128)}, f32[512,128]{1,0:T(8,128)S(1)}, u32[]{:S(2)}, u32[]{:S(2)}) collective-permute-start(f32[512,128]{1,0:T(8,128)} %get-tuple-element.94), channel_id=1, source_target_pairs={{0,4},{4,8},{8,12},{12,0},{1,5},{5,9},{9,13},{13,1},{2,6},{6,10},{... | collective-permute-start | bytes 786440 | tf_op jit(solution)/shard_map/ppermute | solution.py:484
  36.2 49.1 %collective-permute-start.9 = (f32[512,128]{1,0:T(8,128)}, f32[512,128]{1,0:T(8,128)}, u32[]{:S(2)}, u32[]{:S(2)}) collective-permute-start(f32[512,128]{1,0:T(8,128)} %get-tuple-element.95), channel_id=1, source_target_pairs={{0,8},{4,12},{8,0},{12,4},{1,9},{5,13},{9,1},{13,5},{2,10},{6,14},... | collective-permute-start | bytes 786440 | tf_op jit(solution)/shard_map/ppermute | solution.py:484
  38.1 48.2 %copy-start.8 = (f32[128,128]{1,0:T(8,128)S(1)}, f32[128,128]{1,0:T(8,128)}, u32[]{:S(2)}) copy-start(f32[128,128]{1,0:T(8,128)} %constant.28.clone.table) | copy-start | bytes 196612
  41.6 44.7 %copy-start = (bf16[8,2,256,256]{3,2,1,0:T(8,128)(2,1)S(1)}, bf16[8,2,256,256]{3,2,1,0:T(8,128)(2,1)}, u32[]{:S(2)}) copy-start(bf16[8,2,256,256]{3,2,1,0:T(8,128)(2,1)} %constant.27.clone.matrices.dft) | copy-start | bytes 6291460
  41.6 44.7 %copy-start.21 = (f32[16,128]{1,0:T(8,128)S(1)}, f32[16,128]{1,0:T(8,128)}, u32[]{:S(2)}) copy-start(f32[16,128]{1,0:T(8,128)} %constant.29.clone.side_table) | copy-start | bytes 24580
  69.5 21.9 %collective-permute-start.5 = (f32[288,128]{1,0:T(8,128)}, f32[288,128]{1,0:T(8,128)S(1)}, u32[]{:S(2)}, u32[]{:S(2)}) collective-permute-start(f32[288,128]{1,0:T(8,128)} %copy-done.34), channel_id=1, source_target_pairs={{0,4},{4,8},{8,12},{12,0},{1,5},{5,9},{9,13},{13,1},{2,6},{6,10},{... | collective-permute-start | bytes 442376 | tf_op jit(solution)/shard_map/ppermute | solution.py:484
  69.5 21.9 %collective-permute-start.6 = (f32[288,128]{1,0:T(8,128)}, f32[288,128]{1,0:T(8,128)S(1)}, u32[]{:S(2)}, u32[]{:S(2)}) collective-permute-start(f32[288,128]{1,0:T(8,128)} %copy-done.33), channel_id=1, source_target_pairs={{0,8},{4,12},{8,0},{12,4},{1,9},{5,13},{9,1},{13,5},{2,10},{6,14},... | collective-permute-start | bytes 442376 | tf_op jit(solution)/shard_map/ppermute | solution.py:484
  79.6 11.9 %collective-permute-start.7 = (f32[288,128]{1,0:T(8,128)}, f32[288,128]{1,0:T(8,128)S(1)}, u32[]{:S(2)}, u32[]{:S(2)}) collective-permute-start(f32[288,128]{1,0:T(8,128)} %copy-done.32), channel_id=1, source_target_pairs={{0,12},{4,0},{8,4},{12,8},{1,13},{5,1},{9,5},{13,9},{2,14},{6,2},{... | collective-permute-start | bytes 442376 | tf_op jit(solution)/shard_map/ppermute | solution.py:484
  100.8 35.1 %all-to-all-start.2 = ((f32[16,136,128]{2,1,0:T(8,128)}), f32[16,136,128]{2,1,0:T(8,128)}, u32[]{:S(2)}, u32[]{:S(2)}) async-start(f32[16,136,128]{2,1,0:T(8,128)} %copy-done.6), calls=%async_computation.2 | async-start | bytes 2228224 | tf_op jit(solution)/shard_map/all_to_all | solution.py:1044
  108.5 11.2 %collective-permute-start = (f32[72,512]{1,0:T(8,128)S(1)}, f32[72,512]{1,0:T(8,128)S(1)}, u32[]{:S(2)}, u32[]{:S(2)}) collective-permute-start(f32[72,512]{1,0:T(8,128)S(1)} %copy-done.31), channel_id=1, source_target_pairs={{0,1},{1,2},{2,3},{3,0},{4,5},{5,6},{6,7},{7,4},{8,9},{9,10},{10,1... | collective-permute-start | bytes 442376 | tf_op jit(solution)/shard_map/ppermute | solution.py:484
  108.7 12.2 %collective-permute-start.1 = (f32[72,512]{1,0:T(8,128)S(1)}, f32[72,512]{1,0:T(8,128)S(1)}, u32[]{:S(2)}, u32[]{:S(2)}) collective-permute-start(f32[72,512]{1,0:T(8,128)S(1)} %copy-done.29), channel_id=1, source_target_pairs={{0,2},{1,3},{2,0},{3,1},{4,6},{5,7},{6,4},{7,5},{8,10},{9,11},{10,... | collective-permute-start | bytes 442376 | tf_op jit(solution)/shard_map/ppermute | solution.py:484
  110.2 14.3 %collective-permute-start.2 = (f32[72,512]{1,0:T(8,128)S(1)}, f32[72,512]{1,0:T(8,128)S(1)}, u32[]{:S(2)}, u32[]{:S(2)}) collective-permute-start(f32[72,512]{1,0:T(8,128)S(1)} %copy-done.27), channel_id=1, source_target_pairs={{0,3},{1,0},{2,1},{3,2},{4,7},{5,4},{6,5},{7,6},{8,11},{9,8},{10,9... | collective-permute-start | bytes 442376 | tf_op jit(solution)/shard_map/ppermute | solution.py:484
  126.0 9.9 %collective-permute-start.11 = (f32[8,2048]{1,0:T(8,128)S(1)}, f32[8,2048]{1,0:T(8,128)S(1)}, u32[]{:S(2)}, u32[]{:S(2)}) collective-permute-start(f32[8,2048]{1,0:T(8,128)S(1)} %get-tuple-element.122), channel_id=1, source_target_pairs={{0,1},{1,2},{2,3},{3,4},{4,5},{5,6},{6,7},{7,8},{8,9},{9,10},{10,1... | collective-permute-start | bytes 196616 | tf_op jit(solution)/shard_map/ppermute | solution.py:845
  129.1 6.8 %collective-permute-start.12 = (f32[8,2048]{1,0:T(8,128)S(1)}, f32[8,2048]{1,0:T(8,128)S(1)}, u32[]{:S(2)}, u32[]{:S(2)}) collective-permute-start(f32[8,2048]{1,0:T(8,128)S(1)} %get-tuple-element.121), channel_id=1, source_target_pairs={{1,0},{2,1},{3,2},{4,3},{5,4},{6,5},{7,6},{8,7},{9,8},{10,9},{11,1... | collective-permute-start | bytes 196616 | tf_op jit(solution)/shard_map/ppermute | solution.py:845
  193.3 31.4 %all-to-all-start.4 = ((f32[16,128,128]{2,1,0:T(8,128)}), f32[16,128,128]{2,1,0:T(8,128)}, u32[]{:S(2)}, u32[]{:S(2)}) async-start(f32[16,128,128]{2,1,0:T(8,128)} %copy-done.14), calls=%async_computation.4 | async-start | bytes 2097152 | tf_op jit(solution)/shard_map/all_to_all | solution.py:1044
  336.2 22.8 %all-to-all-start.10 = ((f32[4,128,512]{2,1,0:T(8,128)}), f32[4,128,512]{2,1,0:T(8,128)S(1)}, u32[]{:S(2)}, u32[]{:S(2)}) async-start(f32[4,128,512]{2,1,0:T(8,128)} %shard_map.285), calls=%async_computation.10 | async-start | bytes 2097152 | tf_op jit(solution)/shard_map/all_to_all | solution.py:1044
  339.7 16.6 %collective-permute-start.13 = (f32[64,512]{1,0:T(8,128)S(1)}, f32[64,512]{1,0:T(8,128)S(1)}, u32[]{:S(2)}, u32[]{:S(2)}) collective-permute-start(f32[64,512]{1,0:T(8,128)S(1)} %get-tuple-element.116), channel_id=1, source_target_pairs={{0,1},{1,2},{2,3},{3,0},{4,5},{5,6},{6,7},{7,4},{8,9},{9,10},{10,1... | collective-permute-start | bytes 393224 | tf_op jit(solution)/shard_map/ppermute | solution.py:484
  340.2 17.3 %collective-permute-start.14 = (f32[64,512]{1,0:T(8,128)S(1)}, f32[64,512]{1,0:T(8,128)S(1)}, u32[]{:S(2)}, u32[]{:S(2)}) collective-permute-start(f32[64,512]{1,0:T(8,128)S(1)} %get-tuple-element.117), channel_id=1, source_target_pairs={{0,2},{1,3},{2,0},{3,1},{4,6},{5,7},{6,4},{7,5},{8,10},{9,11},{10,... | collective-permute-start | bytes 393224 | tf_op jit(solution)/shard_map/ppermute | solution.py:484
  341.8 15.8 %collective-permute-start.15 = (f32[64,512]{1,0:T(8,128)S(1)}, f32[64,512]{1,0:T(8,128)S(1)}, u32[]{:S(2)}, u32[]{:S(2)}) collective-permute-start(f32[64,512]{1,0:T(8,128)S(1)} %get-tuple-element.118), channel_id=1, source_target_pairs={{0,3},{1,0},{2,1},{3,2},{4,7},{5,4},{6,5},{7,6},{8,11},{9,8},{10,9... | collective-permute-start | bytes 393224 | tf_op jit(solution)/shard_map/ppermute | solution.py:484
  (32 other events, 246.0 us)

commit v6 on v5

--- a/solution.py
+++ b/solution.py
@@ -345,14 +345,17 @@
         ]
 
 
-def call(body, outs, scratch, near=(), near_outs=(), far=()):
+def call(body, outs, scratch, near=(), near_outs=(), far=(), far_outs=()):
     def run(*args):
         specs = [SCALAR if a.size <= 16 else WHOLE for a in args]
         spaces = [pltpu.VMEM if i in near else pltpu.HBM if i in far else None for i in range(len(args))]
         args = [pltpu.with_memory_space_constraint(a, space) if space else a for a, space in zip(args, spaces)]
         return pl.pallas_call(
             body,
-            out_shape=[pltpu.VMEM(o.shape, o.dtype) if i in near_outs else o for i, o in enumerate(outs)],
+            out_shape=[
+                pltpu.VMEM(o.shape, o.dtype) if i in near_outs else pltpu.HBM(o.shape, o.dtype) if i in far_outs else o
+                for i, o in enumerate(outs)
+            ],
             in_specs=specs,
             out_specs=[WHOLE] * len(outs),
             scratch_shapes=scratch,
@@ -696,7 +699,7 @@
         outs += [jax.ShapeDtypeStruct((h, plan.cols_here), F32)] * plan.cross
     else:
         outs = [jax.ShapeDtypeStruct(flat, F32)]
-    return call(body, outs, [tall] * 3 + [pltpu.VMEM(flat, F32)], (), () if keep else (0,))(
+    return call(body, outs, [tall] * 3 + [pltpu.VMEM(flat, F32)], (), () if keep else (0,), (), range(len(outs)) if keep else ())(
         kappa, above, below, part, beside, *rest
     )
 
@@ -781,12 +784,14 @@
     return call(body, [out], plan.work_a(), (0, 1, 2), (0,))(dft, table, screen, field)[0]
 
 
-def rows_smooth(plan, heat, from_left, from_right, kappa, kappa_left, kappa_right, me):
+def rows_smooth(plan, heat, from_left, from_right, kappa, kappa_left, kappa_right, me, *ahead):
     width = plan.width
     PAD = 8
     step_rows = 32
 
-    def body(heat, from_left, from_right, kappa, kappa_left, kappa_right, me, screen, h0, h1, kx):
+    def body(heat, from_left, from_right, kappa, kappa_left, kappa_right, me, *refs):
+        screen, h0, h1, kx = refs[-4:]
+
         place = me[1] * plan.wind + plan.local(me[0], me[1])
         zeros = jnp.zeros((PAD, 2 * width), F32)
         for ref in (h0, h1, kx):
@@ -836,7 +841,9 @@
 
     tall = pltpu.VMEM((plan.rows + 2 * PAD, 2 * width), F32)
     outs = [jax.ShapeDtypeStruct((plan.rows, width), F32)]
-    return call(body, outs, [tall] * 3, (), (0,))(heat, from_left, from_right, kappa, kappa_left, kappa_right, me)[0]
+    return call(body, outs, [tall] * 3, range(7, 7 + len(ahead)), (0,))(
+        heat, from_left, from_right, kappa, kappa_left, kappa_right, me, *ahead
+    )[0]
 
 
 def next_prev(value_up, value_down, axes, order):
@@ -1059,11 +1066,11 @@
     tab_b_of = lambda length: jnp.asarray(chirp_columns(length, ()))
     tab_b = lambda *shares: jnp.asarray(chirp_columns(plan.cols, shares))
 
-    def smooth_a(layer, share, received):
+    def smooth_a(layer, share, received, *ahead):
         heat, from_left, from_right = rows_heat(
             plan, *tab_a(share), received, alpha_a[layer : layer + 1], tab_b_of(plan.rows), side_alpha[layer]
         )
-        return rows_smooth(plan, heat, from_left, from_right, *kappas, place)
+        return rows_smooth(plan, heat, from_left, from_right, *kappas, place, *ahead)
 
     def smooth_b(layer, keep, received):
         part, beside, totals = cols_heat(plan, layer, plan.devices, dft, tab_b(0.5), received, alpha_b)
@@ -1084,14 +1091,15 @@
     sent_middle, sent_field = cols_turn(plan, plan.home_b, 2, dft, tab_b(1.5, 1.0), screen, home_b)
     middle = flip(sent_middle)
     field = flip(sent_field)
-    screen = smooth_a(1, 1.5, middle)
+    whole_share = tab_a(1.0)
+    screen = smooth_a(1, 1.5, middle, whole_share[0])
     field, screen = lax.optimization_barrier((field, screen))
-    field = rows_field(plan, plan.flip_a, *tab_a(1.0), field)
+    field = rows_field(plan, plan.flip_a, *whole_share, field)
     sent = rows_turn(plan, plan.flip_a, True, *tab_a(0.5), screen, field)
     screen, *home_parts = smooth_b(1, True, flip(sent))
     home_parts = shifted(home_parts, "cross")
     screen = flip(screen).reshape(plan.rows, plan.width)
-    sent = rows_turn(plan, plan.flip_a, False, *tab_a(1.0), screen, field)
+    sent = rows_turn(plan, plan.flip_a, False, *whole_share, screen, field)
     back = cols_send(plan, plan.flip_b, True, dft, tab_b(1.0), flip(sent))
     screen = home_screen(plan, home_parts, place)
     back = exchange(back, "cross")

time: 364 us -> 362 us (level)
    unnamed x70 -> x76, local copies, waits for them, and re-layouts: 12 us -> 9.51 us
where the time goes in v6:
time: 362 us; the launch traced here: 359 us
  blocking collectives  133 us (37%)
  waiting for transfers between devices  98.1 us (27%)
  Pallas kernels  67.7 us (19%)
  starting transfers between devices  48.1 us (13%)
  local copies, waits for them, and re-layouts  10.6 us (3%)
    all_to_all x6, blocking collectives, exchange(): return lax.all_to_all(x, axes, split_axis=0, concat_axis=0, tiled=True)  133 us
    pallas_call x22, Pallas kernels, run(): pl.pallas_call(body, out_shape=[pltpu.VMEM(o.shape, o.dtype) if i in near...  67.7 us
    all_to_all x5, waiting for transfers between devices, exchange(): return lax.all_to_all(x, axes, split_axis=0, concat_axis=0, tiled=True)  53 us
    ppermute x12, waiting for transfers between devices, shifted(): lax.ppermute(parts[s], axis, [(i, (i + s) % size) for i in range(size)])  39.5 us
    all_to_all x5, starting transfers between devices, exchange(): return lax.all_to_all(x, axes, split_axis=0, concat_axis=0, tiled=True)  25.9 us
    ppermute x12, starting transfers between devices, shifted(): lax.ppermute(parts[s], axis, [(i, (i + s) % size) for i in range(size)])  12.8 us
    unnamed x76, local copies, waits for them, and re-layouts  9.51 us
  transfers between devices with their start and end apart: 21, of which 12 were waited for; matrix products, arithmetic and copies ran while one was open for 0% of the time, Pallas kernels for 5%

profile of v6, /device:TPU:16, one launch (start us, length us, event | category | flops | bytes accessed | tf_op | source)
XLA Modules:
  0.0 358.5 jit_solution(6200786114281753271)
XLA Ops:
  9.8 11.5 %all-to-all-done.field = f32[4,128,512]{2,1,0:T(8,128)S(1)} async-done(((f32[4,128,512]{2,1,0:T(8,128)}), f32[4,128,512]{2,1,0:T(8,128)S(1)}, u32[]{:S(2)}, u32[]{:S(2)}) %all-to-all-start) | async-done | bytes 1048608 | tf_op jit(solution)/shard_map/all_to_all | solution.py:1051
  21.4 4.5 %shard_map.250 = f32[16,136,128]{2,1,0:T(8,128)} custom-call(bf16[4,256,256]{2,1,0:T(8,128)(2,1)S(1)} %copy-done.3, f32[64,128]{1,0:T(8,128)S(1)} %copy-done.14, f32[4,128,512]{2,1,0:T(8,128)S(1)} %all-to-all-done.field), custom_call_target="tpu_custom_call" | custom-call | tf_op jit(solution)/shard_map/pallas_call | solution.py:353
  25.8 5.2 %all-to-all-start.1 = ((f32[16,136,128]{2,1,0:T(8,128)}), f32[16,136,128]{2,1,0:T(8,128)}, u32[]{:S(2)}, u32[]{:S(2)}) async-start(f32[16,136,128]{2,1,0:T(8,128)} %shard_map.250), calls=%async_computation.1 | async-start | bytes 2228224 | tf_op jit(solution)/shard_map/all_to_all | solution.py:1051
  41.6 28.0 %all-to-all-done.1.received = f32[16,136,128]{2,1,0:T(8,128)} async-done(((f32[16,136,128]{2,1,0:T(8,128)}), f32[16,136,128]{2,1,0:T(8,128)}, u32[]{:S(2)}, u32[]{:S(2)}) %all-to-all-start.1) | async-done | bytes 1114144 | tf_op jit(solution)/shard_map/all_to_all | solution.py:1051
  69.6 10.0 %collective-permute-done.10.refs_3_ = f32[512,128]{1,0:T(8,128)S(1)} collective-permute-done((f32[512,128]{1,0:T(8,128)}, f32[512,128]{1,0:T(8,128)S(1)}, u32[]{:S(2)}, u32[]{:S(2)}) %collective-permute-start.10) | collective-permute-done | bytes 262176 | tf_op jit(solution)/shard_map/ppermute | solution.py:487
  86.3 5.1 %shard_map.252 = (f32[1024,128]{1,0:T(8,128)S(1)}, f32[8,1024]{1,0:T(8,128)S(1)}, f32[8,1024]{1,0:T(8,128)S(1)}) custom-call(bf16[8,2,256,256]{3,2,1,0:T(8,128)(2,1)S(1)} %copy-done.1, f32[128,128]{1,0:T(8,128)S(1)} %copy-done.8, f32[16,136,128]{2,1,0:T(8,128)} %all-to-all-done.1.received, f32[1,128]{1,0:T(1,128)S(1)} %get-tuple-element.126.alpha, ...), custom_call_target="tpu_custom_call" | custom-call | tf_op jit(solution)/shard_map/pallas_call | solution.py:353
  92.1 4.3 %shard_map.254.screen = f32[1024,128]{1,0:T(8,128)S(1)} custom-call(f32[1024,128]{1,0:T(8,128)S(1)} %get-tuple-element.83.heat, f32[8,1024]{1,0:T(8,128)S(1)} %get-tuple-element.84.from_left, f32[8,1024]{1,0:T(8,128)S(1)} %get-tuple-element.85.from_right, f32[1024,128]{1,0:T(8,128)S(1)} %get-tuple-element.90.kappa, ...), custom_call_target="tpu_custom_call" | custom-call | tf_op jit(solution)/shard_map/pallas_call | solution.py:353
  100.8 7.1 %all-to-all-start.2 = ((f32[16,136,128]{2,1,0:T(8,128)}), f32[16,136,128]{2,1,0:T(8,128)S(1)}, u32[]{:S(2)}, u32[]{:S(2)}) async-start(f32[16,136,128]{2,1,0:T(8,128)} %copy-done.6), calls=%async_computation.2 | async-start | bytes 2228224 | tf_op jit(solution)/shard_map/all_to_all | solution.py:1051
  110.9 8.2 %collective-permute-done.refs_1_ = f32[72,512]{1,0:T(8,128)S(1)} collective-permute-done((f32[72,512]{1,0:T(8,128)S(1)}, f32[72,512]{1,0:T(8,128)S(1)}, u32[]{:S(2)}, u32[]{:S(2)}) %collective-permute-start) | collective-permute-done | bytes 147488 | tf_op jit(solution)/shard_map/ppermute | solution.py:487
  123.3 4.2 %collective-permute-start.11 = (f32[8,2048]{1,0:T(8,128)S(1)}, f32[8,2048]{1,0:T(8,128)S(1)}, u32[]{:S(2)}, u32[]{:S(2)}) collective-permute-start(f32[8,2048]{1,0:T(8,128)S(1)} %get-tuple-element.122), channel_id=1, source_target_pairs={{0,1},{1,2},{2,3},{3,4},{4,5},{5,6},{6,7},{7,8},{8,9},{9,10},{10,1... | collective-permute-start | bytes 196616 | tf_op jit(solution)/shard_map/ppermute | solution.py:852
  129.8 5.5 %collective-permute-done.11.above = f32[8,2048]{1,0:T(8,128)S(1)} collective-permute-done((f32[8,2048]{1,0:T(8,128)S(1)}, f32[8,2048]{1,0:T(8,128)S(1)}, u32[]{:S(2)}, u32[]{:S(2)}) %collective-permute-start.11) | collective-permute-done | bytes 65568 | tf_op jit(solution)/shard_map/ppermute | solution.py:852
  139.4 10.1 %all_to_all.55.refs_0_ = f32[16,16,128]{2,1,0:T(8,128)S(1)} all-to-all(f32[16,16,128]{2,1,0:T(8,128)S(1)} %get-tuple-element.103), channel_id=1, replica_groups=mesh['beams'=2,'wind'=4,'cross'=4] {'wind','cross'}, dimensions={0} | all-to-all | bytes 262144 | tf_op jit(solution)/shard_map/all_to_all | solution.py:1051
  152.9 6.2 %shard_map.259 = (f32[16,136,128]{2,1,0:T(8,128)S(1)}, f32[16,128,128]{2,1,0:T(8,128)}) custom-call(bf16[4,256,256]{2,1,0:T(8,128)(2,1)S(1)} %copy-done.3, f32[96,128]{1,0:T(8,128)S(1)} %copy-done.20, f32[64,2048]{1,0:T(8,128)S(1)} %shard_map.258.screen, f32[4,128,512]{2,1,0:T(8,128)S(1)} %copy-done.5), custom_call_target="tpu_custom_call" | custom-call | tf_op jit(solution)/shard_map/pallas_call | solution.py:353
  159.0 32.1 %all_to_all.56.received = f32[16,136,128]{2,1,0:T(8,128)} all-to-all(f32[16,136,128]{2,1,0:T(8,128)S(1)} %get-tuple-element.105), channel_id=1, replica_groups=mesh['beams'=2,'wind'=4,'cross'=4] {'wind','cross'}, dimensions={0} | all-to-all | bytes 2228224 | tf_op jit(solution)/shard_map/all_to_all | solution.py:1051
  191.2 6.2 %all-to-all-start.4 = ((f32[16,128,128]{2,1,0:T(8,128)}), f32[16,128,128]{2,1,0:T(8,128)}, u32[]{:S(2)}, u32[]{:S(2)}) async-start(f32[16,128,128]{2,1,0:T(8,128)} %get-tuple-element.104), calls=%async_computation.4 | async-start | bytes 2097152 | tf_op jit(solution)/shard_map/all_to_all | solution.py:1051
  204.0 4.3 %shard_map.261.screen = f32[1024,128]{1,0:T(8,128)S(1)} custom-call(f32[1024,128]{1,0:T(8,128)S(1)} %get-tuple-element.106.heat, f32[8,1024]{1,0:T(8,128)S(1)} %get-tuple-element.107.from_left, f32[8,1024]{1,0:T(8,128)S(1)} %get-tuple-element.108.from_right, f32[1024,128]{1,0:T(8,128)S(1)} %copy-done.13, f32[8,1024]{1,0:T(8,128)S(1)} %get-tuple-element.91.kappa_left, ...), custom_call_target="tpu_custom_call" | custom-call | tf_op jit(solution)/shard_map/pallas_call | solution.py:353
  209.1 13.5 %all-to-all-done.4.field = f32[16,128,128]{2,1,0:T(8,128)} async-done(((f32[16,128,128]{2,1,0:T(8,128)}), f32[16,128,128]{2,1,0:T(8,128)}, u32[]{:S(2)}, u32[]{:S(2)}) %all-to-all-start.4) | async-done | bytes 1048608 | tf_op jit(solution)/shard_map/all_to_all | solution.py:1051
  228.8 30.8 %all_to_all.57.received = f32[16,136,128]{2,1,0:T(8,128)S(1)} all-to-all(f32[16,136,128]{2,1,0:T(8,128)S(1)} %shard_map.263), channel_id=1, replica_groups=mesh['beams'=2,'wind'=4,'cross'=4] {'wind','cross'}, dimensions={0} | all-to-all | bytes 2228224 | tf_op jit(solution)/shard_map/all_to_all | solution.py:1051
  263.7 10.3 %all_to_all.58.refs_0_ = f32[16,16,128]{2,1,0:T(8,128)S(1)} all-to-all(f32[16,16,128]{2,1,0:T(8,128)S(1)} %get-tuple-element.113), channel_id=1, replica_groups=mesh['beams'=2,'wind'=4,'cross'=4] {'wind','cross'}, dimensions={0} | all-to-all | bytes 262144 | tf_op jit(solution)/shard_map/all_to_all | solution.py:1051
  274.0 4.3 %shard_map.265 = (f32[16,64,128]{2,1,0:T(8,128)}, f32[64,512]{1,0:T(8,128)}, f32[64,512]{1,0:T(8,128)}, f32[64,512]{1,0:T(8,128)}, f32[64,512]{1,0:T(8,128)}) custom-call(f32[64,2048]{1,0:T(8,128)S(1)} %get-tuple-element.70.kappa, f32[8,2048]{1,0:T(8,128)S(1)} %collective-permute-done.11.above, f32[8,2048]{1,0:T(8,128)S(1)} %collective-permute-done.12.below, ...), custom_call_target="tpu_custom_call" | custom-call | tf_op jit(solution)/shard_map/pallas_call | solution.py:353
  278.3 20.0 %all_to_all.59 = f32[16,64,128]{2,1,0:T(8,128)S(1)} all-to-all(f32[16,64,128]{2,1,0:T(8,128)} %get-tuple-element.114), channel_id=1, replica_groups=mesh['beams'=2,'wind'=4,'cross'=4] {'wind','cross'}, dimensions={0} | all-to-all | bytes 1048576 | tf_op jit(solution)/shard_map/all_to_all | solution.py:1051
  300.9 29.4 %all_to_all.60.field = f32[16,128,128]{2,1,0:T(8,128)S(1)} all-to-all(f32[16,128,128]{2,1,0:T(8,128)S(1)} %shard_map.266), channel_id=1, replica_groups=mesh['beams'=2,'wind'=4,'cross'=4] {'wind','cross'}, dimensions={0} | all-to-all | bytes 2097152 | tf_op jit(solution)/shard_map/all_to_all | solution.py:1051
  330.3 4.1 %shard_map.267 = f32[4,128,512]{2,1,0:T(8,128)} custom-call(bf16[4,256,256]{2,1,0:T(8,128)(2,1)S(1)} %copy-done.3, f32[64,128]{1,0:T(8,128)S(1)} %copy-done.22, f32[16,128,128]{2,1,0:T(8,128)S(1)} %all_to_all.60.field), custom_call_target="tpu_custom_call" | custom-call | tf_op jit(solution)/shard_map/pallas_call | solution.py:353
  341.6 13.2 %collective-permute-done.13.refs_1_ = f32[64,512]{1,0:T(8,128)S(1)} collective-permute-done((f32[64,512]{1,0:T(8,128)S(1)}, f32[64,512]{1,0:T(8,128)S(1)}, u32[]{:S(2)}, u32[]{:S(2)}) %collective-permute-start.13) | collective-permute-done | bytes 131104 | tf_op jit(solution)/shard_map/ppermute | solution.py:487
  (127 shorter events, 79.2 us)
Async XLA Ops:
  3.3 18.1 %all-to-all-start = ((f32[4,128,512]{2,1,0:T(8,128)}), f32[4,128,512]{2,1,0:T(8,128)S(1)}, u32[]{:S(2)}, u32[]{:S(2)}) async-start(f32[4,128,512]{2,1,0:T(8,128)} %get-tuple-element.61), calls=%async_computation | async-start | bytes 2097152 | tf_op jit(solution)/shard_map/all_to_all | solution.py:1051
  25.8 43.7 %all-to-all-start.1 = ((f32[16,136,128]{2,1,0:T(8,128)}), f32[16,136,128]{2,1,0:T(8,128)}, u32[]{:S(2)}, u32[]{:S(2)}) async-start(f32[16,136,128]{2,1,0:T(8,128)} %shard_map.250), calls=%async_computation.1 | async-start | bytes 2228224 | tf_op jit(solution)/shard_map/all_to_all | solution.py:1051
  31.1 48.5 %collective-permute-start.10 = (f32[512,128]{1,0:T(8,128)}, f32[512,128]{1,0:T(8,128)S(1)}, u32[]{:S(2)}, u32[]{:S(2)}) collective-permute-start(f32[512,128]{1,0:T(8,128)} %get-tuple-element.96), channel_id=1, source_target_pairs={{0,12},{4,0},{8,4},{12,8},{1,13},{5,1},{9,5},{13,9},{2,14},{6,2},{... | collective-permute-start | bytes 786440 | tf_op jit(solution)/shard_map/ppermute | solution.py:487
  31.6 6.4 %collective-permute-start.3 = (f32[16,256]{1,0:T(8,128)S(1)}, f32[16,256]{1,0:T(8,128)S(1)}, u32[]{:S(2)}, u32[]{:S(2)}) collective-permute-start(f32[16,256]{1,0:T(8,128)S(1)} %get-tuple-element.73), channel_id=1, source_target_pairs={{0,1},{1,2},{2,3},{4,5},{5,6},{6,7},{8,9},{9,10},{10,11},{12,13},{... | collective-permute-start | bytes 49160 | tf_op jit(solution)/shard_map/ppermute | solution.py:852
  33.4 4.7 %collective-permute-start.4 = (f32[16,256]{1,0:T(8,128)S(1)}, f32[16,256]{1,0:T(8,128)S(1)}, u32[]{:S(2)}, u32[]{:S(2)}) collective-permute-start(f32[16,256]{1,0:T(8,128)S(1)} %get-tuple-element.74), channel_id=1, source_target_pairs={{1,0},{2,1},{3,2},{5,4},{6,5},{7,6},{9,8},{10,9},{11,10},{13,12},{... | collective-permute-start | bytes 49160 | tf_op jit(solution)/shard_map/ppermute | solution.py:852
  34.7 47.3 %collective-permute-start.8 = (f32[512,128]{1,0:T(8,128)}, f32[512,128]{1,0:T(8,128)S(1)}, u32[]{:S(2)}, u32[]{:S(2)}) collective-permute-start(f32[512,128]{1,0:T(8,128)} %get-tuple-element.94), channel_id=1, source_target_pairs={{0,4},{4,8},{8,12},{12,0},{1,5},{5,9},{9,13},{13,1},{2,6},{6,10},{... | collective-permute-start | bytes 786440 | tf_op jit(solution)/shard_map/ppermute | solution.py:487
  36.2 49.1 %collective-permute-start.9 = (f32[512,128]{1,0:T(8,128)}, f32[512,128]{1,0:T(8,128)}, u32[]{:S(2)}, u32[]{:S(2)}) collective-permute-start(f32[512,128]{1,0:T(8,128)} %get-tuple-element.95), channel_id=1, source_target_pairs={{0,8},{4,12},{8,0},{12,4},{1,9},{5,13},{9,1},{13,5},{2,10},{6,14},... | collective-permute-start | bytes 786440 | tf_op jit(solution)/shard_map/ppermute | solution.py:487
  38.1 48.2 %copy-start.8 = (f32[128,128]{1,0:T(8,128)S(1)}, f32[128,128]{1,0:T(8,128)}, u32[]{:S(2)}) copy-start(f32[128,128]{1,0:T(8,128)} %constant.28.clone.table) | copy-start | bytes 196612
  41.6 44.7 %copy-start.1 = (bf16[8,2,256,256]{3,2,1,0:T(8,128)(2,1)S(1)}, bf16[8,2,256,256]{3,2,1,0:T(8,128)(2,1)}, u32[]{:S(2)}) copy-start(bf16[8,2,256,256]{3,2,1,0:T(8,128)(2,1)} %constant.27.clone.matrices.dft) | copy-start | bytes 6291460
  41.6 44.7 %copy-start.21 = (f32[16,128]{1,0:T(8,128)S(1)}, f32[16,128]{1,0:T(8,128)}, u32[]{:S(2)}) copy-start(f32[16,128]{1,0:T(8,128)} %constant.29.clone.side_table) | copy-start | bytes 24580
  69.6 21.9 %collective-permute-start.5 = (f32[288,128]{1,0:T(8,128)}, f32[288,128]{1,0:T(8,128)S(1)}, u32[]{:S(2)}, u32[]{:S(2)}) collective-permute-start(f32[288,128]{1,0:T(8,128)} %copy-done.34), channel_id=1, source_target_pairs={{0,4},{4,8},{8,12},{12,0},{1,5},{5,9},{9,13},{13,1},{2,6},{6,10},{... | collective-permute-start | bytes 442376 | tf_op jit(solution)/shard_map/ppermute | solution.py:487
  69.6 21.9 %collective-permute-start.6 = (f32[288,128]{1,0:T(8,128)}, f32[288,128]{1,0:T(8,128)S(1)}, u32[]{:S(2)}, u32[]{:S(2)}) collective-permute-start(f32[288,128]{1,0:T(8,128)} %copy-done.33), channel_id=1, source_target_pairs={{0,8},{4,12},{8,0},{12,4},{1,9},{5,13},{9,1},{13,5},{2,10},{6,14},... | collective-permute-start | bytes 442376 | tf_op jit(solution)/shard_map/ppermute | solution.py:487
  79.6 11.8 %collective-permute-start.7 = (f32[288,128]{1,0:T(8,128)}, f32[288,128]{1,0:T(8,128)S(1)}, u32[]{:S(2)}, u32[]{:S(2)}) collective-permute-start(f32[288,128]{1,0:T(8,128)} %copy-done.32), channel_id=1, source_target_pairs={{0,12},{4,0},{8,4},{12,8},{1,13},{5,1},{9,5},{13,9},{2,14},{6,2},{... | collective-permute-start | bytes 442376 | tf_op jit(solution)/shard_map/ppermute | solution.py:487
  100.8 34.5 %all-to-all-start.2 = ((f32[16,136,128]{2,1,0:T(8,128)}), f32[16,136,128]{2,1,0:T(8,128)S(1)}, u32[]{:S(2)}, u32[]{:S(2)}) async-start(f32[16,136,128]{2,1,0:T(8,128)} %copy-done.6), calls=%async_computation.2 | async-start | bytes 2228224 | tf_op jit(solution)/shard_map/all_to_all | solution.py:1051
  107.9 11.2 %collective-permute-start = (f32[72,512]{1,0:T(8,128)S(1)}, f32[72,512]{1,0:T(8,128)S(1)}, u32[]{:S(2)}, u32[]{:S(2)}) collective-permute-start(f32[72,512]{1,0:T(8,128)S(1)} %copy-done.31), channel_id=1, source_target_pairs={{0,1},{1,2},{2,3},{3,0},{4,5},{5,6},{6,7},{7,4},{8,9},{9,10},{10,1... | collective-permute-start | bytes 442376 | tf_op jit(solution)/shard_map/ppermute | solution.py:487
  108.1 12.2 %collective-permute-start.1 = (f32[72,512]{1,0:T(8,128)S(1)}, f32[72,512]{1,0:T(8,128)S(1)}, u32[]{:S(2)}, u32[]{:S(2)}) collective-permute-start(f32[72,512]{1,0:T(8,128)S(1)} %copy-done.29), channel_id=1, source_target_pairs={{0,2},{1,3},{2,0},{3,1},{4,6},{5,7},{6,4},{7,5},{8,10},{9,11},{10,... | collective-permute-start | bytes 442376 | tf_op jit(solution)/shard_map/ppermute | solution.py:487
  109.6 13.1 %collective-permute-start.2 = (f32[72,512]{1,0:T(8,128)S(1)}, f32[72,512]{1,0:T(8,128)S(1)}, u32[]{:S(2)}, u32[]{:S(2)}) collective-permute-start(f32[72,512]{1,0:T(8,128)S(1)} %copy-done.27), channel_id=1, source_target_pairs={{0,3},{1,0},{2,1},{3,2},{4,7},{5,4},{6,5},{7,6},{8,11},{9,8},{10,9... | collective-permute-start | bytes 442376 | tf_op jit(solution)/shard_map/ppermute | solution.py:487
  123.3 12.0 %collective-permute-start.11 = (f32[8,2048]{1,0:T(8,128)S(1)}, f32[8,2048]{1,0:T(8,128)S(1)}, u32[]{:S(2)}, u32[]{:S(2)}) collective-permute-start(f32[8,2048]{1,0:T(8,128)S(1)} %get-tuple-element.122), channel_id=1, source_target_pairs={{0,1},{1,2},{2,3},{3,4},{4,5},{5,6},{6,7},{7,8},{8,9},{9,10},{10,1... | collective-permute-start | bytes 196616 | tf_op jit(solution)/shard_map/ppermute | solution.py:852
  127.5 7.8 %collective-permute-start.12 = (f32[8,2048]{1,0:T(8,128)S(1)}, f32[8,2048]{1,0:T(8,128)S(1)}, u32[]{:S(2)}, u32[]{:S(2)}) collective-permute-start(f32[8,2048]{1,0:T(8,128)S(1)} %get-tuple-element.121), channel_id=1, source_target_pairs={{1,0},{2,1},{3,2},{4,3},{5,4},{6,5},{7,6},{8,7},{9,8},{10,9},{11,1... | collective-permute-start | bytes 196616 | tf_op jit(solution)/shard_map/ppermute | solution.py:852
  191.2 31.5 %all-to-all-start.4 = ((f32[16,128,128]{2,1,0:T(8,128)}), f32[16,128,128]{2,1,0:T(8,128)}, u32[]{:S(2)}, u32[]{:S(2)}) async-start(f32[16,128,128]{2,1,0:T(8,128)} %get-tuple-element.104), calls=%async_computation.4 | async-start | bytes 2097152 | tf_op jit(solution)/shard_map/all_to_all | solution.py:1051
  334.5 23.0 %all-to-all-start.10 = ((f32[4,128,512]{2,1,0:T(8,128)}), f32[4,128,512]{2,1,0:T(8,128)S(1)}, u32[]{:S(2)}, u32[]{:S(2)}) async-start(f32[4,128,512]{2,1,0:T(8,128)} %shard_map.267), calls=%async_computation.10 | async-start | bytes 2097152 | tf_op jit(solution)/shard_map/all_to_all | solution.py:1051
  338.1 16.6 %collective-permute-start.13 = (f32[64,512]{1,0:T(8,128)S(1)}, f32[64,512]{1,0:T(8,128)S(1)}, u32[]{:S(2)}, u32[]{:S(2)}) collective-permute-start(f32[64,512]{1,0:T(8,128)S(1)} %copy-done.37), channel_id=1, source_target_pairs={{0,1},{1,2},{2,3},{3,0},{4,5},{5,6},{6,7},{7,4},{8,9},{9,10},{10,1... | collective-permute-start | bytes 393224 | tf_op jit(solution)/shard_map/ppermute | solution.py:487
  338.6 17.3 %collective-permute-start.14 = (f32[64,512]{1,0:T(8,128)S(1)}, f32[64,512]{1,0:T(8,128)S(1)}, u32[]{:S(2)}, u32[]{:S(2)}) collective-permute-start(f32[64,512]{1,0:T(8,128)S(1)} %copy-done.36), channel_id=1, source_target_pairs={{0,2},{1,3},{2,0},{3,1},{4,6},{5,7},{6,4},{7,5},{8,10},{9,11},{10,... | collective-permute-start | bytes 393224 | tf_op jit(solution)/shard_map/ppermute | solution.py:487
  340.2 15.8 %collective-permute-start.15 = (f32[64,512]{1,0:T(8,128)S(1)}, f32[64,512]{1,0:T(8,128)S(1)}, u32[]{:S(2)}, u32[]{:S(2)}) collective-permute-start(f32[64,512]{1,0:T(8,128)S(1)} %copy-done.35), channel_id=1, source_target_pairs={{0,3},{1,0},{2,1},{3,2},{4,7},{5,4},{6,5},{7,6},{8,11},{9,8},{10,9... | collective-permute-start | bytes 393224 | tf_op jit(solution)/shard_map/ppermute | solution.py:487
  (35 other events, 249.7 us)

commit v7 on v6

--- a/solution.py
+++ b/solution.py
@@ -652,8 +652,7 @@
             return left, right
 
         def smooth(src, dst, low, count, masked):
-            def step(i, carry):
-                base = pl.multiple_of(low + i * 8, 8)
+            def one(base):
                 value = src[pl.ds(base - 8, 24), :]
                 kap = kx[pl.ds(base - 8, 24), :]
                 mid, k_mid = value[8:16], kap[8:16]
@@ -672,13 +671,18 @@
                     at = pl.ds(base - PAD, 8)
                     if not keep:
                         outs[0][at, :] = -new
-                        return carry
+                        return
                     for b in range(blocks):
                         outs[0][plan.slot(b), at, :] = -new[:, b * INNER : (b + 1) * INNER]
                     kept[pl.ds(base - PAD, 8), :] = -new
+                return
+
+            def step(i, carry):
+                for n in range(2):
+                    one(pl.multiple_of(low + (2 * i + n) * 8, 8))
                 return carry
 
-            lax.fori_loop(0, count, step, 0)
+            lax.fori_loop(0, count // 2, step, 0)
 
         refs = [h0, h1]
         for n in range(SMOOTH):
@@ -771,7 +775,7 @@
     return call(body, outs, scratch, (0, 1, 2), ())(matrices, table, received, alpha, side_table, side_alpha)
 
 
-def rows_turn(plan, read_field, wide, dft, table, screen, field):
+def rows_turn(plan, read_field, wide, dft, table, screen, field, far=False):
     def body(dft, table, screen, field, out, *work):
         def read(a, off):
             return screened(read_field(field, a, off), screen[pl.ds(a * INNER + off, CHUNK), :])
@@ -781,7 +785,7 @@
             plan.send_edges(out)
 
     out = plan.sent_wide if wide else plan.sent
-    return call(body, [out], plan.work_a(), (0, 1, 2), (0,))(dft, table, screen, field)[0]
+    return call(body, [out], plan.work_a(), (0, 1, 2), () if far else (0,), (), (0,) if far else ())(dft, table, screen, field)[0]
 
 
 def rows_smooth(plan, heat, from_left, from_right, kappa, kappa_left, kappa_right, me, *ahead):
@@ -1085,7 +1089,7 @@
     kappas = rows_kappa(plan, along, place)
     home_a = in_order(field_blocks, place, 0)
     screen = smooth_a(0, 0.5, received)
-    sent = rows_turn(plan, plan.home_a, True, *tab_a(0.5), screen, home_a)
+    sent = rows_turn(plan, plan.home_a, True, *tab_a(0.5), screen, home_a, True)
     received, above, below = lax.optimization_barrier((flip(sent), above, below))
     (screen,) = smooth_b(0, False, received)
     sent_middle, sent_field = cols_turn(plan, plan.home_b, 2, dft, tab_b(1.5, 1.0), screen, home_b)

time: 362 us -> 359 us (level)
    unnamed x76 -> x74, local copies, waits for them, and re-layouts: 9.51 us -> 7.71 us
where the time goes in v7:
time: 359 us; the launch traced here: 356 us
  blocking collectives  133 us (37%)
  waiting for transfers between devices  98.1 us (27%)
  Pallas kernels  67.2 us (19%)
  starting transfers between devices  48.1 us (13%)
  local copies, waits for them, and re-layouts  8.81 us (2%)
    all_to_all x6, blocking collectives, exchange(): return lax.all_to_all(x, axes, split_axis=0, concat_axis=0, tiled=True)  133 us
    pallas_call x22, Pallas kernels, run(): pl.pallas_call(body, out_shape=[pltpu.VMEM(o.shape, o.dtype) if i in near...  67.2 us
    all_to_all x5, waiting for transfers between devices, exchange(): return lax.all_to_all(x, axes, split_axis=0, concat_axis=0, tiled=True)  53 us
    ppermute x12, waiting for transfers between devices, shifted(): lax.ppermute(parts[s], axis, [(i, (i + s) % size) for i in range(size)])  39.5 us
    all_to_all x5, starting transfers between devices, exchange(): return lax.all_to_all(x, axes, split_axis=0, concat_axis=0, tiled=True)  25.9 us
    ppermute x12, starting transfers between devices, shifted(): lax.ppermute(parts[s], axis, [(i, (i + s) % size) for i in range(size)])  12.8 us
    unnamed x74, local copies, waits for them, and re-layouts  7.71 us
  transfers between devices with their start and end apart: 21, of which 12 were waited for; matrix products, arithmetic and copies ran while one was open for 0% of the time, Pallas kernels for 5%

profile of v7, /device:TPU:16, one launch (start us, length us, event | category | flops | bytes accessed | tf_op | source)
XLA Modules:
  0.0 356.0 jit_solution(11603776009349449784)
XLA Ops:
  9.8 11.5 %all-to-all-done.field = f32[4,128,512]{2,1,0:T(8,128)S(1)} async-done(((f32[4,128,512]{2,1,0:T(8,128)}), f32[4,128,512]{2,1,0:T(8,128)S(1)}, u32[]{:S(2)}, u32[]{:S(2)}) %all-to-all-start) | async-done | bytes 1048608 | tf_op jit(solution)/shard_map/all_to_all | solution.py:1055
  21.4 4.4 %shard_map.250 = f32[16,136,128]{2,1,0:T(8,128)} custom-call(bf16[4,256,256]{2,1,0:T(8,128)(2,1)S(1)} %copy-done.3, f32[64,128]{1,0:T(8,128)S(1)} %copy-done.13, f32[4,128,512]{2,1,0:T(8,128)S(1)} %all-to-all-done.field), custom_call_target="tpu_custom_call" | custom-call | tf_op jit(solution)/shard_map/pallas_call | solution.py:353
  25.8 5.2 %all-to-all-start.1 = ((f32[16,136,128]{2,1,0:T(8,128)}), f32[16,136,128]{2,1,0:T(8,128)}, u32[]{:S(2)}, u32[]{:S(2)}) async-start(f32[16,136,128]{2,1,0:T(8,128)} %shard_map.250), calls=%async_computation.1 | async-start | bytes 2228224 | tf_op jit(solution)/shard_map/all_to_all | solution.py:1055
  41.5 28.0 %all-to-all-done.1.received = f32[16,136,128]{2,1,0:T(8,128)} async-done(((f32[16,136,128]{2,1,0:T(8,128)}), f32[16,136,128]{2,1,0:T(8,128)}, u32[]{:S(2)}, u32[]{:S(2)}) %all-to-all-start.1) | async-done | bytes 1114144 | tf_op jit(solution)/shard_map/all_to_all | solution.py:1055
  69.5 10.0 %collective-permute-done.10.refs_3_ = f32[512,128]{1,0:T(8,128)S(1)} collective-permute-done((f32[512,128]{1,0:T(8,128)}, f32[512,128]{1,0:T(8,128)S(1)}, u32[]{:S(2)}, u32[]{:S(2)}) %collective-permute-start.10) | collective-permute-done | bytes 262176 | tf_op jit(solution)/shard_map/ppermute | solution.py:487
  86.3 5.1 %shard_map.252 = (f32[1024,128]{1,0:T(8,128)S(1)}, f32[8,1024]{1,0:T(8,128)S(1)}, f32[8,1024]{1,0:T(8,128)S(1)}) custom-call(bf16[8,2,256,256]{3,2,1,0:T(8,128)(2,1)S(1)} %copy-done.1, f32[128,128]{1,0:T(8,128)S(1)} %copy-done.7, f32[16,136,128]{2,1,0:T(8,128)} %all-to-all-done.1.received, f32[1,128]{1,0:T(1,128)S(1)} %get-tuple-element.126.alpha, ...), custom_call_target="tpu_custom_call" | custom-call | tf_op jit(solution)/shard_map/pallas_call | solution.py:353
  92.0 4.3 %shard_map.254.screen = f32[1024,128]{1,0:T(8,128)S(1)} custom-call(f32[1024,128]{1,0:T(8,128)S(1)} %get-tuple-element.83.heat, f32[8,1024]{1,0:T(8,128)S(1)} %get-tuple-element.84.from_left, f32[8,1024]{1,0:T(8,128)S(1)} %get-tuple-element.85.from_right, f32[1024,128]{1,0:T(8,128)S(1)} %get-tuple-element.90.kappa, ...), custom_call_target="tpu_custom_call" | custom-call | tf_op jit(solution)/shard_map/pallas_call | solution.py:353
  100.0 7.1 %all-to-all-start.2 = ((f32[16,136,128]{2,1,0:T(8,128)}), f32[16,136,128]{2,1,0:T(8,128)S(1)}, u32[]{:S(2)}, u32[]{:S(2)}) async-start(f32[16,136,128]{2,1,0:T(8,128)} %shard_map.256), calls=%async_computation.2 | async-start | bytes 2228224 | tf_op jit(solution)/shard_map/all_to_all | solution.py:1055
  110.1 8.2 %collective-permute-done.refs_1_ = f32[72,512]{1,0:T(8,128)S(1)} collective-permute-done((f32[72,512]{1,0:T(8,128)S(1)}, f32[72,512]{1,0:T(8,128)S(1)}, u32[]{:S(2)}, u32[]{:S(2)}) %collective-permute-start) | collective-permute-done | bytes 147488 | tf_op jit(solution)/shard_map/ppermute | solution.py:487
  122.5 4.2 %collective-permute-start.11 = (f32[8,2048]{1,0:T(8,128)S(1)}, f32[8,2048]{1,0:T(8,128)S(1)}, u32[]{:S(2)}, u32[]{:S(2)}) collective-permute-start(f32[8,2048]{1,0:T(8,128)S(1)} %get-tuple-element.122), channel_id=1, source_target_pairs={{0,1},{1,2},{2,3},{3,4},{4,5},{5,6},{6,7},{7,8},{8,9},{9,10},{10,1... | collective-permute-start | bytes 196616 | tf_op jit(solution)/shard_map/ppermute | solution.py:856
  129.0 5.5 %collective-permute-done.11.above = f32[8,2048]{1,0:T(8,128)S(1)} collective-permute-done((f32[8,2048]{1,0:T(8,128)S(1)}, f32[8,2048]{1,0:T(8,128)S(1)}, u32[]{:S(2)}, u32[]{:S(2)}) %collective-permute-start.11) | collective-permute-done | bytes 65568 | tf_op jit(solution)/shard_map/ppermute | solution.py:856
  134.5 4.0 %shard_map.257 = (f32[64,2048]{1,0:T(8,128)S(1)}, f32[8,2048]{1,0:T(8,128)S(1)}, f32[16,16,128]{2,1,0:T(8,128)S(1)}) custom-call(bf16[4,256,256]{2,1,0:T(8,128)(2,1)S(1)} %copy-done.3, f32[64,128]{1,0:T(8,128)S(1)} %copy-done.13, f32[16,136,128]{2,1,0:T(8,128)S(1)} %all-to-all-done.2.received, f32[8,2048]{1,0:T(8,128)S(1)} %get-tuple-element.100.absorption), custom_call_target="tpu_custom_call" | custom-call | tf_op jit(solution)/shard_map/pallas_call | solution.py:353
  138.6 10.1 %all_to_all.55.refs_0_ = f32[16,16,128]{2,1,0:T(8,128)S(1)} all-to-all(f32[16,16,128]{2,1,0:T(8,128)S(1)} %get-tuple-element.103), channel_id=1, replica_groups=mesh['beams'=2,'wind'=4,'cross'=4] {'wind','cross'}, dimensions={0} | all-to-all | bytes 262144 | tf_op jit(solution)/shard_map/all_to_all | solution.py:1055
  151.3 6.1 %shard_map.259 = (f32[16,136,128]{2,1,0:T(8,128)S(1)}, f32[16,128,128]{2,1,0:T(8,128)}) custom-call(bf16[4,256,256]{2,1,0:T(8,128)(2,1)S(1)} %copy-done.3, f32[96,128]{1,0:T(8,128)S(1)} %copy-done.19, f32[64,2048]{1,0:T(8,128)S(1)} %shard_map.258.screen, f32[4,128,512]{2,1,0:T(8,128)S(1)} %copy-done.5), custom_call_target="tpu_custom_call" | custom-call | tf_op jit(solution)/shard_map/pallas_call | solution.py:353
  157.5 32.2 %all_to_all.56.received = f32[16,136,128]{2,1,0:T(8,128)} all-to-all(f32[16,136,128]{2,1,0:T(8,128)S(1)} %get-tuple-element.105), channel_id=1, replica_groups=mesh['beams'=2,'wind'=4,'cross'=4] {'wind','cross'}, dimensions={0} | all-to-all | bytes 2228224 | tf_op jit(solution)/shard_map/all_to_all | solution.py:1055
  189.6 6.2 %all-to-all-start.4 = ((f32[16,128,128]{2,1,0:T(8,128)}), f32[16,128,128]{2,1,0:T(8,128)}, u32[]{:S(2)}, u32[]{:S(2)}) async-start(f32[16,128,128]{2,1,0:T(8,128)} %get-tuple-element.104), calls=%async_computation.4 | async-start | bytes 2097152 | tf_op jit(solution)/shard_map/all_to_all | solution.py:1055
  202.5 4.3 %shard_map.261.screen = f32[1024,128]{1,0:T(8,128)S(1)} custom-call(f32[1024,128]{1,0:T(8,128)S(1)} %get-tuple-element.106.heat, f32[8,1024]{1,0:T(8,128)S(1)} %get-tuple-element.107.from_left, f32[8,1024]{1,0:T(8,128)S(1)} %get-tuple-element.108.from_right, f32[1024,128]{1,0:T(8,128)S(1)} %copy-done.12, f32[8,1024]{1,0:T(8,128)S(1)} %get-tuple-element.91.kappa_left, ...), custom_call_target="tpu_custom_call" | custom-call | tf_op jit(solution)/shard_map/pallas_call | solution.py:353
  207.6 13.5 %all-to-all-done.4.field = f32[16,128,128]{2,1,0:T(8,128)} async-done(((f32[16,128,128]{2,1,0:T(8,128)}), f32[16,128,128]{2,1,0:T(8,128)}, u32[]{:S(2)}, u32[]{:S(2)}) %all-to-all-start.4) | async-done | bytes 1048608 | tf_op jit(solution)/shard_map/all_to_all | solution.py:1055
  227.2 30.8 %all_to_all.57.received = f32[16,136,128]{2,1,0:T(8,128)S(1)} all-to-all(f32[16,136,128]{2,1,0:T(8,128)S(1)} %shard_map.263), channel_id=1, replica_groups=mesh['beams'=2,'wind'=4,'cross'=4] {'wind','cross'}, dimensions={0} | all-to-all | bytes 2228224 | tf_op jit(solution)/shard_map/all_to_all | solution.py:1055
  262.0 10.3 %all_to_all.58.refs_0_ = f32[16,16,128]{2,1,0:T(8,128)S(1)} all-to-all(f32[16,16,128]{2,1,0:T(8,128)S(1)} %get-tuple-element.113), channel_id=1, replica_groups=mesh['beams'=2,'wind'=4,'cross'=4] {'wind','cross'}, dimensions={0} | all-to-all | bytes 262144 | tf_op jit(solution)/shard_map/all_to_all | solution.py:1055
  276.0 19.7 %all_to_all.59 = f32[16,64,128]{2,1,0:T(8,128)S(1)} all-to-all(f32[16,64,128]{2,1,0:T(8,128)} %get-tuple-element.114), channel_id=1, replica_groups=mesh['beams'=2,'wind'=4,'cross'=4] {'wind','cross'}, dimensions={0} | all-to-all | bytes 1048576 | tf_op jit(solution)/shard_map/all_to_all | solution.py:1055
  298.4 29.4 %all_to_all.60.field = f32[16,128,128]{2,1,0:T(8,128)S(1)} all-to-all(f32[16,128,128]{2,1,0:T(8,128)S(1)} %shard_map.266), channel_id=1, replica_groups=mesh['beams'=2,'wind'=4,'cross'=4] {'wind','cross'}, dimensions={0} | all-to-all | bytes 2097152 | tf_op jit(solution)/shard_map/all_to_all | solution.py:1055
  327.8 4.1 %shard_map.267 = f32[4,128,512]{2,1,0:T(8,128)} custom-call(bf16[4,256,256]{2,1,0:T(8,128)(2,1)S(1)} %copy-done.3, f32[64,128]{1,0:T(8,128)S(1)} %copy-done.21, f32[16,128,128]{2,1,0:T(8,128)S(1)} %all_to_all.60.field), custom_call_target="tpu_custom_call" | custom-call | tf_op jit(solution)/shard_map/pallas_call | solution.py:353
  339.0 13.2 %collective-permute-done.13.refs_1_ = f32[64,512]{1,0:T(8,128)S(1)} collective-permute-done((f32[64,512]{1,0:T(8,128)S(1)}, f32[64,512]{1,0:T(8,128)S(1)}, u32[]{:S(2)}, u32[]{:S(2)}) %collective-permute-start.13) | collective-permute-done | bytes 131104 | tf_op jit(solution)/shard_map/ppermute | solution.py:487
  (125 shorter events, 77.2 us)
Async XLA Ops:
  3.3 18.1 %all-to-all-start = ((f32[4,128,512]{2,1,0:T(8,128)}), f32[4,128,512]{2,1,0:T(8,128)S(1)}, u32[]{:S(2)}, u32[]{:S(2)}) async-start(f32[4,128,512]{2,1,0:T(8,128)} %get-tuple-element.61), calls=%async_computation | async-start | bytes 2097152 | tf_op jit(solution)/shard_map/all_to_all | solution.py:1055
  25.8 43.7 %all-to-all-start.1 = ((f32[16,136,128]{2,1,0:T(8,128)}), f32[16,136,128]{2,1,0:T(8,128)}, u32[]{:S(2)}, u32[]{:S(2)}) async-start(f32[16,136,128]{2,1,0:T(8,128)} %shard_map.250), calls=%async_computation.1 | async-start | bytes 2228224 | tf_op jit(solution)/shard_map/all_to_all | solution.py:1055
  31.0 48.5 %collective-permute-start.10 = (f32[512,128]{1,0:T(8,128)}, f32[512,128]{1,0:T(8,128)S(1)}, u32[]{:S(2)}, u32[]{:S(2)}) collective-permute-start(f32[512,128]{1,0:T(8,128)} %get-tuple-element.96), channel_id=1, source_target_pairs={{0,12},{4,0},{8,4},{12,8},{1,13},{5,1},{9,5},{13,9},{2,14},{6,2},{... | collective-permute-start | bytes 786440 | tf_op jit(solution)/shard_map/ppermute | solution.py:487
  31.6 6.4 %collective-permute-start.3 = (f32[16,256]{1,0:T(8,128)S(1)}, f32[16,256]{1,0:T(8,128)S(1)}, u32[]{:S(2)}, u32[]{:S(2)}) collective-permute-start(f32[16,256]{1,0:T(8,128)S(1)} %get-tuple-element.73), channel_id=1, source_target_pairs={{0,1},{1,2},{2,3},{4,5},{5,6},{6,7},{8,9},{9,10},{10,11},{12,13},{... | collective-permute-start | bytes 49160 | tf_op jit(solution)/shard_map/ppermute | solution.py:856
  33.3 4.7 %collective-permute-start.4 = (f32[16,256]{1,0:T(8,128)S(1)}, f32[16,256]{1,0:T(8,128)S(1)}, u32[]{:S(2)}, u32[]{:S(2)}) collective-permute-start(f32[16,256]{1,0:T(8,128)S(1)} %get-tuple-element.74), channel_id=1, source_target_pairs={{1,0},{2,1},{3,2},{5,4},{6,5},{7,6},{9,8},{10,9},{11,10},{13,12},{... | collective-permute-start | bytes 49160 | tf_op jit(solution)/shard_map/ppermute | solution.py:856
  34.6 47.3 %collective-permute-start.8 = (f32[512,128]{1,0:T(8,128)}, f32[512,128]{1,0:T(8,128)S(1)}, u32[]{:S(2)}, u32[]{:S(2)}) collective-permute-start(f32[512,128]{1,0:T(8,128)} %get-tuple-element.94), channel_id=1, source_target_pairs={{0,4},{4,8},{8,12},{12,0},{1,5},{5,9},{9,13},{13,1},{2,6},{6,10},{... | collective-permute-start | bytes 786440 | tf_op jit(solution)/shard_map/ppermute | solution.py:487
  36.1 49.1 %collective-permute-start.9 = (f32[512,128]{1,0:T(8,128)}, f32[512,128]{1,0:T(8,128)}, u32[]{:S(2)}, u32[]{:S(2)}) collective-permute-start(f32[512,128]{1,0:T(8,128)} %get-tuple-element.95), channel_id=1, source_target_pairs={{0,8},{4,12},{8,0},{12,4},{1,9},{5,13},{9,1},{13,5},{2,10},{6,14},... | collective-permute-start | bytes 786440 | tf_op jit(solution)/shard_map/ppermute | solution.py:487
  38.0 48.2 %copy-start.7 = (f32[128,128]{1,0:T(8,128)S(1)}, f32[128,128]{1,0:T(8,128)}, u32[]{:S(2)}) copy-start(f32[128,128]{1,0:T(8,128)} %constant.28.clone.table) | copy-start | bytes 196612
  41.5 44.7 %copy-start.1 = (bf16[8,2,256,256]{3,2,1,0:T(8,128)(2,1)S(1)}, bf16[8,2,256,256]{3,2,1,0:T(8,128)(2,1)}, u32[]{:S(2)}) copy-start(bf16[8,2,256,256]{3,2,1,0:T(8,128)(2,1)} %constant.27.clone.matrices.dft) | copy-start | bytes 6291460
  41.5 44.7 %copy-start.20 = (f32[16,128]{1,0:T(8,128)S(1)}, f32[16,128]{1,0:T(8,128)}, u32[]{:S(2)}) copy-start(f32[16,128]{1,0:T(8,128)} %constant.29.clone.side_table) | copy-start | bytes 24580
  69.5 21.9 %collective-permute-start.5 = (f32[288,128]{1,0:T(8,128)}, f32[288,128]{1,0:T(8,128)S(1)}, u32[]{:S(2)}, u32[]{:S(2)}) collective-permute-start(f32[288,128]{1,0:T(8,128)} %copy-done.33), channel_id=1, source_target_pairs={{0,4},{4,8},{8,12},{12,0},{1,5},{5,9},{9,13},{13,1},{2,6},{6,10},{... | collective-permute-start | bytes 442376 | tf_op jit(solution)/shard_map/ppermute | solution.py:487
  69.5 21.9 %collective-permute-start.6 = (f32[288,128]{1,0:T(8,128)}, f32[288,128]{1,0:T(8,128)S(1)}, u32[]{:S(2)}, u32[]{:S(2)}) collective-permute-start(f32[288,128]{1,0:T(8,128)} %copy-done.32), channel_id=1, source_target_pairs={{0,8},{4,12},{8,0},{12,4},{1,9},{5,13},{9,1},{13,5},{2,10},{6,14},... | collective-permute-start | bytes 442376 | tf_op jit(solution)/shard_map/ppermute | solution.py:487
  79.5 11.8 %collective-permute-start.7 = (f32[288,128]{1,0:T(8,128)}, f32[288,128]{1,0:T(8,128)S(1)}, u32[]{:S(2)}, u32[]{:S(2)}) collective-permute-start(f32[288,128]{1,0:T(8,128)} %copy-done.31), channel_id=1, source_target_pairs={{0,12},{4,0},{8,4},{12,8},{1,13},{5,1},{9,5},{13,9},{2,14},{6,2},{... | collective-permute-start | bytes 442376 | tf_op jit(solution)/shard_map/ppermute | solution.py:487
  100.0 34.5 %all-to-all-start.2 = ((f32[16,136,128]{2,1,0:T(8,128)}), f32[16,136,128]{2,1,0:T(8,128)S(1)}, u32[]{:S(2)}, u32[]{:S(2)}) async-start(f32[16,136,128]{2,1,0:T(8,128)} %shard_map.256), calls=%async_computation.2 | async-start | bytes 2228224 | tf_op jit(solution)/shard_map/all_to_all | solution.py:1055
  107.1 11.2 %collective-permute-start = (f32[72,512]{1,0:T(8,128)S(1)}, f32[72,512]{1,0:T(8,128)S(1)}, u32[]{:S(2)}, u32[]{:S(2)}) collective-permute-start(f32[72,512]{1,0:T(8,128)S(1)} %copy-done.30), channel_id=1, source_target_pairs={{0,1},{1,2},{2,3},{3,0},{4,5},{5,6},{6,7},{7,4},{8,9},{9,10},{10,1... | collective-permute-start | bytes 442376 | tf_op jit(solution)/shard_map/ppermute | solution.py:487
  107.3 12.2 %collective-permute-start.1 = (f32[72,512]{1,0:T(8,128)S(1)}, f32[72,512]{1,0:T(8,128)S(1)}, u32[]{:S(2)}, u32[]{:S(2)}) collective-permute-start(f32[72,512]{1,0:T(8,128)S(1)} %copy-done.28), channel_id=1, source_target_pairs={{0,2},{1,3},{2,0},{3,1},{4,6},{5,7},{6,4},{7,5},{8,10},{9,11},{10,... | collective-permute-start | bytes 442376 | tf_op jit(solution)/shard_map/ppermute | solution.py:487
  108.8 13.1 %collective-permute-start.2 = (f32[72,512]{1,0:T(8,128)S(1)}, f32[72,512]{1,0:T(8,128)S(1)}, u32[]{:S(2)}, u32[]{:S(2)}) collective-permute-start(f32[72,512]{1,0:T(8,128)S(1)} %copy-done.26), channel_id=1, source_target_pairs={{0,3},{1,0},{2,1},{3,2},{4,7},{5,4},{6,5},{7,6},{8,11},{9,8},{10,9... | collective-permute-start | bytes 442376 | tf_op jit(solution)/shard_map/ppermute | solution.py:487
  122.5 12.0 %collective-permute-start.11 = (f32[8,2048]{1,0:T(8,128)S(1)}, f32[8,2048]{1,0:T(8,128)S(1)}, u32[]{:S(2)}, u32[]{:S(2)}) collective-permute-start(f32[8,2048]{1,0:T(8,128)S(1)} %get-tuple-element.122), channel_id=1, source_target_pairs={{0,1},{1,2},{2,3},{3,4},{4,5},{5,6},{6,7},{7,8},{8,9},{9,10},{10,1... | collective-permute-start | bytes 196616 | tf_op jit(solution)/shard_map/ppermute | solution.py:856
  126.7 7.8 %collective-permute-start.12 = (f32[8,2048]{1,0:T(8,128)S(1)}, f32[8,2048]{1,0:T(8,128)S(1)}, u32[]{:S(2)}, u32[]{:S(2)}) collective-permute-start(f32[8,2048]{1,0:T(8,128)S(1)} %get-tuple-element.121), channel_id=1, source_target_pairs={{1,0},{2,1},{3,2},{4,3},{5,4},{6,5},{7,6},{8,7},{9,8},{10,9},{11,1... | collective-permute-start | bytes 196616 | tf_op jit(solution)/shard_map/ppermute | solution.py:856
  189.6 31.4 %all-to-all-start.4 = ((f32[16,128,128]{2,1,0:T(8,128)}), f32[16,128,128]{2,1,0:T(8,128)}, u32[]{:S(2)}, u32[]{:S(2)}) async-start(f32[16,128,128]{2,1,0:T(8,128)} %get-tuple-element.104), calls=%async_computation.4 | async-start | bytes 2097152 | tf_op jit(solution)/shard_map/all_to_all | solution.py:1055
  331.9 23.0 %all-to-all-start.10 = ((f32[4,128,512]{2,1,0:T(8,128)}), f32[4,128,512]{2,1,0:T(8,128)S(1)}, u32[]{:S(2)}, u32[]{:S(2)}) async-start(f32[4,128,512]{2,1,0:T(8,128)} %shard_map.267), calls=%async_computation.10 | async-start | bytes 2097152 | tf_op jit(solution)/shard_map/all_to_all | solution.py:1055
  335.6 16.6 %collective-permute-start.13 = (f32[64,512]{1,0:T(8,128)S(1)}, f32[64,512]{1,0:T(8,128)S(1)}, u32[]{:S(2)}, u32[]{:S(2)}) collective-permute-start(f32[64,512]{1,0:T(8,128)S(1)} %copy-done.36), channel_id=1, source_target_pairs={{0,1},{1,2},{2,3},{3,0},{4,5},{5,6},{6,7},{7,4},{8,9},{9,10},{10,1... | collective-permute-start | bytes 393224 | tf_op jit(solution)/shard_map/ppermute | solution.py:487
  336.0 17.3 %collective-permute-start.14 = (f32[64,512]{1,0:T(8,128)S(1)}, f32[64,512]{1,0:T(8,128)S(1)}, u32[]{:S(2)}, u32[]{:S(2)}) collective-permute-start(f32[64,512]{1,0:T(8,128)S(1)} %copy-done.35), channel_id=1, source_target_pairs={{0,2},{1,3},{2,0},{3,1},{4,6},{5,7},{6,4},{7,5},{8,10},{9,11},{10,... | collective-permute-start | bytes 393224 | tf_op jit(solution)/shard_map/ppermute | solution.py:487
  337.7 15.8 %collective-permute-start.15 = (f32[64,512]{1,0:T(8,128)S(1)}, f32[64,512]{1,0:T(8,128)S(1)}, u32[]{:S(2)}, u32[]{:S(2)}) collective-permute-start(f32[64,512]{1,0:T(8,128)S(1)} %copy-done.34), channel_id=1, source_target_pairs={{0,3},{1,0},{2,1},{3,2},{4,7},{5,4},{6,5},{7,6},{8,11},{9,8},{10,9... | collective-permute-start | bytes 393224 | tf_op jit(solution)/shard_map/ppermute | solution.py:487
  (34 other events, 254.3 us)
